TPU v7x, 512 devices: a whole 4x8x8 slice. The times are simulated.
512 devices in a mesh: dp: 32 (over y_hi, z, core), expert: 16 (over x, y_lo).
Axes of the slice: x: 4, y: 8 (y_hi: 2, y_lo: 4; y = y_hi * 4 + y_lo), z: 8, core: 2. Of those that a mesh axis runs over, the one named last changes fastest.
Arguments:
- tokens: bfloat16 [2048, 4096], P('expert', 'dp'), may hold values from -6 to 6
- cotangent: bfloat16 [2048, 4096], P('expert', 'dp'), may hold values from -1.125 to 1.125
- routes: int32 [2048, 2], P('expert'), may hold values from 0 to 15, all different within a row; in each aligned block of 128 rows (0 to 127, 128 to 255, ...) at most 40 rows name the same one
- gates: float32 [2048, 2], P('expert'), may hold values from 0.05 to 1
- expert_weights: bfloat16 [16, 3, 2048, 4096], P('expert', None, 'dp'), may hold values from -0.09375 to 0.09375
Outputs:
- weight_grads: bfloat16 [16, 3, 2048, 4096], P('expert', None, 'dp')
Inputs may be any that keep to these rules, and one draw needn't show every extreme that they name: Each row names 2 different experts; within the 128 rows of one index of the expert axis no expert is named by more than 40 routes.
All inputs are finite; a program needn't handle non-finite values.
Results may differ from a plain program's by a relative error of at most 0.0057.
Values may be sent and summed in bfloat16 or wider, within the bound.
No kernel may reach another device: no remote copies, remote signals or barrier semaphores. Data moves between devices by JAX's collectives and lax.ppermute only.
A program may use at most 64 MiB of HBM per device.

v0:
```python
import functools

import jax
import jax.numpy as jnp
from jax import lax
from jax.experimental import pallas as pl
from jax.experimental.pallas import tpu as pltpu
from jax.sharding import Mesh
from jax.sharding import PartitionSpec as P

CAP = 40
BF16 = jnp.bfloat16
F32 = jnp.float32
EARLY_VMEM = 12 << 20
GRADS_VMEM = 18 << 20


def pack_kernel(routes_ref, gates_ref, tokens_ref, cotangent_ref, out_ref):
    tokens = routes_ref.shape[1]
    copies, slots, width = out_ref.shape
    experts = slots // CAP
    ids = lax.broadcasted_iota(jnp.int32, (experts, tokens), 0)
    named = jnp.zeros((experts, tokens), F32)
    weight = jnp.zeros((experts, tokens), F32)
    for k in range(routes_ref.shape[0]):
        hit = routes_ref[k : k + 1, :] == ids
        named = named + jnp.where(hit, 1.0, 0.0)
        weight = weight + jnp.where(hit, gates_ref[k : k + 1, :], 0.0)
    down = lax.broadcasted_iota(jnp.int32, (tokens, tokens), 0)
    across = lax.broadcasted_iota(jnp.int32, (tokens, tokens), 1)
    before = jnp.where(down < across, 1.0, 0.0).astype(BF16)
    earlier = jnp.dot(named.astype(BF16), before, preferred_element_type=F32)
    place = jnp.where(named > 0.0, earlier, -1.0)
    places = lax.broadcasted_iota(jnp.int32, (CAP, tokens), 0).astype(F32)
    select, weights = [], []
    for e in range(experts):
        hit = place[e : e + 1, :] == places
        select.append(jnp.where(hit, 1.0, 0.0))
        weights.append(jnp.sum(jnp.where(hit, weight[e : e + 1, :], 0.0), axis=1, keepdims=True))
    select = jnp.concatenate(select, axis=0).astype(BF16)
    weights = jnp.concatenate(weights, axis=0)
    rows = jnp.dot(select, tokens_ref[...], preferred_element_type=F32).astype(BF16)
    scaled = jnp.dot(select, cotangent_ref[...], preferred_element_type=F32)
    scaled = (scaled * weights).astype(BF16)
    for j in range(copies):
        out_ref[j, :, : width // 2] = rows
        out_ref[j, :, width // 2 :] = scaled


def fetch(sources, buffers, sems):
    copies = []
    for n, (source, place) in enumerate(zip(sources, buffers)):
        copy = pltpu.make_async_copy(source, place, sems.at[n])
        copy.start()
        copies.append(copy)
    return copies


def column(index_ref, ring_size, half, block, j):
    step, chain, turned = block
    ring, core = index_ref[0], index_ref[1]
    way = (1 - 2 * core) * (1 - 2 * turned)
    z = lax.rem(ring - way * step + 2 * ring_size, ring_size)
    other = chain ^ turned
    c = core + other - 2 * core * other
    return pl.multiple_of(((j * ring_size + z) * 2 + c) * half, half)


def add_forward(index_ref, ring_size, weights_buf, total, piece, block):
    halves, half = piece.shape[0], piece.shape[2] // 2
    hidden_units = weights_buf.shape[2]
    along = (((1,), (1,)), ((), ()))

    def weight_block(m):
        return jnp.concatenate(
            [
                weights_buf[0, m, :, pl.ds(column(index_ref, ring_size, half, block, j), half)]
                for j in range(halves)
            ],
            axis=1,
        )

    pair = jnp.concatenate([weight_block(0), weight_block(1)], axis=0)
    total[:, : 2 * hidden_units] += lax.dot_general(
        joined(piece, 0), pair, along, preferred_element_type=F32
    )
    total[:, 2 * hidden_units :] += lax.dot_general(
        joined(piece, 1), weight_block(2), along, preferred_element_type=F32
    )


def joined(piece, part):
    halves, half = piece.shape[0], piece.shape[2] // 2
    cut = slice(part * half, (part + 1) * half)
    return jnp.concatenate([piece[j, :, cut] for j in range(halves)], axis=1)


def forward_kernel(ring_size, blocks, index_ref, weights_ref, *refs):
    count = len(blocks)
    sources, total = refs[:count], refs[count]
    pieces_buf, weights_buf, sems = refs[count + 1 :]
    copies = fetch(
        (weights_ref,) + sources, [weights_buf] + [pieces_buf.at[k] for k in range(count)], sems
    )
    total[...] = jnp.zeros_like(total)
    copies[0].wait()
    for k, block in enumerate(blocks):
        copies[1 + k].wait()
        add_forward(index_ref, ring_size, weights_buf, total, pieces_buf.at[k], block)


def grads_kernel(ring_size, blocks, early, sums, index_ref, weights_ref, *refs):
    count = len(blocks)
    partials, sources, out_ref = refs[:sums], refs[sums : sums + count], refs[sums + count]
    pieces_buf, weights_buf, partial_buf, total, sems = refs[sums + count + 1 :]
    half = pieces_buf.shape[3] // 2
    halves = pieces_buf.shape[1]
    late = [k for k in range(count) if blocks[k] not in early]
    order = late + [k for k in range(count) if blocks[k] in early]
    base = 1 + sums
    copies = fetch(
        [weights_ref] + list(partials) + [sources[k] for k in order],
        [weights_buf] + [partial_buf.at[m] for m in range(sums)] + [pieces_buf.at[k] for k in order],
        sems,
    )
    for copy in copies[:base]:
        copy.wait()
    running = partial_buf[0]
    for m in range(1, sums):
        running = running + partial_buf[m]
    total[...] = running
    hidden_units = weights_buf.shape[2]
    for n, k in enumerate(late):
        copies[base + n].wait()
        add_forward(index_ref, ring_size, weights_buf, total, pieces_buf.at[k], blocks[k])
    gate_part = total[:, :hidden_units]
    up_part = total[:, hidden_units : 2 * hidden_units]
    back_hidden = total[:, 2 * hidden_units :]
    sigmoid_part = jax.nn.sigmoid(gate_part)
    silu = gate_part * sigmoid_part
    hidden = (silu * up_part).astype(BF16)
    derivative = sigmoid_part * (1.0 + gate_part * (1.0 - sigmoid_part))
    pre_gate = (back_hidden * up_part * derivative).astype(BF16)
    pre_up = (back_hidden * silu).astype(BF16)
    both = jnp.concatenate([pre_gate, pre_up], axis=1).T
    hidden_t = hidden.T
    for n, k in enumerate(order):
        if n >= len(late):
            copies[base + n].wait()
        piece = pieces_buf.at[k]
        ins = jnp.dot(both, joined(piece, 0), preferred_element_type=F32).astype(BF16)
        outs = jnp.dot(hidden_t, joined(piece, 1), preferred_element_type=F32).astype(BF16)
        for j in range(halves):
            cols = pl.ds(column(index_ref, ring_size, half, blocks[k], j), half)
            cut = slice(j * half, (j + 1) * half)
            out_ref[0, 0, :, cols] = ins[:hidden_units, cut]
            out_ref[0, 1, :, cols] = ins[hidden_units:, cut]
            out_ref[0, 2, :, cols] = outs[:, cut]


def device_step(tokens, cotangent, routes, gates, expert_weights):
    groups = lax.axis_size("expert")
    ring_size = lax.axis_size("ring")
    slots = groups * CAP
    width = tokens.shape[1]
    send = pl.pallas_call(
        pack_kernel, out_shape=jax.ShapeDtypeStruct((2, slots, 2 * width), BF16)
    )(routes.T, gates.T, tokens, cotangent)
    around = [
        (z * 2 + c, ((z + 1 - 2 * c) % ring_size) * 2 + c)
        for z in range(ring_size)
        for c in range(2)
    ]

    def swapped(x):
        return lax.ppermute(x, "core", [(0, 1), (1, 0)])

    own = lax.all_to_all(
        send.reshape(2 * groups, CAP, 2 * width),
        ("half", "expert"),
        split_axis=0,
        concat_axis=0,
        tiled=True,
    ).reshape(2, slots, 2 * width)
    far = ring_size // 2
    held = {(0, 0, 0): own, (0, 1, 0): swapped(own)}
    raw = {}
    for step in range(1, far + 1):
        for chain in range(2 if step < far else 1):
            piece = lax.ppermute(held[step - 1, chain, 0], ("ring", "core"), around)
            raw[step, chain, 0] = piece
            if step > 1:
                crossed = swapped(held[step - 1, chain, 0])
                raw[step - 1, chain, 1] = crossed
                piece, crossed = lax.optimization_barrier((piece, crossed))
                held[step - 1, chain, 1] = crossed
            held[step, chain, 0] = piece
    held[far - 1, 1, 1] = swapped(held[far - 1, 1, 0])
    held[far, 0, 1] = swapped(held[far, 0, 0])
    blocks = list(held)
    index = jnp.stack([lax.axis_index("ring"), lax.axis_index("core")]).astype(jnp.int32)
    hidden_units = expert_weights.shape[2]
    features = expert_weights.shape[3]
    any_spec = pl.BlockSpec(memory_space=pl.ANY)
    smem_spec = pl.BlockSpec(memory_space=pltpu.SMEM)
    piece_bytes = 8 * slots * width
    weight_bytes = 6 * hidden_units * features
    block_flops = 12 * slots * width * hidden_units
    groups_early = [
        [(0, 0, 0), (0, 1, 0)],
        [(s, c, t) for s in range(1, far - 1) for t in range(2) for c in range(2)],
    ]
    groups_early = [g for g in groups_early if g]
    partials = []
    for chosen in groups_early:
        partials.append(
            pl.pallas_call(
                functools.partial(forward_kernel, ring_size, chosen),
                out_shape=jax.ShapeDtypeStruct((slots, 3 * hidden_units), F32),
                in_specs=[smem_spec, any_spec] + [any_spec] * len(chosen),
                out_specs=pl.BlockSpec(memory_space=pltpu.VMEM),
                scratch_shapes=[
                    pltpu.VMEM((len(chosen), 2, slots, 2 * width), BF16),
                    pltpu.VMEM(expert_weights.shape, BF16),
                    pltpu.SemaphoreType.DMA((1 + len(chosen),)),
                ],
                cost_estimate=pl.CostEstimate(
                    flops=len(chosen) * block_flops,
                    bytes_accessed=len(chosen) * piece_bytes + weight_bytes,
                    transcendentals=0,
                ),
                compiler_params=pltpu.CompilerParams(vmem_limit_bytes=EARLY_VMEM),
            )(index, expert_weights, *[raw.get(k, held[k]) for k in chosen])
        )
    early = [k for g in groups_early for k in g]
    return pl.pallas_call(
        functools.partial(grads_kernel, ring_size, blocks, early, len(partials)),
        out_shape=jax.ShapeDtypeStruct(expert_weights.shape, BF16),
        in_specs=[smem_spec, any_spec] + [any_spec] * (len(partials) + len(blocks)),
        out_specs=pl.BlockSpec(memory_space=pltpu.VMEM),
        scratch_shapes=[
            pltpu.VMEM((len(blocks), 2, slots, 2 * width), BF16),
            pltpu.VMEM(expert_weights.shape, BF16),
            pltpu.VMEM((len(partials), slots, 3 * hidden_units), F32),
            pltpu.VMEM((slots, 3 * hidden_units), F32),
            pltpu.SemaphoreType.DMA((1 + len(partials) + len(blocks),)),
        ],
        cost_estimate=pl.CostEstimate(
            flops=2 * len(blocks) * block_flops,
            bytes_accessed=len(blocks) * piece_bytes + 2 * weight_bytes,
            transcendentals=slots * hidden_units,
        ),
        compiler_params=pltpu.CompilerParams(vmem_limit_bytes=GRADS_VMEM),
    )(index, expert_weights, *partials, *[held[k] for k in blocks])


def solution(mesh):
    sizes = dict(zip(mesh.axis_names, mesh.devices.shape))
    fine = Mesh(
        mesh.devices.reshape(2, sizes["dp"] // 4, 2, sizes["expert"]),
        ("half", "ring", "core", "expert"),
    )
    dp = ("half", "ring", "core")
    return jax.shard_map(
        device_step,
        mesh=fine,
        in_specs=(
            P("expert", dp),
            P("expert", dp),
            P("expert", None),
            P("expert", None),
            P("expert", None, dp, None),
        ),
        out_specs=P("expert", None, dp, None),
        check_vma=False,
    )
```

profile of v0, /device:TPU:1, one launch (start us, length us, event | category | flops | bytes accessed | tf_op | source)
XLA Modules:
  0.0 129.0 jit_solution(572562570830024812)
XLA Ops:
  0.0 2.2 %shard_map.55 = bf16[2,640,256]{2,1,0:T(8,128)(2,1)} custom-call(s32[2,128]{1,0:T(2,128)} %bitcast.11, f32[2,128]{1,0:T(2,128)} %bitcast.12, bf16[128,128]{1,0:T(8,128)(2,1)} %tokens_ref.1, bf16[128,128]{1,0:T(8,128)(2,1)} %cotangent_ref.1), custom_call_target="tpu_custom_call" | custom-call | tf_op jit(solution)/shard_map/pallas_call | solution.py:166
  2.2 30.5 %all_to_all.5 = bf16[32,40,256]{2,1,0:T(8,128)(2,1)S(1)} all-to-all(bf16[32,40,256]{2,1,0:T(8,128)(2,1)} %bitcast.10), channel_id=1, replica_groups=mesh['half'=2,'ring'=8,'core'=2,'expert'=16] {'half','expert'}, dimensions={0} | all-to-all | bytes 1310720 | tf_op jit(solution)/shard_map/all_to_all | solution.py:178
  32.8 10.7 %collective-permute-start.1 = (bf16[2,640,256]{2,1,0:T(8,128)(2,1)S(1)}, bf16[2,640,256]{2,1,0:T(8,128)(2,1)S(1)}, u32[]{:S(2)}, u32[]{:S(2)}) collective-permute-start(bf16[2,640,256]{2,1,0:T(8,128)(2,1)S(1)} %bitcast.6), channel_id=1, source_target_pairs={{0,32},{16,240},{32,64},{48,16},{64,96},{80,48},{96,128},{112,80},... | collective-permute-start | bytes 1966088 | tf_op jit(solution)/shard_map/ppermute | solution.py:190
  43.4 1.9 %collective-permute-start = (bf16[2,640,256]{2,1,0:T(8,128)(2,1)S(1)}, bf16[2,640,256]{2,1,0:T(8,128)(2,1)S(1)}, u32[]{:S(2)}, u32[]{:S(2)}) collective-permute-start(bf16[2,640,256]{2,1,0:T(8,128)(2,1)S(1)} %bitcast.7), channel_id=1, source_target_pairs={{0,16},{16,0},{1,17},{17,1},{2,18},{18,2},{3,19},{19,3},{4,20},{20... | collective-permute-start | bytes 1966088 | tf_op jit(solution)/shard_map/ppermute | solution.py:176
  45.4 5.6 %collective-permute-done.1.refs_0_.refs_4_ = bf16[2,640,256]{2,1,0:T(8,128)(2,1)S(1)} collective-permute-done((bf16[2,640,256]{2,1,0:T(8,128)(2,1)S(1)}, bf16[2,640,256]{2,1,0:T(8,128)(2,1)S(1)}, u32[]{:S(2)}, u32[]{:S(2)}) %collective-permute-start.1) | collective-permute-done | bytes 655392 | tf_op jit(solution)/shard_map/ppermute | solution.py:190
  50.9 5.0 %collective-permute-start.5 = (bf16[2,640,256]{2,1,0:T(8,128)(2,1)S(1)}, bf16[2,640,256]{2,1,0:T(8,128)(2,1)S(1)}, u32[]{:S(2)}, u32[]{:S(2)}) collective-permute-start(bf16[2,640,256]{2,1,0:T(8,128)(2,1)S(1)} %collective-permute-done.1.refs_0_.refs_4_), channel_id=1, source_target_pairs={{0,32},{16,240},{32,64},{48,16},{64,96},{80,48},{96,128},{112,80},... | collective-permute-start | bytes 1966088 | tf_op jit(solution)/shard_map/ppermute | solution.py:190
  56.0 2.4 %collective-permute-start.3 = (bf16[2,640,256]{2,1,0:T(8,128)(2,1)S(1)}, bf16[2,640,256]{2,1,0:T(8,128)(2,1)S(1)}, u32[]{:S(2)}, u32[]{:S(2)}) collective-permute-start(bf16[2,640,256]{2,1,0:T(8,128)(2,1)S(1)} %collective-permute-done.1.refs_0_.refs_4_), channel_id=1, source_target_pairs={{0,16},{16,0},{1,17},{17,1},{2,18},{18,2},{3,19},{19,3},{4,20},{20... | collective-permute-start | bytes 1966088 | tf_op jit(solution)/shard_map/ppermute | solution.py:176
  58.3 0.0 collective-permute-done.refs_1_.refs_3_
  58.4 4.9 %collective-permute-start.2 = (bf16[2,640,256]{2,1,0:T(8,128)(2,1)S(1)}, bf16[2,640,256]{2,1,0:T(8,128)(2,1)S(1)}, u32[]{:S(2)}, u32[]{:S(2)}) collective-permute-start(bf16[2,640,256]{2,1,0:T(8,128)(2,1)S(1)} %collective-permute-done.refs_1_.refs_3_), channel_id=1, source_target_pairs={{0,32},{16,240},{32,64},{48,16},{64,96},{80,48},{96,128},{112,80},... | collective-permute-start | bytes 1966088 | tf_op jit(solution)/shard_map/ppermute | solution.py:190
  63.2 0.2 collective-permute-done.5.refs_4_.refs_7_
  63.5 0.0 collective-permute-done.3.refs_2_.refs_6_
  63.5 0.8 copy-done.3
  64.3 5.0 %collective-permute-start.9 = (bf16[2,640,256]{2,1,0:T(8,128)(2,1)S(1)}, bf16[2,640,256]{2,1,0:T(8,128)(2,1)S(1)}, u32[]{:S(2)}, u32[]{:S(2)}) collective-permute-start(bf16[2,640,256]{2,1,0:T(8,128)(2,1)S(1)} %collective-permute-done.5.refs_4_.refs_7_), channel_id=1, source_target_pairs={{0,32},{16,240},{32,64},{48,16},{64,96},{80,48},{96,128},{112,80},... | collective-permute-start | bytes 1966088 | tf_op jit(solution)/shard_map/ppermute | solution.py:190
  69.3 3.5 %collective-permute-start.7 = (bf16[2,640,256]{2,1,0:T(8,128)(2,1)S(1)}, bf16[2,640,256]{2,1,0:T(8,128)(2,1)S(1)}, u32[]{:S(2)}, u32[]{:S(2)}) collective-permute-start(bf16[2,640,256]{2,1,0:T(8,128)(2,1)S(1)} %collective-permute-done.5.refs_4_.refs_7_), channel_id=1, source_target_pairs={{0,16},{16,0},{1,17},{17,1},{2,18},{18,2},{3,19},{19,3},{4,20},{20... | collective-permute-start | bytes 1966088 | tf_op jit(solution)/shard_map/ppermute | solution.py:176
  72.9 0.8 copy-done.1
  73.7 0.0 collective-permute-done.2.refs_1_.refs_5_
  73.7 4.8 %collective-permute-start.6 = (bf16[2,640,256]{2,1,0:T(8,128)(2,1)S(1)}, bf16[2,640,256]{2,1,0:T(8,128)(2,1)S(1)}, u32[]{:S(2)}, u32[]{:S(2)}) collective-permute-start(bf16[2,640,256]{2,1,0:T(8,128)(2,1)S(1)} %collective-permute-done.2.refs_1_.refs_5_), channel_id=1, source_target_pairs={{0,32},{16,240},{32,64},{48,16},{64,96},{80,48},{96,128},{112,80},... | collective-permute-start | bytes 1966088 | tf_op jit(solution)/shard_map/ppermute | solution.py:190
  78.6 1.9 %collective-permute-start.4 = (bf16[2,640,256]{2,1,0:T(8,128)(2,1)S(1)}, bf16[2,640,256]{2,1,0:T(8,128)(2,1)S(1)}, u32[]{:S(2)}, u32[]{:S(2)}) collective-permute-start(bf16[2,640,256]{2,1,0:T(8,128)(2,1)S(1)} %collective-permute-done.2.refs_1_.refs_5_), channel_id=1, source_target_pairs={{0,16},{16,0},{1,17},{17,1},{2,18},{18,2},{3,19},{19,3},{4,20},{20... | collective-permute-start | bytes 1966088 | tf_op jit(solution)/shard_map/ppermute | solution.py:176
  80.5 0.0 copy-start.5
  80.5 0.8 copy-done.5
  81.3 0.0 collective-permute-done.9.refs_11_
  81.3 0.0 collective-permute-done.7.refs_6_.refs_10_
  81.3 0.8 copy-done.7
  82.2 3.3 %collective-permute-start.12 = (bf16[2,640,256]{2,1,0:T(8,128)(2,1)S(1)}, bf16[2,640,256]{2,1,0:T(8,128)(2,1)S(1)}, u32[]{:S(2)}, u32[]{:S(2)}) collective-permute-start(bf16[2,640,256]{2,1,0:T(8,128)(2,1)S(1)} %collective-permute-done.9.refs_11_), channel_id=1, source_target_pairs={{0,16},{16,0},{1,17},{17,1},{2,18},{18,2},{3,19},{19,3},{4,20},{20... | collective-permute-start | bytes 1966088 | tf_op jit(solution)/shard_map/ppermute | solution.py:176
  85.5 2.0 %collective-permute-start.11 = (bf16[2,640,256]{2,1,0:T(8,128)(2,1)S(1)}, bf16[2,640,256]{2,1,0:T(8,128)(2,1)}, u32[]{:S(2)}, u32[]{:S(2)}) collective-permute-start(bf16[2,640,256]{2,1,0:T(8,128)(2,1)S(1)} %collective-permute-done.9.refs_11_), channel_id=1, source_target_pairs={{0,32},{16,240},{32,64},{48,16},{64,96},{80,48},{96,128},{112,80},... | collective-permute-start | bytes 1966088 | tf_op jit(solution)/shard_map/ppermute | solution.py:190
  87.5 0.8 copy-done.15
  88.4 0.0 collective-permute-done.6.refs_5_.refs_9_
  88.4 0.0 collective-permute-done.4.refs_3_.refs_8_
  88.4 0.8 copy-done.11
  89.2 2.7 %collective-permute-start.10 = (bf16[2,640,256]{2,1,0:T(8,128)(2,1)S(1)}, bf16[2,640,256]{2,1,0:T(8,128)(2,1)}, u32[]{:S(2)}, u32[]{:S(2)}) collective-permute-start(bf16[2,640,256]{2,1,0:T(8,128)(2,1)S(1)} %collective-permute-done.6.refs_5_.refs_9_), channel_id=1, source_target_pairs={{0,32},{16,240},{32,64},{48,16},{64,96},{80,48},{96,128},{112,80},... | collective-permute-start | bytes 1966088 | tf_op jit(solution)/shard_map/ppermute | solution.py:190
  92.0 2.5 %collective-permute-start.8 = (bf16[2,640,256]{2,1,0:T(8,128)(2,1)S(1)}, bf16[2,640,256]{2,1,0:T(8,128)(2,1)S(1)}, u32[]{:S(2)}, u32[]{:S(2)}) collective-permute-start(bf16[2,640,256]{2,1,0:T(8,128)(2,1)S(1)} %collective-permute-done.6.refs_5_.refs_9_), channel_id=1, source_target_pairs={{0,16},{16,0},{1,17},{17,1},{2,18},{18,2},{3,19},{19,3},{4,20},{20... | collective-permute-start | bytes 1966088 | tf_op jit(solution)/shard_map/ppermute | solution.py:176
  94.4 0.8 copy-done.9
  95.3 0.0 collective-permute-done.12.refs_14_
  95.3 0.8 copy-done.17
  96.1 1.1 collective-permute-done.11.refs_15_
  97.2 4.0 %collective-permute-start.14 = (bf16[2,640,256]{2,1,0:T(8,128)(2,1)}, bf16[2,640,256]{2,1,0:T(8,128)(2,1)}, u32[]{:S(2)}, u32[]{:S(2)}) collective-permute-start(bf16[2,640,256]{2,1,0:T(8,128)(2,1)} %collective-permute-done.11.refs_15_), channel_id=1, source_target_pairs={{0,16},{16,0},{1,17},{17,1},{2,18},{18,2},{3,19},{19,3},{4,20},{20... | collective-permute-start | bytes 1966088 | tf_op jit(solution)/shard_map/ppermute | solution.py:176
  101.2 3.0 %collective-permute-done.10.refs_13_ = bf16[2,640,256]{2,1,0:T(8,128)(2,1)} collective-permute-done((bf16[2,640,256]{2,1,0:T(8,128)(2,1)S(1)}, bf16[2,640,256]{2,1,0:T(8,128)(2,1)}, u32[]{:S(2)}, u32[]{:S(2)}) %collective-permute-start.10) | collective-permute-done | bytes 655392 | tf_op jit(solution)/shard_map/ppermute | solution.py:190
  104.2 0.0 collective-permute-done.8.refs_7_.refs_12_
  104.2 0.9 copy-done.13
  105.1 4.0 %collective-permute-start.13 = (bf16[2,640,256]{2,1,0:T(8,128)(2,1)}, bf16[2,640,256]{2,1,0:T(8,128)(2,1)}, u32[]{:S(2)}, u32[]{:S(2)}) collective-permute-start(bf16[2,640,256]{2,1,0:T(8,128)(2,1)} %collective-permute-done.10.refs_13_), channel_id=1, source_target_pairs={{0,16},{16,0},{1,17},{17,1},{2,18},{18,2},{3,19},{19,3},{4,20},{20... | collective-permute-start | bytes 1966088 | tf_op jit(solution)/shard_map/ppermute | solution.py:176
  109.1 0.1 pad_add_fusion.index_ref
  109.2 1.8 %shard_map.56.refs_0_ = f32[640,192]{1,0:T(8,128)S(1)} custom-call(s32[2]{0:T(128)S(1)} %pad_add_fusion.index_ref, bf16[1,3,64,4096]{3,2,1,0:T(8,128)(2,1)S(1)} %copy-done, bf16[2,640,256]{2,1,0:T(8,128)(2,1)S(1)} %bitcast.8, bf16[2,640,256]{2,1,0:T(8,128)(2,1)S(1)} %collective-permute-done.refs_1_.refs_3_), custom_call_target="tpu_custom_call" | custom-call | flops 125829120 | bytes 2883584 | tf_op jit(solution)/shard_map/pallas_call | solution.py:217
  111.1 1.1 copy-done.12
  112.1 1.1 copy-done.14
  113.2 5.1 %shard_map.57.refs_1_ = f32[640,192]{1,0:T(8,128)S(1)} custom-call(s32[2]{0:T(128)S(1)} %pad_add_fusion.index_ref, bf16[1,3,64,4096]{3,2,1,0:T(8,128)(2,1)S(1)} %copy-done, bf16[2,640,256]{2,1,0:T(8,128)(2,1)S(1)} %collective-permute-done.1.refs_0_.refs_4_, bf16[2,640,256]{2,1,0:T(8,128)(2,1)S(1)} %copy-done.6, bf16[2,640,256]{2,1,0:T(8,128)(2,1)S(1)} %copy-done.4, ...), custom_call_target="tpu_custom_call" | custom-call | flops 503316480 | bytes 6815744 | tf_op jit(solution)/shard_map/pallas_call | solution.py:217
  118.4 0.0 collective-permute-done.14.refs_17_
  118.4 0.0 collective-permute-done.13.refs_16_
  118.4 10.6 %shard_map.58 = bf16[1,3,64,4096]{3,2,1,0:T(8,128)(2,1)} custom-call(s32[2]{0:T(128)S(1)} %pad_add_fusion.index_ref, bf16[1,3,64,4096]{3,2,1,0:T(8,128)(2,1)S(1)} %copy-done, f32[640,192]{1,0:T(8,128)S(1)} %shard_map.56.refs_0_, f32[640,192]{1,0:T(8,128)S(1)} %shard_map.57.refs_1_, bf16[2,640,256]{2,1,0:T(8,128)(2,1)S(1)} %bitcast.9, ...), custom_call_target="tpu_custom_call" | custom-call | flops 2013265920 | bytes 13631488 | tf_op jit(solution)/shard_map/pallas_call | solution.py:236
  (26 shorter events, 0.0 us)
Async XLA Ops:
  0.0 109.2 %copy-start = (bf16[1,3,64,4096]{3,2,1,0:T(8,128)(2,1)S(1)}, bf16[1,3,64,4096]{3,2,1,0:T(8,128)(2,1)}, u32[]{:S(2)}) copy-start(bf16[1,3,64,4096]{3,2,1,0:T(8,128)(2,1)} %weights_ref.5) | copy-start | bytes 4718596
  32.8 18.2 %collective-permute-start.1 = (bf16[2,640,256]{2,1,0:T(8,128)(2,1)S(1)}, bf16[2,640,256]{2,1,0:T(8,128)(2,1)S(1)}, u32[]{:S(2)}, u32[]{:S(2)}) collective-permute-start(bf16[2,640,256]{2,1,0:T(8,128)(2,1)S(1)} %bitcast.6), channel_id=1, source_target_pairs={{0,32},{16,240},{32,64},{48,16},{64,96},{80,48},{96,128},{112,80},... | collective-permute-start | bytes 1966088 | tf_op jit(solution)/shard_map/ppermute | solution.py:190
  43.4 14.9 %collective-permute-start = (bf16[2,640,256]{2,1,0:T(8,128)(2,1)S(1)}, bf16[2,640,256]{2,1,0:T(8,128)(2,1)S(1)}, u32[]{:S(2)}, u32[]{:S(2)}) collective-permute-start(bf16[2,640,256]{2,1,0:T(8,128)(2,1)S(1)} %bitcast.7), channel_id=1, source_target_pairs={{0,16},{16,0},{1,17},{17,1},{2,18},{18,2},{3,19},{19,3},{4,20},{20... | collective-permute-start | bytes 1966088 | tf_op jit(solution)/shard_map/ppermute | solution.py:176
  50.9 12.5 %collective-permute-start.5 = (bf16[2,640,256]{2,1,0:T(8,128)(2,1)S(1)}, bf16[2,640,256]{2,1,0:T(8,128)(2,1)S(1)}, u32[]{:S(2)}, u32[]{:S(2)}) collective-permute-start(bf16[2,640,256]{2,1,0:T(8,128)(2,1)S(1)} %collective-permute-done.1.refs_0_.refs_4_), channel_id=1, source_target_pairs={{0,32},{16,240},{32,64},{48,16},{64,96},{80,48},{96,128},{112,80},... | collective-permute-start | bytes 1966088 | tf_op jit(solution)/shard_map/ppermute | solution.py:190
  56.0 7.5 %collective-permute-start.3 = (bf16[2,640,256]{2,1,0:T(8,128)(2,1)S(1)}, bf16[2,640,256]{2,1,0:T(8,128)(2,1)S(1)}, u32[]{:S(2)}, u32[]{:S(2)}) collective-permute-start(bf16[2,640,256]{2,1,0:T(8,128)(2,1)S(1)} %collective-permute-done.1.refs_0_.refs_4_), channel_id=1, source_target_pairs={{0,16},{16,0},{1,17},{17,1},{2,18},{18,2},{3,19},{19,3},{4,20},{20... | collective-permute-start | bytes 1966088 | tf_op jit(solution)/shard_map/ppermute | solution.py:176
  58.4 15.4 %collective-permute-start.2 = (bf16[2,640,256]{2,1,0:T(8,128)(2,1)S(1)}, bf16[2,640,256]{2,1,0:T(8,128)(2,1)S(1)}, u32[]{:S(2)}, u32[]{:S(2)}) collective-permute-start(bf16[2,640,256]{2,1,0:T(8,128)(2,1)S(1)} %collective-permute-done.refs_1_.refs_3_), channel_id=1, source_target_pairs={{0,32},{16,240},{32,64},{48,16},{64,96},{80,48},{96,128},{112,80},... | collective-permute-start | bytes 1966088 | tf_op jit(solution)/shard_map/ppermute | solution.py:190
  63.5 0.8 copy-start.3
  64.3 17.0 %collective-permute-start.9 = (bf16[2,640,256]{2,1,0:T(8,128)(2,1)S(1)}, bf16[2,640,256]{2,1,0:T(8,128)(2,1)S(1)}, u32[]{:S(2)}, u32[]{:S(2)}) collective-permute-start(bf16[2,640,256]{2,1,0:T(8,128)(2,1)S(1)} %collective-permute-done.5.refs_4_.refs_7_), channel_id=1, source_target_pairs={{0,32},{16,240},{32,64},{48,16},{64,96},{80,48},{96,128},{112,80},... | collective-permute-start | bytes 1966088 | tf_op jit(solution)/shard_map/ppermute | solution.py:190
  69.3 12.0 %collective-permute-start.7 = (bf16[2,640,256]{2,1,0:T(8,128)(2,1)S(1)}, bf16[2,640,256]{2,1,0:T(8,128)(2,1)S(1)}, u32[]{:S(2)}, u32[]{:S(2)}) collective-permute-start(bf16[2,640,256]{2,1,0:T(8,128)(2,1)S(1)} %collective-permute-done.5.refs_4_.refs_7_), channel_id=1, source_target_pairs={{0,16},{16,0},{1,17},{17,1},{2,18},{18,2},{3,19},{19,3},{4,20},{20... | collective-permute-start | bytes 1966088 | tf_op jit(solution)/shard_map/ppermute | solution.py:176
  72.9 0.8 copy-start.1
  73.7 14.6 %collective-permute-start.6 = (bf16[2,640,256]{2,1,0:T(8,128)(2,1)S(1)}, bf16[2,640,256]{2,1,0:T(8,128)(2,1)S(1)}, u32[]{:S(2)}, u32[]{:S(2)}) collective-permute-start(bf16[2,640,256]{2,1,0:T(8,128)(2,1)S(1)} %collective-permute-done.2.refs_1_.refs_5_), channel_id=1, source_target_pairs={{0,32},{16,240},{32,64},{48,16},{64,96},{80,48},{96,128},{112,80},... | collective-permute-start | bytes 1966088 | tf_op jit(solution)/shard_map/ppermute | solution.py:190
  78.6 9.8 %collective-permute-start.4 = (bf16[2,640,256]{2,1,0:T(8,128)(2,1)S(1)}, bf16[2,640,256]{2,1,0:T(8,128)(2,1)S(1)}, u32[]{:S(2)}, u32[]{:S(2)}) collective-permute-start(bf16[2,640,256]{2,1,0:T(8,128)(2,1)S(1)} %collective-permute-done.2.refs_1_.refs_5_), channel_id=1, source_target_pairs={{0,16},{16,0},{1,17},{17,1},{2,18},{18,2},{3,19},{19,3},{4,20},{20... | collective-permute-start | bytes 1966088 | tf_op jit(solution)/shard_map/ppermute | solution.py:176
  80.5 0.8 copy-start.5
  81.3 0.8 copy-start.7
  82.2 13.1 %collective-permute-start.12 = (bf16[2,640,256]{2,1,0:T(8,128)(2,1)S(1)}, bf16[2,640,256]{2,1,0:T(8,128)(2,1)S(1)}, u32[]{:S(2)}, u32[]{:S(2)}) collective-permute-start(bf16[2,640,256]{2,1,0:T(8,128)(2,1)S(1)} %collective-permute-done.9.refs_11_), channel_id=1, source_target_pairs={{0,16},{16,0},{1,17},{17,1},{2,18},{18,2},{3,19},{19,3},{4,20},{20... | collective-permute-start | bytes 1966088 | tf_op jit(solution)/shard_map/ppermute | solution.py:176
  85.5 11.7 %collective-permute-start.11 = (bf16[2,640,256]{2,1,0:T(8,128)(2,1)S(1)}, bf16[2,640,256]{2,1,0:T(8,128)(2,1)}, u32[]{:S(2)}, u32[]{:S(2)}) collective-permute-start(bf16[2,640,256]{2,1,0:T(8,128)(2,1)S(1)} %collective-permute-done.9.refs_11_), channel_id=1, source_target_pairs={{0,32},{16,240},{32,64},{48,16},{64,96},{80,48},{96,128},{112,80},... | collective-permute-start | bytes 1966088 | tf_op jit(solution)/shard_map/ppermute | solution.py:190
  87.5 0.8 copy-start.15
  88.4 0.9 copy-start.11
  89.2 15.0 %collective-permute-start.10 = (bf16[2,640,256]{2,1,0:T(8,128)(2,1)S(1)}, bf16[2,640,256]{2,1,0:T(8,128)(2,1)}, u32[]{:S(2)}, u32[]{:S(2)}) collective-permute-start(bf16[2,640,256]{2,1,0:T(8,128)(2,1)S(1)} %collective-permute-done.6.refs_5_.refs_9_), channel_id=1, source_target_pairs={{0,32},{16,240},{32,64},{48,16},{64,96},{80,48},{96,128},{112,80},... | collective-permute-start | bytes 1966088 | tf_op jit(solution)/shard_map/ppermute | solution.py:190
  92.0 12.3 %collective-permute-start.8 = (bf16[2,640,256]{2,1,0:T(8,128)(2,1)S(1)}, bf16[2,640,256]{2,1,0:T(8,128)(2,1)S(1)}, u32[]{:S(2)}, u32[]{:S(2)}) collective-permute-start(bf16[2,640,256]{2,1,0:T(8,128)(2,1)S(1)} %collective-permute-done.6.refs_5_.refs_9_), channel_id=1, source_target_pairs={{0,16},{16,0},{1,17},{17,1},{2,18},{18,2},{3,19},{19,3},{4,20},{20... | collective-permute-start | bytes 1966088 | tf_op jit(solution)/shard_map/ppermute | solution.py:176
  94.4 0.8 copy-start.9
  95.3 0.8 copy-start.17
  97.2 21.2 %collective-permute-start.14 = (bf16[2,640,256]{2,1,0:T(8,128)(2,1)}, bf16[2,640,256]{2,1,0:T(8,128)(2,1)}, u32[]{:S(2)}, u32[]{:S(2)}) collective-permute-start(bf16[2,640,256]{2,1,0:T(8,128)(2,1)} %collective-permute-done.11.refs_15_), channel_id=1, source_target_pairs={{0,16},{16,0},{1,17},{17,1},{2,18},{18,2},{3,19},{19,3},{4,20},{20... | collective-permute-start | bytes 1966088 | tf_op jit(solution)/shard_map/ppermute | solution.py:176
  104.2 0.9 copy-start.13
  105.1 13.3 %collective-permute-start.13 = (bf16[2,640,256]{2,1,0:T(8,128)(2,1)}, bf16[2,640,256]{2,1,0:T(8,128)(2,1)}, u32[]{:S(2)}, u32[]{:S(2)}) collective-permute-start(bf16[2,640,256]{2,1,0:T(8,128)(2,1)} %collective-permute-done.10.refs_13_), channel_id=1, source_target_pairs={{0,16},{16,0},{1,17},{17,1},{2,18},{18,2},{3,19},{19,3},{4,20},{20... | collective-permute-start | bytes 1966088 | tf_op jit(solution)/shard_map/ppermute | solution.py:176
  109.2 1.8 %copy-start.2 = (bf16[2,640,256]{2,1,0:T(8,128)(2,1)S(1)}, bf16[2,640,256]{2,1,0:T(8,128)(2,1)}, u32[]{:S(2)}) copy-start(bf16[2,640,256]{2,1,0:T(8,128)(2,1)} %copy-done.1) | copy-start | bytes 1966084
  109.2 1.9 %copy-start.4 = (bf16[2,640,256]{2,1,0:T(8,128)(2,1)S(1)}, bf16[2,640,256]{2,1,0:T(8,128)(2,1)}, u32[]{:S(2)}) copy-start(bf16[2,640,256]{2,1,0:T(8,128)(2,1)} %copy-done.3) | copy-start | bytes 1966084
  109.2 1.9 %copy-start.6 = (bf16[2,640,256]{2,1,0:T(8,128)(2,1)S(1)}, bf16[2,640,256]{2,1,0:T(8,128)(2,1)}, u32[]{:S(2)}) copy-start(bf16[2,640,256]{2,1,0:T(8,128)(2,1)} %copy-done.5) | copy-start | bytes 1966084
  109.2 1.9 %copy-start.8 = (bf16[2,640,256]{2,1,0:T(8,128)(2,1)S(1)}, bf16[2,640,256]{2,1,0:T(8,128)(2,1)}, u32[]{:S(2)}) copy-start(bf16[2,640,256]{2,1,0:T(8,128)(2,1)} %copy-done.7) | copy-start | bytes 1966084
  109.2 1.9 %copy-start.10 = (bf16[2,640,256]{2,1,0:T(8,128)(2,1)S(1)}, bf16[2,640,256]{2,1,0:T(8,128)(2,1)}, u32[]{:S(2)}) copy-start(bf16[2,640,256]{2,1,0:T(8,128)(2,1)} %copy-done.9) | copy-start | bytes 1966084
  111.1 1.1 copy-start.12
  112.1 1.1 copy-start.14
  113.2 5.2 %copy-start.16 = (bf16[2,640,256]{2,1,0:T(8,128)(2,1)S(1)}, bf16[2,640,256]{2,1,0:T(8,128)(2,1)}, u32[]{:S(2)}) copy-start(bf16[2,640,256]{2,1,0:T(8,128)(2,1)} %copy-done.15) | copy-start | bytes 1966084
  113.2 5.2 %copy-start.18 = (bf16[2,640,256]{2,1,0:T(8,128)(2,1)S(1)}, bf16[2,640,256]{2,1,0:T(8,128)(2,1)}, u32[]{:S(2)}) copy-start(bf16[2,640,256]{2,1,0:T(8,128)(2,1)} %copy-done.17) | copy-start | bytes 1966084
where the time goes:
time: 130 us; the launch traced here: 129 us
  starting transfers between devices  58.6 us (45%)
  blocking collectives  30.5 us (23%)
  Pallas kernels  19.8 us (15%)
  waiting for transfers between devices  9.98 us (8%)
  local copies, waits for them, and re-layouts  9.77 us (8%)
    ppermute x7, starting transfers between devices, device_step(): piece = lax.ppermute(held[step - 1, chain, 0], ('ring', 'core'), around)  35.1 us
    all_to_all x1, blocking collectives, device_step(): lax.all_to_all(send.reshape(2 * groups, CAP, 2 * width), ('half', 'expert...  30.5 us
    ppermute x8, starting transfers between devices, swapped(): return lax.ppermute(x, 'core', [(0, 1), (1, 0)])  23.5 us
    pallas_call x1, Pallas kernels, device_step(): pl.pallas_call(functools.partial(grads_kernel, ring_size, blocks, early,...  10.6 us
    ppermute x7, waiting for transfers between devices, device_step(): piece = lax.ppermute(held[step - 1, chain, 0], ('ring', 'core'), around)  9.96 us
    unnamed x38, local copies, waits for them, and re-layouts  9.77 us
    pallas_call x2, Pallas kernels, device_step(): pl.pallas_call(functools.partial(forward_kernel, ring_size, chosen), out_...  6.92 us
  transfers between devices with their start and end apart: 15, of which 4 were waited for; matrix products, arithmetic and copies ran while one was open for 0% of the time, Pallas kernels for 5%

commit v1 on v0

--- a/solution.py
+++ b/solution.py
@@ -11,8 +11,10 @@
 CAP = 40
 BF16 = jnp.bfloat16
 F32 = jnp.float32
-EARLY_VMEM = 12 << 20
-GRADS_VMEM = 18 << 20
+EARLY_VMEM = 60 << 20
+GRADS_VMEM = 60 << 20
+FORWARD_GROUP = 4
+GRADS_GROUP = 4
 
 
 def pack_kernel(routes_ref, gates_ref, tokens_ref, cotangent_ref, out_ref):
@@ -66,8 +68,16 @@
     return pl.multiple_of(((j * ring_size + z) * 2 + c) * half, half)
 
 
-def add_forward(index_ref, ring_size, weights_buf, total, piece, block):
-    halves, half = piece.shape[0], piece.shape[2] // 2
+def joined(pieces, part):
+    half = pieces[0].shape[2] // 2
+    cut = slice(part * half, (part + 1) * half)
+    return jnp.concatenate(
+        [piece[j, :, cut] for piece in pieces for j in range(piece.shape[0])], axis=1
+    )
+
+
+def add_forward(index_ref, ring_size, weights_buf, total, pieces, blocks):
+    halves, half = pieces[0].shape[0], pieces[0].shape[2] // 2
     hidden_units = weights_buf.shape[2]
     along = (((1,), (1,)), ((), ()))
 
@@ -75,6 +85,7 @@
         return jnp.concatenate(
             [
                 weights_buf[0, m, :, pl.ds(column(index_ref, ring_size, half, block, j), half)]
+                for block in blocks
                 for j in range(halves)
             ],
             axis=1,
@@ -82,17 +93,11 @@
 
     pair = jnp.concatenate([weight_block(0), weight_block(1)], axis=0)
     total[:, : 2 * hidden_units] += lax.dot_general(
-        joined(piece, 0), pair, along, preferred_element_type=F32
+        joined(pieces, 0), pair, along, preferred_element_type=F32
     )
     total[:, 2 * hidden_units :] += lax.dot_general(
-        joined(piece, 1), weight_block(2), along, preferred_element_type=F32
-    )
-
-
-def joined(piece, part):
-    halves, half = piece.shape[0], piece.shape[2] // 2
-    cut = slice(part * half, (part + 1) * half)
-    return jnp.concatenate([piece[j, :, cut] for j in range(halves)], axis=1)
+        joined(pieces, 1), weight_block(2), along, preferred_element_type=F32
+    )
 
 
 def forward_kernel(ring_size, blocks, index_ref, weights_ref, *refs):
@@ -104,9 +109,14 @@
     )
     total[...] = jnp.zeros_like(total)
     copies[0].wait()
-    for k, block in enumerate(blocks):
-        copies[1 + k].wait()
-        add_forward(index_ref, ring_size, weights_buf, total, pieces_buf.at[k], block)
+    for k in range(0, count, FORWARD_GROUP):
+        chosen = range(k, min(k + FORWARD_GROUP, count))
+        for n in chosen:
+            copies[1 + n].wait()
+        add_forward(
+            index_ref, ring_size, weights_buf, total,
+            [pieces_buf.at[n] for n in chosen], [blocks[n] for n in chosen],
+        )
 
 
 def grads_kernel(ring_size, blocks, early, sums, index_ref, weights_ref, *refs):
@@ -130,9 +140,14 @@
         running = running + partial_buf[m]
     total[...] = running
     hidden_units = weights_buf.shape[2]
-    for n, k in enumerate(late):
-        copies[base + n].wait()
-        add_forward(index_ref, ring_size, weights_buf, total, pieces_buf.at[k], blocks[k])
+    for n in range(0, len(late), FORWARD_GROUP):
+        chosen = late[n : n + FORWARD_GROUP]
+        for m in range(len(chosen)):
+            copies[base + n + m].wait()
+        add_forward(
+            index_ref, ring_size, weights_buf, total,
+            [pieces_buf.at[k] for k in chosen], [blocks[k] for k in chosen],
+        )
     gate_part = total[:, :hidden_units]
     up_part = total[:, hidden_units : 2 * hidden_units]
     back_hidden = total[:, 2 * hidden_units :]
@@ -144,18 +159,21 @@
     pre_up = (back_hidden * silu).astype(BF16)
     both = jnp.concatenate([pre_gate, pre_up], axis=1).T
     hidden_t = hidden.T
-    for n, k in enumerate(order):
-        if n >= len(late):
-            copies[base + n].wait()
-        piece = pieces_buf.at[k]
-        ins = jnp.dot(both, joined(piece, 0), preferred_element_type=F32).astype(BF16)
-        outs = jnp.dot(hidden_t, joined(piece, 1), preferred_element_type=F32).astype(BF16)
-        for j in range(halves):
-            cols = pl.ds(column(index_ref, ring_size, half, blocks[k], j), half)
-            cut = slice(j * half, (j + 1) * half)
-            out_ref[0, 0, :, cols] = ins[:hidden_units, cut]
-            out_ref[0, 1, :, cols] = ins[hidden_units:, cut]
-            out_ref[0, 2, :, cols] = outs[:, cut]
+    for n in range(0, count, GRADS_GROUP):
+        chosen = order[n : n + GRADS_GROUP]
+        for m in range(len(chosen)):
+            if n + m >= len(late):
+                copies[base + n + m].wait()
+        pieces = [pieces_buf.at[k] for k in chosen]
+        ins = jnp.dot(both, joined(pieces, 0), preferred_element_type=F32).astype(BF16)
+        outs = jnp.dot(hidden_t, joined(pieces, 1), preferred_element_type=F32).astype(BF16)
+        for m, k in enumerate(chosen):
+            for j in range(halves):
+                cols = pl.ds(column(index_ref, ring_size, half, blocks[k], j), half)
+                cut = slice((m * halves + j) * half, (m * halves + j + 1) * half)
+                out_ref[0, 0, :, cols] = ins[:hidden_units, cut]
+                out_ref[0, 1, :, cols] = ins[hidden_units:, cut]
+                out_ref[0, 2, :, cols] = outs[:, cut]
 
 
 def device_step(tokens, cotangent, routes, gates, expert_weights):

time: 130 us -> 126 us (0.969)
  local copies, waits for them, and re-layouts: 9.77 us -> 0.05 us
  starting transfers between devices: 58.6 us -> 62.3 us
  waiting for transfers between devices: 9.98 us -> 11.6 us
    unnamed x38 -> x24, local copies, waits for them, and re-layouts: 9.77 us -> 0.05 us
    ppermute x8, starting transfers between devices: 23.5 us -> 26.3 us  [swapped(): return lax.ppermute(x, 'core', [(0, 1), (1, 0)])]
    pallas_call x2, Pallas kernels: 6.92 us -> 9.28 us  [device_step(): pl.pallas_call(functools.partial(forward_kernel, ring_size, chosen), out_...]
    pallas_call x1, Pallas kernels: 10.6 us -> 8.46 us  [device_step(): pl.pallas_call(functools.partial(grads_kernel, ring_size, blocks, early,...]
    ppermute x7, waiting for transfers between devices: 9.96 us -> 11.6 us  [device_step(): piece = lax.ppermute(held[step - 1, chain, 0], ('ring', 'core'), around)]
  transfers between devices with their start and end apart: 15 -> 15, of which waited for: 4 -> 4; matrix products, arithmetic and copies ran while one was open for 0% -> 1% of each run, Pallas kernels for 5% -> 7%
where the time goes in v1:
time: 126 us; the launch traced here: 125 us
  starting transfers between devices  62.3 us (49%)
  blocking collectives  30.5 us (24%)
  Pallas kernels  19.8 us (16%)
  waiting for transfers between devices  11.6 us (9%)
    ppermute x7, starting transfers between devices, device_step(): piece = lax.ppermute(held[step - 1, chain, 0], ('ring', 'core'), around)  36 us
    all_to_all x1, blocking collectives, device_step(): lax.all_to_all(send.reshape(2 * groups, CAP, 2 * width), ('half', 'expert...  30.5 us
    ppermute x8, starting transfers between devices, swapped(): return lax.ppermute(x, 'core', [(0, 1), (1, 0)])  26.3 us
    ppermute x7, waiting for transfers between devices, device_step(): piece = lax.ppermute(held[step - 1, chain, 0], ('ring', 'core'), around)  11.6 us
    pallas_call x2, Pallas kernels, device_step(): pl.pallas_call(functools.partial(forward_kernel, ring_size, chosen), out_...  9.28 us
    pallas_call x1, Pallas kernels, device_step(): pl.pallas_call(functools.partial(grads_kernel, ring_size, blocks, early,...  8.46 us
  transfers between devices with their start and end apart: 15, of which 4 were waited for; matrix products, arithmetic and copies ran while one was open for 1% of the time, Pallas kernels for 7%

profile of v1, /device:TPU:1, one launch (start us, length us, event | category | flops | bytes accessed | tf_op | source)
XLA Modules:
  0.0 125.3 jit_solution(11405867781533357379)
XLA Ops:
  0.0 2.1 %shard_map.55 = bf16[2,640,256]{2,1,0:T(8,128)(2,1)} custom-call(s32[2,128]{1,0:T(2,128)} %bitcast.11, f32[2,128]{1,0:T(2,128)} %bitcast.12, bf16[128,128]{1,0:T(8,128)(2,1)} %tokens_ref.1, bf16[128,128]{1,0:T(8,128)(2,1)} %cotangent_ref.1), custom_call_target="tpu_custom_call" | custom-call | tf_op jit(solution)/shard_map/pallas_call | solution.py:184
  2.1 30.5 %all_to_all.5 = bf16[32,40,256]{2,1,0:T(8,128)(2,1)S(1)} all-to-all(bf16[32,40,256]{2,1,0:T(8,128)(2,1)} %bitcast.10), channel_id=1, replica_groups=mesh['half'=2,'ring'=8,'core'=2,'expert'=16] {'half','expert'}, dimensions={0} | all-to-all | bytes 1310720 | tf_op jit(solution)/shard_map/all_to_all | solution.py:196
  32.6 10.7 %collective-permute-start.1 = (bf16[2,640,256]{2,1,0:T(8,128)(2,1)S(1)}, bf16[2,640,256]{2,1,0:T(8,128)(2,1)S(1)}, u32[]{:S(2)}, u32[]{:S(2)}) collective-permute-start(bf16[2,640,256]{2,1,0:T(8,128)(2,1)S(1)} %bitcast.6), channel_id=1, source_target_pairs={{0,32},{16,240},{32,64},{48,16},{64,96},{80,48},{96,128},{112,80},... | collective-permute-start | bytes 1966088 | tf_op jit(solution)/shard_map/ppermute | solution.py:208
  43.3 1.9 %collective-permute-start = (bf16[2,640,256]{2,1,0:T(8,128)(2,1)S(1)}, bf16[2,640,256]{2,1,0:T(8,128)(2,1)S(1)}, u32[]{:S(2)}, u32[]{:S(2)}) collective-permute-start(bf16[2,640,256]{2,1,0:T(8,128)(2,1)S(1)} %bitcast.7), channel_id=1, source_target_pairs={{0,16},{16,0},{1,17},{17,1},{2,18},{18,2},{3,19},{19,3},{4,20},{20... | collective-permute-start | bytes 1966088 | tf_op jit(solution)/shard_map/ppermute | solution.py:194
  45.2 5.6 %collective-permute-done.1.refs_0_.refs_4_ = bf16[2,640,256]{2,1,0:T(8,128)(2,1)S(1)} collective-permute-done((bf16[2,640,256]{2,1,0:T(8,128)(2,1)S(1)}, bf16[2,640,256]{2,1,0:T(8,128)(2,1)S(1)}, u32[]{:S(2)}, u32[]{:S(2)}) %collective-permute-start.1) | collective-permute-done | bytes 655392 | tf_op jit(solution)/shard_map/ppermute | solution.py:208
  50.8 5.0 %collective-permute-start.5 = (bf16[2,640,256]{2,1,0:T(8,128)(2,1)S(1)}, bf16[2,640,256]{2,1,0:T(8,128)(2,1)S(1)}, u32[]{:S(2)}, u32[]{:S(2)}) collective-permute-start(bf16[2,640,256]{2,1,0:T(8,128)(2,1)S(1)} %collective-permute-done.1.refs_0_.refs_4_), channel_id=1, source_target_pairs={{0,32},{16,240},{32,64},{48,16},{64,96},{80,48},{96,128},{112,80},... | collective-permute-start | bytes 1966088 | tf_op jit(solution)/shard_map/ppermute | solution.py:208
  55.8 2.4 %collective-permute-start.3 = (bf16[2,640,256]{2,1,0:T(8,128)(2,1)S(1)}, bf16[2,640,256]{2,1,0:T(8,128)(2,1)S(1)}, u32[]{:S(2)}, u32[]{:S(2)}) collective-permute-start(bf16[2,640,256]{2,1,0:T(8,128)(2,1)S(1)} %collective-permute-done.1.refs_0_.refs_4_), channel_id=1, source_target_pairs={{0,16},{16,0},{1,17},{17,1},{2,18},{18,2},{3,19},{19,3},{4,20},{20... | collective-permute-start | bytes 1966088 | tf_op jit(solution)/shard_map/ppermute | solution.py:194
  58.2 0.0 collective-permute-done.refs_1_.refs_3_
  58.2 0.0 copy-start.2
  58.2 4.9 %collective-permute-start.2 = (bf16[2,640,256]{2,1,0:T(8,128)(2,1)S(1)}, bf16[2,640,256]{2,1,0:T(8,128)(2,1)S(1)}, u32[]{:S(2)}, u32[]{:S(2)}) collective-permute-start(bf16[2,640,256]{2,1,0:T(8,128)(2,1)S(1)} %collective-permute-done.refs_1_.refs_3_), channel_id=1, source_target_pairs={{0,32},{16,240},{32,64},{48,16},{64,96},{80,48},{96,128},{112,80},... | collective-permute-start | bytes 1966088 | tf_op jit(solution)/shard_map/ppermute | solution.py:208
  63.1 0.2 collective-permute-done.5.refs_4_.refs_7_
  63.3 0.0 collective-permute-done.3.refs_2_.refs_6_
  63.4 5.0 %collective-permute-start.9 = (bf16[2,640,256]{2,1,0:T(8,128)(2,1)S(1)}, bf16[2,640,256]{2,1,0:T(8,128)(2,1)S(1)}, u32[]{:S(2)}, u32[]{:S(2)}) collective-permute-start(bf16[2,640,256]{2,1,0:T(8,128)(2,1)S(1)} %collective-permute-done.5.refs_4_.refs_7_), channel_id=1, source_target_pairs={{0,32},{16,240},{32,64},{48,16},{64,96},{80,48},{96,128},{112,80},... | collective-permute-start | bytes 1966088 | tf_op jit(solution)/shard_map/ppermute | solution.py:208
  68.4 3.5 %collective-permute-start.7 = (bf16[2,640,256]{2,1,0:T(8,128)(2,1)S(1)}, bf16[2,640,256]{2,1,0:T(8,128)(2,1)S(1)}, u32[]{:S(2)}, u32[]{:S(2)}) collective-permute-start(bf16[2,640,256]{2,1,0:T(8,128)(2,1)S(1)} %collective-permute-done.5.refs_4_.refs_7_), channel_id=1, source_target_pairs={{0,16},{16,0},{1,17},{17,1},{2,18},{18,2},{3,19},{19,3},{4,20},{20... | collective-permute-start | bytes 1966088 | tf_op jit(solution)/shard_map/ppermute | solution.py:194
  71.9 0.0 collective-permute-done.2.refs_1_.refs_5_
  71.9 0.0 copy-start.5
  71.9 4.9 %collective-permute-start.6 = (bf16[2,640,256]{2,1,0:T(8,128)(2,1)S(1)}, bf16[2,640,256]{2,1,0:T(8,128)(2,1)S(1)}, u32[]{:S(2)}, u32[]{:S(2)}) collective-permute-start(bf16[2,640,256]{2,1,0:T(8,128)(2,1)S(1)} %collective-permute-done.2.refs_1_.refs_5_), channel_id=1, source_target_pairs={{0,32},{16,240},{32,64},{48,16},{64,96},{80,48},{96,128},{112,80},... | collective-permute-start | bytes 1966088 | tf_op jit(solution)/shard_map/ppermute | solution.py:208
  76.8 2.1 %collective-permute-start.4 = (bf16[2,640,256]{2,1,0:T(8,128)(2,1)S(1)}, bf16[2,640,256]{2,1,0:T(8,128)(2,1)S(1)}, u32[]{:S(2)}, u32[]{:S(2)}) collective-permute-start(bf16[2,640,256]{2,1,0:T(8,128)(2,1)S(1)} %collective-permute-done.2.refs_1_.refs_5_), channel_id=1, source_target_pairs={{0,16},{16,0},{1,17},{17,1},{2,18},{18,2},{3,19},{19,3},{4,20},{20... | collective-permute-start | bytes 1966088 | tf_op jit(solution)/shard_map/ppermute | solution.py:194
  78.9 0.0 collective-permute-done.9.refs_11_
  78.9 0.0 copy-start.10
  79.0 0.0 collective-permute-done.7.refs_6_.refs_10_
  79.0 0.0 copy-done.5
  79.0 0.0 copy-start.6
  79.0 5.1 %collective-permute-start.12 = (bf16[2,640,256]{2,1,0:T(8,128)(2,1)S(1)}, bf16[2,640,256]{2,1,0:T(8,128)(2,1)S(1)}, u32[]{:S(2)}, u32[]{:S(2)}) collective-permute-start(bf16[2,640,256]{2,1,0:T(8,128)(2,1)S(1)} %collective-permute-done.9.refs_11_), channel_id=1, source_target_pairs={{0,16},{16,0},{1,17},{17,1},{2,18},{18,2},{3,19},{19,3},{4,20},{20... | collective-permute-start | bytes 1966088 | tf_op jit(solution)/shard_map/ppermute | solution.py:194
  84.1 2.4 %collective-permute-start.11 = (bf16[2,640,256]{2,1,0:T(8,128)(2,1)S(1)}, bf16[2,640,256]{2,1,0:T(8,128)(2,1)}, u32[]{:S(2)}, u32[]{:S(2)}) collective-permute-start(bf16[2,640,256]{2,1,0:T(8,128)(2,1)S(1)} %collective-permute-done.9.refs_11_), channel_id=1, source_target_pairs={{0,32},{16,240},{32,64},{48,16},{64,96},{80,48},{96,128},{112,80},... | collective-permute-start | bytes 1966088 | tf_op jit(solution)/shard_map/ppermute | solution.py:208
  86.5 0.0 collective-permute-done.6.refs_5_.refs_9_
  86.5 0.0 copy-start.7
  86.5 0.0 collective-permute-done.4.refs_3_.refs_8_
  86.5 0.0 copy-done.6
  86.5 0.0 copy-start.8
  86.5 3.2 %collective-permute-start.10 = (bf16[2,640,256]{2,1,0:T(8,128)(2,1)S(1)}, bf16[2,640,256]{2,1,0:T(8,128)(2,1)}, u32[]{:S(2)}, u32[]{:S(2)}) collective-permute-start(bf16[2,640,256]{2,1,0:T(8,128)(2,1)S(1)} %collective-permute-done.6.refs_5_.refs_9_), channel_id=1, source_target_pairs={{0,32},{16,240},{32,64},{48,16},{64,96},{80,48},{96,128},{112,80},... | collective-permute-start | bytes 1966088 | tf_op jit(solution)/shard_map/ppermute | solution.py:208
  89.7 0.0 copy-done.7
  89.7 3.3 %collective-permute-start.8 = (bf16[2,640,256]{2,1,0:T(8,128)(2,1)S(1)}, bf16[2,640,256]{2,1,0:T(8,128)(2,1)S(1)}, u32[]{:S(2)}, u32[]{:S(2)}) collective-permute-start(bf16[2,640,256]{2,1,0:T(8,128)(2,1)S(1)} %collective-permute-done.6.refs_5_.refs_9_), channel_id=1, source_target_pairs={{0,16},{16,0},{1,17},{17,1},{2,18},{18,2},{3,19},{19,3},{4,20},{20... | collective-permute-start | bytes 1966088 | tf_op jit(solution)/shard_map/ppermute | solution.py:194
  93.0 0.0 collective-permute-done.12.refs_14_
  93.0 0.0 copy-start.11
  93.0 2.7 %collective-permute-done.11.refs_15_ = bf16[2,640,256]{2,1,0:T(8,128)(2,1)} collective-permute-done((bf16[2,640,256]{2,1,0:T(8,128)(2,1)S(1)}, bf16[2,640,256]{2,1,0:T(8,128)(2,1)}, u32[]{:S(2)}, u32[]{:S(2)}) %collective-permute-start.11) | collective-permute-done | bytes 655392 | tf_op jit(solution)/shard_map/ppermute | solution.py:208
  95.8 4.0 %collective-permute-start.14 = (bf16[2,640,256]{2,1,0:T(8,128)(2,1)}, bf16[2,640,256]{2,1,0:T(8,128)(2,1)}, u32[]{:S(2)}, u32[]{:S(2)}) collective-permute-start(bf16[2,640,256]{2,1,0:T(8,128)(2,1)} %collective-permute-done.11.refs_15_), channel_id=1, source_target_pairs={{0,16},{16,0},{1,17},{17,1},{2,18},{18,2},{3,19},{19,3},{4,20},{20... | collective-permute-start | bytes 1966088 | tf_op jit(solution)/shard_map/ppermute | solution.py:194
  99.8 3.0 %collective-permute-done.10.refs_13_ = bf16[2,640,256]{2,1,0:T(8,128)(2,1)} collective-permute-done((bf16[2,640,256]{2,1,0:T(8,128)(2,1)S(1)}, bf16[2,640,256]{2,1,0:T(8,128)(2,1)}, u32[]{:S(2)}, u32[]{:S(2)}) %collective-permute-start.10) | collective-permute-done | bytes 655392 | tf_op jit(solution)/shard_map/ppermute | solution.py:208
  102.8 0.0 collective-permute-done.8.refs_7_.refs_12_
  102.8 0.0 copy-done.8
  102.8 4.0 %collective-permute-start.13 = (bf16[2,640,256]{2,1,0:T(8,128)(2,1)}, bf16[2,640,256]{2,1,0:T(8,128)(2,1)}, u32[]{:S(2)}, u32[]{:S(2)}) collective-permute-start(bf16[2,640,256]{2,1,0:T(8,128)(2,1)} %collective-permute-done.10.refs_13_), channel_id=1, source_target_pairs={{0,16},{16,0},{1,17},{17,1},{2,18},{18,2},{3,19},{19,3},{4,20},{20... | collective-permute-start | bytes 1966088 | tf_op jit(solution)/shard_map/ppermute | solution.py:194
  106.8 0.0 copy-done.10
  106.8 0.7 pad_add_fusion.index_ref
  107.5 3.8 %shard_map.56.refs_0_ = f32[640,192]{1,0:T(8,128)} custom-call(s32[2]{0:T(128)} %pad_add_fusion.index_ref, bf16[1,3,64,4096]{3,2,1,0:T(8,128)(2,1)} %weights_ref.5, bf16[2,640,256]{2,1,0:T(8,128)(2,1)} %bitcast.8, bf16[2,640,256]{2,1,0:T(8,128)(2,1)} %copy-done.2), custom_call_target="tpu_custom_call" | custom-call | flops 125829120 | bytes 2883584 | tf_op jit(solution)/shard_map/pallas_call | solution.py:235
  111.4 5.5 %shard_map.57.refs_1_ = f32[640,192]{1,0:T(8,128)} custom-call(s32[2]{0:T(128)} %pad_add_fusion.index_ref, bf16[1,3,64,4096]{3,2,1,0:T(8,128)(2,1)} %weights_ref.5, bf16[2,640,256]{2,1,0:T(8,128)(2,1)} %copy-done.1, bf16[2,640,256]{2,1,0:T(8,128)(2,1)} %copy-done.5, bf16[2,640,256]{2,1,0:T(8,128)(2,1)} %copy-done.4, bf16[2,640,256]{2,1,0:T(8,128)(2,1)} %copy-done.8, ...), custom_call_target="tpu_custom_call" | custom-call | flops 503316480 | bytes 6815744 | tf_op jit(solution)/shard_map/pallas_call | solution.py:235
  116.8 0.0 collective-permute-done.14.refs_17_
  116.9 0.0 collective-permute-done.13.refs_16_
  116.9 8.5 %shard_map.58 = bf16[1,3,64,4096]{3,2,1,0:T(8,128)(2,1)} custom-call(s32[2]{0:T(128)} %pad_add_fusion.index_ref, bf16[1,3,64,4096]{3,2,1,0:T(8,128)(2,1)} %weights_ref.5, f32[640,192]{1,0:T(8,128)} %shard_map.56.refs_0_, f32[640,192]{1,0:T(8,128)} %shard_map.57.refs_1_, bf16[2,640,256]{2,1,0:T(8,128)(2,1)} %bitcast.9, bf16[2,640,256]{2,1,0:T(8,128)(2,1)} %copy-done.2, ...), custom_call_target="tpu_custom_call" | custom-call | flops 2013265920 | bytes 13631488 | tf_op jit(solution)/shard_map/pallas_call | solution.py:254
  (12 shorter events, 0.0 us)
Async XLA Ops:
  32.6 74.9 %copy-start = (bf16[32,40,256]{2,1,0:T(8,128)(2,1)}, bf16[32,40,256]{2,1,0:T(8,128)(2,1)S(1)}, u32[]{:S(2)}) copy-start(bf16[32,40,256]{2,1,0:T(8,128)(2,1)S(1)} %all_to_all.5) | copy-start | bytes 1966084
  32.6 18.2 %collective-permute-start.1 = (bf16[2,640,256]{2,1,0:T(8,128)(2,1)S(1)}, bf16[2,640,256]{2,1,0:T(8,128)(2,1)S(1)}, u32[]{:S(2)}, u32[]{:S(2)}) collective-permute-start(bf16[2,640,256]{2,1,0:T(8,128)(2,1)S(1)} %bitcast.6), channel_id=1, source_target_pairs={{0,32},{16,240},{32,64},{48,16},{64,96},{80,48},{96,128},{112,80},... | collective-permute-start | bytes 1966088 | tf_op jit(solution)/shard_map/ppermute | solution.py:208
  43.3 14.9 %collective-permute-start = (bf16[2,640,256]{2,1,0:T(8,128)(2,1)S(1)}, bf16[2,640,256]{2,1,0:T(8,128)(2,1)S(1)}, u32[]{:S(2)}, u32[]{:S(2)}) collective-permute-start(bf16[2,640,256]{2,1,0:T(8,128)(2,1)S(1)} %bitcast.7), channel_id=1, source_target_pairs={{0,16},{16,0},{1,17},{17,1},{2,18},{18,2},{3,19},{19,3},{4,20},{20... | collective-permute-start | bytes 1966088 | tf_op jit(solution)/shard_map/ppermute | solution.py:194
  50.8 60.5 %copy-start.1 = (bf16[2,640,256]{2,1,0:T(8,128)(2,1)}, bf16[2,640,256]{2,1,0:T(8,128)(2,1)S(1)}, u32[]{:S(2)}) copy-start(bf16[2,640,256]{2,1,0:T(8,128)(2,1)S(1)} %collective-permute-done.1.refs_0_.refs_4_) | copy-start | bytes 1966084
  50.8 12.5 %collective-permute-start.5 = (bf16[2,640,256]{2,1,0:T(8,128)(2,1)S(1)}, bf16[2,640,256]{2,1,0:T(8,128)(2,1)S(1)}, u32[]{:S(2)}, u32[]{:S(2)}) collective-permute-start(bf16[2,640,256]{2,1,0:T(8,128)(2,1)S(1)} %collective-permute-done.1.refs_0_.refs_4_), channel_id=1, source_target_pairs={{0,32},{16,240},{32,64},{48,16},{64,96},{80,48},{96,128},{112,80},... | collective-permute-start | bytes 1966088 | tf_op jit(solution)/shard_map/ppermute | solution.py:208
  55.8 7.5 %collective-permute-start.3 = (bf16[2,640,256]{2,1,0:T(8,128)(2,1)S(1)}, bf16[2,640,256]{2,1,0:T(8,128)(2,1)S(1)}, u32[]{:S(2)}, u32[]{:S(2)}) collective-permute-start(bf16[2,640,256]{2,1,0:T(8,128)(2,1)S(1)} %collective-permute-done.1.refs_0_.refs_4_), channel_id=1, source_target_pairs={{0,16},{16,0},{1,17},{17,1},{2,18},{18,2},{3,19},{19,3},{4,20},{20... | collective-permute-start | bytes 1966088 | tf_op jit(solution)/shard_map/ppermute | solution.py:194
  58.2 49.3 %copy-start.2 = (bf16[2,640,256]{2,1,0:T(8,128)(2,1)}, bf16[2,640,256]{2,1,0:T(8,128)(2,1)S(1)}, u32[]{:S(2)}) copy-start(bf16[2,640,256]{2,1,0:T(8,128)(2,1)S(1)} %collective-permute-done.refs_1_.refs_3_) | copy-start | bytes 1966084
  58.2 13.7 %collective-permute-start.2 = (bf16[2,640,256]{2,1,0:T(8,128)(2,1)S(1)}, bf16[2,640,256]{2,1,0:T(8,128)(2,1)S(1)}, u32[]{:S(2)}, u32[]{:S(2)}) collective-permute-start(bf16[2,640,256]{2,1,0:T(8,128)(2,1)S(1)} %collective-permute-done.refs_1_.refs_3_), channel_id=1, source_target_pairs={{0,32},{16,240},{32,64},{48,16},{64,96},{80,48},{96,128},{112,80},... | collective-permute-start | bytes 1966088 | tf_op jit(solution)/shard_map/ppermute | solution.py:208
  63.3 48.0 %copy-start.3 = (bf16[2,640,256]{2,1,0:T(8,128)(2,1)}, bf16[2,640,256]{2,1,0:T(8,128)(2,1)S(1)}, u32[]{:S(2)}) copy-start(bf16[2,640,256]{2,1,0:T(8,128)(2,1)S(1)} %collective-permute-done.5.refs_4_.refs_7_) | copy-start | bytes 1966084
  63.3 48.0 %copy-start.4 = (bf16[2,640,256]{2,1,0:T(8,128)(2,1)}, bf16[2,640,256]{2,1,0:T(8,128)(2,1)S(1)}, u32[]{:S(2)}) copy-start(bf16[2,640,256]{2,1,0:T(8,128)(2,1)S(1)} %collective-permute-done.3.refs_2_.refs_6_) | copy-start | bytes 1966084
  63.4 15.6 %collective-permute-start.9 = (bf16[2,640,256]{2,1,0:T(8,128)(2,1)S(1)}, bf16[2,640,256]{2,1,0:T(8,128)(2,1)S(1)}, u32[]{:S(2)}, u32[]{:S(2)}) collective-permute-start(bf16[2,640,256]{2,1,0:T(8,128)(2,1)S(1)} %collective-permute-done.5.refs_4_.refs_7_), channel_id=1, source_target_pairs={{0,32},{16,240},{32,64},{48,16},{64,96},{80,48},{96,128},{112,80},... | collective-permute-start | bytes 1966088 | tf_op jit(solution)/shard_map/ppermute | solution.py:208
  68.4 10.6 %collective-permute-start.7 = (bf16[2,640,256]{2,1,0:T(8,128)(2,1)S(1)}, bf16[2,640,256]{2,1,0:T(8,128)(2,1)S(1)}, u32[]{:S(2)}, u32[]{:S(2)}) collective-permute-start(bf16[2,640,256]{2,1,0:T(8,128)(2,1)S(1)} %collective-permute-done.5.refs_4_.refs_7_), channel_id=1, source_target_pairs={{0,16},{16,0},{1,17},{17,1},{2,18},{18,2},{3,19},{19,3},{4,20},{20... | collective-permute-start | bytes 1966088 | tf_op jit(solution)/shard_map/ppermute | solution.py:194
  71.9 7.0 %copy-start.5 = (bf16[2,640,256]{2,1,0:T(8,128)(2,1)}, bf16[2,640,256]{2,1,0:T(8,128)(2,1)S(1)}, u32[]{:S(2)}) copy-start(bf16[2,640,256]{2,1,0:T(8,128)(2,1)S(1)} %collective-permute-done.2.refs_1_.refs_5_) | copy-start | bytes 1966084
  71.9 14.6 %collective-permute-start.6 = (bf16[2,640,256]{2,1,0:T(8,128)(2,1)S(1)}, bf16[2,640,256]{2,1,0:T(8,128)(2,1)S(1)}, u32[]{:S(2)}, u32[]{:S(2)}) collective-permute-start(bf16[2,640,256]{2,1,0:T(8,128)(2,1)S(1)} %collective-permute-done.2.refs_1_.refs_5_), channel_id=1, source_target_pairs={{0,32},{16,240},{32,64},{48,16},{64,96},{80,48},{96,128},{112,80},... | collective-permute-start | bytes 1966088 | tf_op jit(solution)/shard_map/ppermute | solution.py:208
  76.8 9.7 %collective-permute-start.4 = (bf16[2,640,256]{2,1,0:T(8,128)(2,1)S(1)}, bf16[2,640,256]{2,1,0:T(8,128)(2,1)S(1)}, u32[]{:S(2)}, u32[]{:S(2)}) collective-permute-start(bf16[2,640,256]{2,1,0:T(8,128)(2,1)S(1)} %collective-permute-done.2.refs_1_.refs_5_), channel_id=1, source_target_pairs={{0,16},{16,0},{1,17},{17,1},{2,18},{18,2},{3,19},{19,3},{4,20},{20... | collective-permute-start | bytes 1966088 | tf_op jit(solution)/shard_map/ppermute | solution.py:194
  78.9 27.9 %copy-start.10 = (bf16[2,640,256]{2,1,0:T(8,128)(2,1)}, bf16[2,640,256]{2,1,0:T(8,128)(2,1)S(1)}, u32[]{:S(2)}) copy-start(bf16[2,640,256]{2,1,0:T(8,128)(2,1)S(1)} %collective-permute-done.9.refs_11_) | copy-start | bytes 1966084
  79.0 7.6 %copy-start.6 = (bf16[2,640,256]{2,1,0:T(8,128)(2,1)}, bf16[2,640,256]{2,1,0:T(8,128)(2,1)S(1)}, u32[]{:S(2)}) copy-start(bf16[2,640,256]{2,1,0:T(8,128)(2,1)S(1)} %collective-permute-done.7.refs_6_.refs_10_) | copy-start | bytes 1966084
  79.0 14.0 %collective-permute-start.12 = (bf16[2,640,256]{2,1,0:T(8,128)(2,1)S(1)}, bf16[2,640,256]{2,1,0:T(8,128)(2,1)S(1)}, u32[]{:S(2)}, u32[]{:S(2)}) collective-permute-start(bf16[2,640,256]{2,1,0:T(8,128)(2,1)S(1)} %collective-permute-done.9.refs_11_), channel_id=1, source_target_pairs={{0,16},{16,0},{1,17},{17,1},{2,18},{18,2},{3,19},{19,3},{4,20},{20... | collective-permute-start | bytes 1966088 | tf_op jit(solution)/shard_map/ppermute | solution.py:194
  84.1 11.7 %collective-permute-start.11 = (bf16[2,640,256]{2,1,0:T(8,128)(2,1)S(1)}, bf16[2,640,256]{2,1,0:T(8,128)(2,1)}, u32[]{:S(2)}, u32[]{:S(2)}) collective-permute-start(bf16[2,640,256]{2,1,0:T(8,128)(2,1)S(1)} %collective-permute-done.9.refs_11_), channel_id=1, source_target_pairs={{0,32},{16,240},{32,64},{48,16},{64,96},{80,48},{96,128},{112,80},... | collective-permute-start | bytes 1966088 | tf_op jit(solution)/shard_map/ppermute | solution.py:208
  86.5 3.2 %copy-start.7 = (bf16[2,640,256]{2,1,0:T(8,128)(2,1)}, bf16[2,640,256]{2,1,0:T(8,128)(2,1)S(1)}, u32[]{:S(2)}) copy-start(bf16[2,640,256]{2,1,0:T(8,128)(2,1)S(1)} %collective-permute-done.6.refs_5_.refs_9_) | copy-start | bytes 1966084
  86.5 16.3 %copy-start.8 = (bf16[2,640,256]{2,1,0:T(8,128)(2,1)}, bf16[2,640,256]{2,1,0:T(8,128)(2,1)S(1)}, u32[]{:S(2)}) copy-start(bf16[2,640,256]{2,1,0:T(8,128)(2,1)S(1)} %collective-permute-done.4.refs_3_.refs_8_) | copy-start | bytes 1966084
  86.5 16.3 %collective-permute-start.10 = (bf16[2,640,256]{2,1,0:T(8,128)(2,1)S(1)}, bf16[2,640,256]{2,1,0:T(8,128)(2,1)}, u32[]{:S(2)}, u32[]{:S(2)}) collective-permute-start(bf16[2,640,256]{2,1,0:T(8,128)(2,1)S(1)} %collective-permute-done.6.refs_5_.refs_9_), channel_id=1, source_target_pairs={{0,32},{16,240},{32,64},{48,16},{64,96},{80,48},{96,128},{112,80},... | collective-permute-start | bytes 1966088 | tf_op jit(solution)/shard_map/ppermute | solution.py:208
  89.7 13.1 %collective-permute-start.8 = (bf16[2,640,256]{2,1,0:T(8,128)(2,1)S(1)}, bf16[2,640,256]{2,1,0:T(8,128)(2,1)S(1)}, u32[]{:S(2)}, u32[]{:S(2)}) collective-permute-start(bf16[2,640,256]{2,1,0:T(8,128)(2,1)S(1)} %collective-permute-done.6.refs_5_.refs_9_), channel_id=1, source_target_pairs={{0,16},{16,0},{1,17},{17,1},{2,18},{18,2},{3,19},{19,3},{4,20},{20... | collective-permute-start | bytes 1966088 | tf_op jit(solution)/shard_map/ppermute | solution.py:194
  93.0 13.8 %copy-start.11 = (bf16[2,640,256]{2,1,0:T(8,128)(2,1)}, bf16[2,640,256]{2,1,0:T(8,128)(2,1)S(1)}, u32[]{:S(2)}) copy-start(bf16[2,640,256]{2,1,0:T(8,128)(2,1)S(1)} %collective-permute-done.12.refs_14_) | copy-start | bytes 1966084
  95.8 21.1 %collective-permute-start.14 = (bf16[2,640,256]{2,1,0:T(8,128)(2,1)}, bf16[2,640,256]{2,1,0:T(8,128)(2,1)}, u32[]{:S(2)}, u32[]{:S(2)}) collective-permute-start(bf16[2,640,256]{2,1,0:T(8,128)(2,1)} %collective-permute-done.11.refs_15_), channel_id=1, source_target_pairs={{0,16},{16,0},{1,17},{17,1},{2,18},{18,2},{3,19},{19,3},{4,20},{20... | collective-permute-start | bytes 1966088 | tf_op jit(solution)/shard_map/ppermute | solution.py:194
  102.8 4.0 %copy-start.9 = (bf16[2,640,256]{2,1,0:T(8,128)(2,1)}, bf16[2,640,256]{2,1,0:T(8,128)(2,1)S(1)}, u32[]{:S(2)}) copy-start(bf16[2,640,256]{2,1,0:T(8,128)(2,1)S(1)} %collective-permute-done.8.refs_7_.refs_12_) | copy-start | bytes 1966084
  102.8 14.0 %collective-permute-start.13 = (bf16[2,640,256]{2,1,0:T(8,128)(2,1)}, bf16[2,640,256]{2,1,0:T(8,128)(2,1)}, u32[]{:S(2)}, u32[]{:S(2)}) collective-permute-start(bf16[2,640,256]{2,1,0:T(8,128)(2,1)} %collective-permute-done.10.refs_13_), channel_id=1, source_target_pairs={{0,16},{16,0},{1,17},{17,1},{2,18},{18,2},{3,19},{19,3},{4,20},{20... | collective-permute-start | bytes 1966088 | tf_op jit(solution)/shard_map/ppermute | solution.py:194

commit v2 on v1

--- a/solution.py
+++ b/solution.py
@@ -11,8 +11,8 @@
 CAP = 40
 BF16 = jnp.bfloat16
 F32 = jnp.float32
-EARLY_VMEM = 60 << 20
-GRADS_VMEM = 60 << 20
+EARLY_VMEM = 8 << 20
+GRADS_VMEM = 16 << 20
 FORWARD_GROUP = 4
 GRADS_GROUP = 4
 
@@ -76,19 +76,24 @@
     )
 
 
-def add_forward(index_ref, ring_size, weights_buf, total, pieces, blocks):
-    halves, half = pieces[0].shape[0], pieces[0].shape[2] // 2
-    hidden_units = weights_buf.shape[2]
+def weight_copies(index_ref, ring_size, weights_ref, weights_buf, blocks):
+    halves, half = weights_buf.shape[1], weights_buf.shape[4]
+    sources, places = [], []
+    for k, block in enumerate(blocks):
+        for j in range(halves):
+            cols = pl.ds(column(index_ref, ring_size, half, block, j), half)
+            sources.append(weights_ref.at[0, :, :, cols])
+            places.append(weights_buf.at[k, j])
+    return sources, places
+
+
+def add_forward(weights_buf, total, pieces, numbers):
+    halves, hidden_units = weights_buf.shape[1], weights_buf.shape[3]
     along = (((1,), (1,)), ((), ()))
 
     def weight_block(m):
         return jnp.concatenate(
-            [
-                weights_buf[0, m, :, pl.ds(column(index_ref, ring_size, half, block, j), half)]
-                for block in blocks
-                for j in range(halves)
-            ],
-            axis=1,
+            [weights_buf[k, j, m] for k in numbers for j in range(halves)], axis=1
         )
 
     pair = jnp.concatenate([weight_block(0), weight_block(1)], axis=0)
@@ -100,54 +105,47 @@
     )
 
 
-def forward_kernel(ring_size, blocks, index_ref, weights_ref, *refs):
+def forward_kernel(ring_size, blocks, chained, index_ref, weights_ref, *refs):
     count = len(blocks)
-    sources, total = refs[:count], refs[count]
-    pieces_buf, weights_buf, sems = refs[count + 1 :]
+    partials, sources, total = refs[:chained], refs[chained : chained + count], refs[chained + count]
+    pieces_buf, weights_buf, sems = refs[chained + count + 1 :]
+    slices, homes = weight_copies(index_ref, ring_size, weights_ref, weights_buf, blocks)
     copies = fetch(
-        (weights_ref,) + sources, [weights_buf] + [pieces_buf.at[k] for k in range(count)], sems
-    )
-    total[...] = jnp.zeros_like(total)
-    copies[0].wait()
+        list(partials) + slices + list(sources),
+        [total] * chained + homes + [pieces_buf.at[k] for k in range(count)],
+        sems,
+    )
+    if not chained:
+        total[...] = jnp.zeros_like(total)
+    base = chained + len(slices)
+    for copy in copies[:base]:
+        copy.wait()
     for k in range(0, count, FORWARD_GROUP):
         chosen = range(k, min(k + FORWARD_GROUP, count))
         for n in chosen:
-            copies[1 + n].wait()
-        add_forward(
-            index_ref, ring_size, weights_buf, total,
-            [pieces_buf.at[n] for n in chosen], [blocks[n] for n in chosen],
-        )
-
-
-def grads_kernel(ring_size, blocks, early, sums, index_ref, weights_ref, *refs):
+            copies[base + n].wait()
+        add_forward(weights_buf, total, [pieces_buf.at[n] for n in chosen], chosen)
+
+
+def grads_kernel(ring_size, blocks, late, index_ref, weights_ref, partial_ref, *refs):
     count = len(blocks)
-    partials, sources, out_ref = refs[:sums], refs[sums : sums + count], refs[sums + count]
-    pieces_buf, weights_buf, partial_buf, total, sems = refs[sums + count + 1 :]
+    sources, out_ref = refs[:count], refs[count]
+    pieces_buf, weights_buf, total, sems = refs[count + 1 :]
     half = pieces_buf.shape[3] // 2
     halves = pieces_buf.shape[1]
-    late = [k for k in range(count) if blocks[k] not in early]
-    order = late + [k for k in range(count) if blocks[k] in early]
-    base = 1 + sums
+    hidden_units = weights_buf.shape[3]
+    last = [blocks.index(block) for block in late]
+    order = last + [k for k in range(count) if k not in last]
+    slices, homes = weight_copies(index_ref, ring_size, weights_ref, weights_buf, late)
     copies = fetch(
-        [weights_ref] + list(partials) + [sources[k] for k in order],
-        [weights_buf] + [partial_buf.at[m] for m in range(sums)] + [pieces_buf.at[k] for k in order],
+        [partial_ref] + slices + [sources[k] for k in order],
+        [total] + homes + [pieces_buf.at[k] for k in order],
         sems,
     )
-    for copy in copies[:base]:
+    base = 1 + len(slices)
+    for copy in copies[: base + len(last)]:
         copy.wait()
-    running = partial_buf[0]
-    for m in range(1, sums):
-        running = running + partial_buf[m]
-    total[...] = running
-    hidden_units = weights_buf.shape[2]
-    for n in range(0, len(late), FORWARD_GROUP):
-        chosen = late[n : n + FORWARD_GROUP]
-        for m in range(len(chosen)):
-            copies[base + n + m].wait()
-        add_forward(
-            index_ref, ring_size, weights_buf, total,
-            [pieces_buf.at[k] for k in chosen], [blocks[k] for k in chosen],
-        )
+    add_forward(weights_buf, total, [pieces_buf.at[k] for k in last], range(len(last)))
     gate_part = total[:, :hidden_units]
     up_part = total[:, hidden_units : 2 * hidden_units]
     back_hidden = total[:, 2 * hidden_units :]
@@ -162,7 +160,7 @@
     for n in range(0, count, GRADS_GROUP):
         chosen = order[n : n + GRADS_GROUP]
         for m in range(len(chosen)):
-            if n + m >= len(late):
+            if n + m >= len(last):
                 copies[base + n + m].wait()
         pieces = [pieces_buf.at[k] for k in chosen]
         ins = jnp.dot(both, joined(pieces, 0), preferred_element_type=F32).astype(BF16)
@@ -224,48 +222,55 @@
     piece_bytes = 8 * slots * width
     weight_bytes = 6 * hidden_units * features
     block_flops = 12 * slots * width * hidden_units
-    groups_early = [
-        [(0, 0, 0), (0, 1, 0)],
-        [(s, c, t) for s in range(1, far - 1) for t in range(2) for c in range(2)],
-    ]
-    groups_early = [g for g in groups_early if g]
+    early = {
+        "early_0": [(0, 0, 0), (0, 1, 0)],
+        "early_1": [(1, c, t) for t in range(2) for c in range(2)],
+        "early_2": [(s, c, t) for s in range(2, far - 1) for t in range(2) for c in range(2)],
+        "early_3": [(far - 1, 0, 0), (far - 1, 0, 1), (far - 1, 1, 0)],
+        "early_4": [(far - 1, 1, 1), (far, 0, 0)],
+    }
+    late = [(far, 0, 1)]
+    sums = jax.ShapeDtypeStruct((slots, 3 * hidden_units), F32)
+
+    def weight_scratch(count):
+        return pltpu.VMEM((count, 2, 3, hidden_units, width), BF16)
+
     partials = []
-    for chosen in groups_early:
-        partials.append(
+    for chosen in early.values():
+        chained = len(partials)
+        partials = [
             pl.pallas_call(
-                functools.partial(forward_kernel, ring_size, chosen),
-                out_shape=jax.ShapeDtypeStruct((slots, 3 * hidden_units), F32),
-                in_specs=[smem_spec, any_spec] + [any_spec] * len(chosen),
+                functools.partial(forward_kernel, ring_size, chosen, chained),
+                out_shape=sums,
+                in_specs=[smem_spec, any_spec] + [any_spec] * (chained + len(chosen)),
                 out_specs=pl.BlockSpec(memory_space=pltpu.VMEM),
                 scratch_shapes=[
                     pltpu.VMEM((len(chosen), 2, slots, 2 * width), BF16),
-                    pltpu.VMEM(expert_weights.shape, BF16),
-                    pltpu.SemaphoreType.DMA((1 + len(chosen),)),
+                    weight_scratch(len(chosen)),
+                    pltpu.SemaphoreType.DMA((chained + 3 * len(chosen),)),
                 ],
                 cost_estimate=pl.CostEstimate(
                     flops=len(chosen) * block_flops,
-                    bytes_accessed=len(chosen) * piece_bytes + weight_bytes,
+                    bytes_accessed=len(chosen) * piece_bytes,
                     transcendentals=0,
                 ),
                 compiler_params=pltpu.CompilerParams(vmem_limit_bytes=EARLY_VMEM),
-            )(index, expert_weights, *[raw.get(k, held[k]) for k in chosen])
-        )
-    early = [k for g in groups_early for k in g]
+            )(index, expert_weights, *partials, *[raw.get(k, held[k]) for k in chosen])
+        ]
     return pl.pallas_call(
-        functools.partial(grads_kernel, ring_size, blocks, early, len(partials)),
+        functools.partial(grads_kernel, ring_size, blocks, late),
         out_shape=jax.ShapeDtypeStruct(expert_weights.shape, BF16),
-        in_specs=[smem_spec, any_spec] + [any_spec] * (len(partials) + len(blocks)),
+        in_specs=[smem_spec, any_spec, any_spec] + [any_spec] * len(blocks),
         out_specs=pl.BlockSpec(memory_space=pltpu.VMEM),
         scratch_shapes=[
             pltpu.VMEM((len(blocks), 2, slots, 2 * width), BF16),
-            pltpu.VMEM(expert_weights.shape, BF16),
-            pltpu.VMEM((len(partials), slots, 3 * hidden_units), F32),
-            pltpu.VMEM((slots, 3 * hidden_units), F32),
-            pltpu.SemaphoreType.DMA((1 + len(partials) + len(blocks),)),
+            weight_scratch(len(late)),
+            pltpu.VMEM(sums.shape, F32),
+            pltpu.SemaphoreType.DMA((1 + 2 * len(late) + len(blocks),)),
         ],
         cost_estimate=pl.CostEstimate(
-            flops=2 * len(blocks) * block_flops,
-            bytes_accessed=len(blocks) * piece_bytes + 2 * weight_bytes,
+            flops=len(blocks) * block_flops,
+            bytes_accessed=len(blocks) * piece_bytes + weight_bytes,
             transcendentals=slots * hidden_units,
         ),
         compiler_params=pltpu.CompilerParams(vmem_limit_bytes=GRADS_VMEM),

time: 126 us -> 125 us (level)
  local copies, waits for them, and re-layouts: 0.05 us -> 9.59 us
  starting transfers between devices: 62.3 us -> 55 us
  waiting for transfers between devices: 11.6 us -> 6.32 us
  Pallas kernels: 19.8 us -> 22.1 us
    unnamed x24 -> x44, local copies, waits for them, and re-layouts: 0.05 us -> 9.59 us
    ppermute x7, waiting for transfers between devices: 11.6 us -> 6.3 us  [device_step(): piece = lax.ppermute(held[step - 1, chain, 0], ('ring', 'core'), around)]
    ppermute x8, starting transfers between devices: 26.3 us -> 21.5 us  [swapped(): return lax.ppermute(x, 'core', [(0, 1), (1, 0)])]
    ppermute x7, starting transfers between devices: 36 us -> 33.6 us  [device_step(): piece = lax.ppermute(held[step - 1, chain, 0], ('ring', 'core'), around)]
    pallas_call x3 -> x6, Pallas kernels: 17.7 us -> 19.8 us  [the longest x5 12 us: device_step(): pl.pallas_call(functools.partial(forward_kernel, ring_size, chosen, chain...]
  transfers between devices with their start and end apart: 15 -> 15, of which waited for: 4 -> 2; matrix products, arithmetic and copies ran while one was open for 1% -> 0% of each run, Pallas kernels for 7% -> 10%
where the time goes in v2:
time: 125 us; the launch traced here: 124 us
  starting transfers between devices  55 us (44%)
  blocking collectives  30.5 us (24%)
  Pallas kernels  22.1 us (18%)
  local copies, waits for them, and re-layouts  9.59 us (8%)
  waiting for transfers between devices  6.32 us (5%)
    ppermute x7, starting transfers between devices, device_step(): piece = lax.ppermute(held[step - 1, chain, 0], ('ring', 'core'), around)  33.6 us
    all_to_all x1, blocking collectives, device_step(): lax.all_to_all(send.reshape(2 * groups, CAP, 2 * width), ('half', 'expert...  30.5 us
    ppermute x8, starting transfers between devices, swapped(): return lax.ppermute(x, 'core', [(0, 1), (1, 0)])  21.5 us
    pallas_call x5, Pallas kernels, device_step(): pl.pallas_call(functools.partial(forward_kernel, ring_size, chosen, chain...  12 us
    unnamed x44, local copies, waits for them, and re-layouts  9.59 us
    pallas_call x1, Pallas kernels, device_step(): pl.pallas_call(functools.partial(grads_kernel, ring_size, blocks, late),...  7.85 us
    ppermute x7, waiting for transfers between devices, device_step(): piece = lax.ppermute(held[step - 1, chain, 0], ('ring', 'core'), around)  6.3 us
  transfers between devices with their start and end apart: 15, of which 2 were waited for; matrix products, arithmetic and copies ran while one was open for 0% of the time, Pallas kernels for 10%

profile of v2, /device:TPU:1, one launch (start us, length us, event | category | flops | bytes accessed | tf_op | source)
XLA Modules:
  0.0 124.0 jit_solution(12711345119995020213)
XLA Ops:
  0.0 2.2 %shard_map.55 = bf16[2,640,256]{2,1,0:T(8,128)(2,1)} custom-call(s32[2,128]{1,0:T(2,128)} %bitcast.11, f32[2,128]{1,0:T(2,128)} %bitcast.12, bf16[128,128]{1,0:T(8,128)(2,1)} %tokens_ref.1, bf16[128,128]{1,0:T(8,128)(2,1)} %cotangent_ref.1), custom_call_target="tpu_custom_call" | custom-call | tf_op jit(solution)/shard_map/pallas_call | solution.py:182
  2.2 30.5 %all_to_all.5 = bf16[32,40,256]{2,1,0:T(8,128)(2,1)S(1)} all-to-all(bf16[32,40,256]{2,1,0:T(8,128)(2,1)} %bitcast.10), channel_id=1, replica_groups=mesh['half'=2,'ring'=8,'core'=2,'expert'=16] {'half','expert'}, dimensions={0} | all-to-all | bytes 1310720 | tf_op jit(solution)/shard_map/all_to_all | solution.py:194
  32.8 4.2 %collective-permute-start = (bf16[2,640,256]{2,1,0:T(8,128)(2,1)S(1)}, bf16[2,640,256]{2,1,0:T(8,128)(2,1)S(1)}, u32[]{:S(2)}, u32[]{:S(2)}) collective-permute-start(bf16[2,640,256]{2,1,0:T(8,128)(2,1)S(1)} %bitcast.6), channel_id=1, source_target_pairs={{0,16},{16,0},{1,17},{17,1},{2,18},{18,2},{3,19},{19,3},{4,20},{20... | collective-permute-start | bytes 1966088 | tf_op jit(solution)/shard_map/ppermute | solution.py:192
  36.9 10.7 %collective-permute-start.1 = (bf16[2,640,256]{2,1,0:T(8,128)(2,1)S(1)}, bf16[2,640,256]{2,1,0:T(8,128)(2,1)S(1)}, u32[]{:S(2)}, u32[]{:S(2)}) collective-permute-start(bf16[2,640,256]{2,1,0:T(8,128)(2,1)S(1)} %bitcast.7), channel_id=1, source_target_pairs={{0,32},{16,240},{32,64},{48,16},{64,96},{80,48},{96,128},{112,80},... | collective-permute-start | bytes 1966088 | tf_op jit(solution)/shard_map/ppermute | solution.py:206
  47.6 0.0 collective-permute-done.refs_1_
  47.6 2.2 %collective-permute-start.2 = (bf16[2,640,256]{2,1,0:T(8,128)(2,1)S(1)}, bf16[2,640,256]{2,1,0:T(8,128)(2,1)S(1)}, u32[]{:S(2)}, u32[]{:S(2)}) collective-permute-start(bf16[2,640,256]{2,1,0:T(8,128)(2,1)S(1)} %collective-permute-done.refs_1_), channel_id=1, source_target_pairs={{0,32},{16,240},{32,64},{48,16},{64,96},{80,48},{96,128},{112,80},... | collective-permute-start | bytes 1966088 | tf_op jit(solution)/shard_map/ppermute | solution.py:206
  49.8 0.0 copy-start.3
  49.8 0.8 copy-done.3
  50.6 4.5 %collective-permute-done.1.refs_1_.refs_2_ = bf16[2,640,256]{2,1,0:T(8,128)(2,1)S(1)} collective-permute-done((bf16[2,640,256]{2,1,0:T(8,128)(2,1)S(1)}, bf16[2,640,256]{2,1,0:T(8,128)(2,1)S(1)}, u32[]{:S(2)}, u32[]{:S(2)}) %collective-permute-start.1) | collective-permute-done | bytes 655392 | tf_op jit(solution)/shard_map/ppermute | solution.py:206
  55.1 5.0 %collective-permute-start.5 = (bf16[2,640,256]{2,1,0:T(8,128)(2,1)S(1)}, bf16[2,640,256]{2,1,0:T(8,128)(2,1)S(1)}, u32[]{:S(2)}, u32[]{:S(2)}) collective-permute-start(bf16[2,640,256]{2,1,0:T(8,128)(2,1)S(1)} %collective-permute-done.1.refs_1_.refs_2_), channel_id=1, source_target_pairs={{0,32},{16,240},{32,64},{48,16},{64,96},{80,48},{96,128},{112,80},... | collective-permute-start | bytes 1966088 | tf_op jit(solution)/shard_map/ppermute | solution.py:206
  60.1 1.9 %collective-permute-start.3 = (bf16[2,640,256]{2,1,0:T(8,128)(2,1)S(1)}, bf16[2,640,256]{2,1,0:T(8,128)(2,1)S(1)}, u32[]{:S(2)}, u32[]{:S(2)}) collective-permute-start(bf16[2,640,256]{2,1,0:T(8,128)(2,1)S(1)} %collective-permute-done.1.refs_1_.refs_2_), channel_id=1, source_target_pairs={{0,16},{16,0},{1,17},{17,1},{2,18},{18,2},{3,19},{19,3},{4,20},{20... | collective-permute-start | bytes 1966088 | tf_op jit(solution)/shard_map/ppermute | solution.py:192
  62.1 0.8 copy-done.6
  62.9 0.0 collective-permute-done.2.refs_2_.refs_3_
  62.9 4.2 %collective-permute-start.6 = (bf16[2,640,256]{2,1,0:T(8,128)(2,1)S(1)}, bf16[2,640,256]{2,1,0:T(8,128)(2,1)S(1)}, u32[]{:S(2)}, u32[]{:S(2)}) collective-permute-start(bf16[2,640,256]{2,1,0:T(8,128)(2,1)S(1)} %collective-permute-done.2.refs_2_.refs_3_), channel_id=1, source_target_pairs={{0,32},{16,240},{32,64},{48,16},{64,96},{80,48},{96,128},{112,80},... | collective-permute-start | bytes 1966088 | tf_op jit(solution)/shard_map/ppermute | solution.py:206
  67.1 1.9 %collective-permute-start.4 = (bf16[2,640,256]{2,1,0:T(8,128)(2,1)S(1)}, bf16[2,640,256]{2,1,0:T(8,128)(2,1)S(1)}, u32[]{:S(2)}, u32[]{:S(2)}) collective-permute-start(bf16[2,640,256]{2,1,0:T(8,128)(2,1)S(1)} %collective-permute-done.2.refs_2_.refs_3_), channel_id=1, source_target_pairs={{0,16},{16,0},{1,17},{17,1},{2,18},{18,2},{3,19},{19,3},{4,20},{20... | collective-permute-start | bytes 1966088 | tf_op jit(solution)/shard_map/ppermute | solution.py:192
  69.1 0.8 copy-done.8
  69.9 0.0 collective-permute-done.5.refs_1_.refs_5_
  69.9 0.0 collective-permute-done.3.refs_3_.refs_4_
  69.9 0.8 copy-done.12
  70.8 4.2 %collective-permute-start.9 = (bf16[2,640,256]{2,1,0:T(8,128)(2,1)S(1)}, bf16[2,640,256]{2,1,0:T(8,128)(2,1)S(1)}, u32[]{:S(2)}, u32[]{:S(2)}) collective-permute-start(bf16[2,640,256]{2,1,0:T(8,128)(2,1)S(1)} %collective-permute-done.5.refs_1_.refs_5_), channel_id=1, source_target_pairs={{0,32},{16,240},{32,64},{48,16},{64,96},{80,48},{96,128},{112,80},... | collective-permute-start | bytes 1966088 | tf_op jit(solution)/shard_map/ppermute | solution.py:206
  75.0 1.9 %collective-permute-start.7 = (bf16[2,640,256]{2,1,0:T(8,128)(2,1)S(1)}, bf16[2,640,256]{2,1,0:T(8,128)(2,1)S(1)}, u32[]{:S(2)}, u32[]{:S(2)}) collective-permute-start(bf16[2,640,256]{2,1,0:T(8,128)(2,1)S(1)} %collective-permute-done.5.refs_1_.refs_5_), channel_id=1, source_target_pairs={{0,16},{16,0},{1,17},{17,1},{2,18},{18,2},{3,19},{19,3},{4,20},{20... | collective-permute-start | bytes 1966088 | tf_op jit(solution)/shard_map/ppermute | solution.py:192
  76.9 0.9 copy-done.10
  77.8 0.0 collective-permute-done.6.refs_2_.refs_7_
  77.8 0.0 collective-permute-done.4.refs_4_.refs_6_
  77.8 0.8 copy-done.16
  78.7 3.4 %collective-permute-start.11 = (bf16[2,640,256]{2,1,0:T(8,128)(2,1)S(1)}, bf16[2,640,256]{2,1,0:T(8,128)(2,1)S(1)}, u32[]{:S(2)}, u32[]{:S(2)}) collective-permute-start(bf16[2,640,256]{2,1,0:T(8,128)(2,1)S(1)} %collective-permute-done.6.refs_2_.refs_7_), channel_id=1, source_target_pairs={{0,32},{16,240},{32,64},{48,16},{64,96},{80,48},{96,128},{112,80},... | collective-permute-start | bytes 1966088 | tf_op jit(solution)/shard_map/ppermute | solution.py:206
  82.0 1.9 %collective-permute-start.8 = (bf16[2,640,256]{2,1,0:T(8,128)(2,1)S(1)}, bf16[2,640,256]{2,1,0:T(8,128)(2,1)S(1)}, u32[]{:S(2)}, u32[]{:S(2)}) collective-permute-start(bf16[2,640,256]{2,1,0:T(8,128)(2,1)S(1)} %collective-permute-done.6.refs_2_.refs_7_), channel_id=1, source_target_pairs={{0,16},{16,0},{1,17},{17,1},{2,18},{18,2},{3,19},{19,3},{4,20},{20... | collective-permute-start | bytes 1966088 | tf_op jit(solution)/shard_map/ppermute | solution.py:192
  84.0 0.8 copy-done.14
  84.8 0.8 copy-done.18
  85.7 3.9 %collective-permute-start.13 = (bf16[2,640,256]{2,1,0:T(8,128)(2,1)S(1)}, bf16[2,640,256]{2,1,0:T(8,128)(2,1)}, u32[]{:S(2)}, u32[]{:S(2)}) collective-permute-start(bf16[2,640,256]{2,1,0:T(8,128)(2,1)S(1)} %collective-permute-done.9.refs_1_.refs_9_), channel_id=1, source_target_pairs={{0,32},{16,240},{32,64},{48,16},{64,96},{80,48},{96,128},{112,80},... | collective-permute-start | bytes 1966088 | tf_op jit(solution)/shard_map/ppermute | solution.py:206
  89.5 1.9 %collective-permute-start.10 = (bf16[2,640,256]{2,1,0:T(8,128)(2,1)S(1)}, bf16[2,640,256]{2,1,0:T(8,128)(2,1)S(1)}, u32[]{:S(2)}, u32[]{:S(2)}) collective-permute-start(bf16[2,640,256]{2,1,0:T(8,128)(2,1)S(1)} %collective-permute-done.9.refs_1_.refs_9_), channel_id=1, source_target_pairs={{0,16},{16,0},{1,17},{17,1},{2,18},{18,2},{3,19},{19,3},{4,20},{20... | collective-permute-start | bytes 1966088 | tf_op jit(solution)/shard_map/ppermute | solution.py:192
  91.5 0.0 collective-permute-done.11.refs_3_.refs_11_
  91.5 0.8 copy-done.20
  92.3 3.2 %collective-permute-start.12 = (bf16[2,640,256]{2,1,0:T(8,128)(2,1)S(1)}, bf16[2,640,256]{2,1,0:T(8,128)(2,1)}, u32[]{:S(2)}, u32[]{:S(2)}) collective-permute-start(bf16[2,640,256]{2,1,0:T(8,128)(2,1)S(1)} %collective-permute-done.11.refs_3_.refs_11_), channel_id=1, source_target_pairs={{0,16},{16,0},{1,17},{17,1},{2,18},{18,2},{3,19},{19,3},{4,20},{20... | collective-permute-start | bytes 1966088 | tf_op jit(solution)/shard_map/ppermute | solution.py:192
  95.6 1.8 %collective-permute-done.13.refs_2_.refs_13_ = bf16[2,640,256]{2,1,0:T(8,128)(2,1)} collective-permute-done((bf16[2,640,256]{2,1,0:T(8,128)(2,1)S(1)}, bf16[2,640,256]{2,1,0:T(8,128)(2,1)}, u32[]{:S(2)}, u32[]{:S(2)}) %collective-permute-start.13) | collective-permute-done | bytes 655392 | tf_op jit(solution)/shard_map/ppermute | solution.py:206
  97.4 0.0 collective-permute-done.10.refs_2_.refs_12_
  97.4 0.9 copy-done.1
  98.3 4.5 %collective-permute-start.14 = (bf16[2,640,256]{2,1,0:T(8,128)(2,1)}, bf16[2,640,256]{2,1,0:T(8,128)(2,1)}, u32[]{:S(2)}, u32[]{:S(2)}) collective-permute-start(bf16[2,640,256]{2,1,0:T(8,128)(2,1)} %collective-permute-done.13.refs_2_.refs_13_), channel_id=1, source_target_pairs={{0,16},{16,0},{1,17},{17,1},{2,18},{18,2},{3,19},{19,3},{4,20},{20... | collective-permute-start | bytes 1966088 | tf_op jit(solution)/shard_map/ppermute | solution.py:192
  102.8 0.1 pad_add_fusion.index_ref
  102.8 1.1 copy-done.4
  103.9 1.6 %shard_map.56.refs_0_ = f32[640,192]{1,0:T(8,128)S(1)} custom-call(s32[2]{0:T(128)S(1)} %pad_add_fusion.index_ref, bf16[1,3,64,4096]{3,2,1,0:T(8,128)(2,1)S(1)} %copy-done, bf16[2,640,256]{2,1,0:T(8,128)(2,1)S(1)} %bitcast.8, bf16[2,640,256]{2,1,0:T(8,128)(2,1)S(1)} %copy-done.4), custom_call_target="tpu_custom_call" | custom-call | flops 125829120 | bytes 1310720 | tf_op jit(solution)/shard_map/pallas_call | solution.py:242
  105.7 2.7 %shard_map.57.refs_0_ = f32[640,192]{1,0:T(8,128)S(1)} custom-call(s32[2]{0:T(128)S(1)} %pad_add_fusion.index_ref, bf16[1,3,64,4096]{3,2,1,0:T(8,128)(2,1)S(1)} %copy-done, f32[640,192]{1,0:T(8,128)S(1)} %shard_map.56.refs_0_, bf16[2,640,256]{2,1,0:T(8,128)(2,1)S(1)} %copy-done.7, bf16[2,640,256]{2,1,0:T(8,128)(2,1)S(1)} %copy-done.9, ...), custom_call_target="tpu_custom_call" | custom-call | flops 251658240 | bytes 2621440 | tf_op jit(solution)/shard_map/pallas_call | solution.py:242
  108.4 2.7 %shard_map.58.refs_0_ = f32[640,192]{1,0:T(8,128)S(1)} custom-call(s32[2]{0:T(128)S(1)} %pad_add_fusion.index_ref, bf16[1,3,64,4096]{3,2,1,0:T(8,128)(2,1)S(1)} %copy-done, f32[640,192]{1,0:T(8,128)S(1)} %shard_map.57.refs_0_, bf16[2,640,256]{2,1,0:T(8,128)(2,1)S(1)} %copy-done.11, bf16[2,640,256]{2,1,0:T(8,128)(2,1)S(1)} %copy-done.15, ...), custom_call_target="tpu_custom_call" | custom-call | flops 251658240 | bytes 2621440 | tf_op jit(solution)/shard_map/pallas_call | solution.py:242
  111.2 2.2 %shard_map.59.refs_0_ = f32[640,192]{1,0:T(8,128)S(1)} custom-call(s32[2]{0:T(128)S(1)} %pad_add_fusion.index_ref, bf16[1,3,64,4096]{3,2,1,0:T(8,128)(2,1)S(1)} %copy-done, f32[640,192]{1,0:T(8,128)S(1)} %shard_map.58.refs_0_, bf16[2,640,256]{2,1,0:T(8,128)(2,1)S(1)} %collective-permute-done.9.refs_1_.refs_9_, bf16[2,640,256]{2,1,0:T(8,128)(2,1)S(1)} %copy-done.2, ...), custom_call_target="tpu_custom_call" | custom-call | flops 188743680 | bytes 1966080 | tf_op jit(solution)/shard_map/pallas_call | solution.py:242
  113.4 0.0 copy-start.5
  113.4 0.0 collective-permute-done.12.refs_1_.refs_14_
  113.4 2.7 %shard_map.60.partial_ref = f32[640,192]{1,0:T(8,128)S(1)} custom-call(s32[2]{0:T(128)S(1)} %pad_add_fusion.index_ref, bf16[1,3,64,4096]{3,2,1,0:T(8,128)(2,1)S(1)} %copy-done, f32[640,192]{1,0:T(8,128)S(1)} %shard_map.59.refs_0_, bf16[2,640,256]{2,1,0:T(8,128)(2,1)} %collective-permute-done.12.refs_1_.refs_14_, ...), custom_call_target="tpu_custom_call" | custom-call | flops 125829120 | bytes 1310720 | tf_op jit(solution)/shard_map/pallas_call | solution.py:242
  116.1 7.9 %shard_map.61 = bf16[1,3,64,4096]{3,2,1,0:T(8,128)(2,1)} custom-call(s32[2]{0:T(128)S(1)} %pad_add_fusion.index_ref, bf16[1,3,64,4096]{3,2,1,0:T(8,128)(2,1)S(1)} %copy-done, f32[640,192]{1,0:T(8,128)S(1)} %shard_map.60.partial_ref, bf16[2,640,256]{2,1,0:T(8,128)(2,1)S(1)} %bitcast.9, bf16[2,640,256]{2,1,0:T(8,128)(2,1)S(1)} %copy-done.5, ...), custom_call_target="tpu_custom_call" | custom-call | flops 1006632960 | bytes 12058624 | tf_op jit(solution)/shard_map/pallas_call | solution.py:260
  (35 shorter events, 0.1 us)
Async XLA Ops:
  0.0 102.8 %copy-start = (bf16[1,3,64,4096]{3,2,1,0:T(8,128)(2,1)S(1)}, bf16[1,3,64,4096]{3,2,1,0:T(8,128)(2,1)}, u32[]{:S(2)}) copy-start(bf16[1,3,64,4096]{3,2,1,0:T(8,128)(2,1)} %weights_ref.11) | copy-start | bytes 4718596
  32.8 14.8 %collective-permute-start = (bf16[2,640,256]{2,1,0:T(8,128)(2,1)S(1)}, bf16[2,640,256]{2,1,0:T(8,128)(2,1)S(1)}, u32[]{:S(2)}, u32[]{:S(2)}) collective-permute-start(bf16[2,640,256]{2,1,0:T(8,128)(2,1)S(1)} %bitcast.6), channel_id=1, source_target_pairs={{0,16},{16,0},{1,17},{17,1},{2,18},{18,2},{3,19},{19,3},{4,20},{20... | collective-permute-start | bytes 1966088 | tf_op jit(solution)/shard_map/ppermute | solution.py:192
  36.9 18.2 %collective-permute-start.1 = (bf16[2,640,256]{2,1,0:T(8,128)(2,1)S(1)}, bf16[2,640,256]{2,1,0:T(8,128)(2,1)S(1)}, u32[]{:S(2)}, u32[]{:S(2)}) collective-permute-start(bf16[2,640,256]{2,1,0:T(8,128)(2,1)S(1)} %bitcast.7), channel_id=1, source_target_pairs={{0,32},{16,240},{32,64},{48,16},{64,96},{80,48},{96,128},{112,80},... | collective-permute-start | bytes 1966088 | tf_op jit(solution)/shard_map/ppermute | solution.py:206
  47.6 15.3 %collective-permute-start.2 = (bf16[2,640,256]{2,1,0:T(8,128)(2,1)S(1)}, bf16[2,640,256]{2,1,0:T(8,128)(2,1)S(1)}, u32[]{:S(2)}, u32[]{:S(2)}) collective-permute-start(bf16[2,640,256]{2,1,0:T(8,128)(2,1)S(1)} %collective-permute-done.refs_1_), channel_id=1, source_target_pairs={{0,32},{16,240},{32,64},{48,16},{64,96},{80,48},{96,128},{112,80},... | collective-permute-start | bytes 1966088 | tf_op jit(solution)/shard_map/ppermute | solution.py:206
  49.8 0.8 copy-start.3
  55.1 14.8 %collective-permute-start.5 = (bf16[2,640,256]{2,1,0:T(8,128)(2,1)S(1)}, bf16[2,640,256]{2,1,0:T(8,128)(2,1)S(1)}, u32[]{:S(2)}, u32[]{:S(2)}) collective-permute-start(bf16[2,640,256]{2,1,0:T(8,128)(2,1)S(1)} %collective-permute-done.1.refs_1_.refs_2_), channel_id=1, source_target_pairs={{0,32},{16,240},{32,64},{48,16},{64,96},{80,48},{96,128},{112,80},... | collective-permute-start | bytes 1966088 | tf_op jit(solution)/shard_map/ppermute | solution.py:206
  60.1 9.8 %collective-permute-start.3 = (bf16[2,640,256]{2,1,0:T(8,128)(2,1)S(1)}, bf16[2,640,256]{2,1,0:T(8,128)(2,1)S(1)}, u32[]{:S(2)}, u32[]{:S(2)}) collective-permute-start(bf16[2,640,256]{2,1,0:T(8,128)(2,1)S(1)} %collective-permute-done.1.refs_1_.refs_2_), channel_id=1, source_target_pairs={{0,16},{16,0},{1,17},{17,1},{2,18},{18,2},{3,19},{19,3},{4,20},{20... | collective-permute-start | bytes 1966088 | tf_op jit(solution)/shard_map/ppermute | solution.py:192
  62.1 0.8 copy-start.6
  62.9 14.9 %collective-permute-start.6 = (bf16[2,640,256]{2,1,0:T(8,128)(2,1)S(1)}, bf16[2,640,256]{2,1,0:T(8,128)(2,1)S(1)}, u32[]{:S(2)}, u32[]{:S(2)}) collective-permute-start(bf16[2,640,256]{2,1,0:T(8,128)(2,1)S(1)} %collective-permute-done.2.refs_2_.refs_3_), channel_id=1, source_target_pairs={{0,32},{16,240},{32,64},{48,16},{64,96},{80,48},{96,128},{112,80},... | collective-permute-start | bytes 1966088 | tf_op jit(solution)/shard_map/ppermute | solution.py:206
  67.1 10.7 %collective-permute-start.4 = (bf16[2,640,256]{2,1,0:T(8,128)(2,1)S(1)}, bf16[2,640,256]{2,1,0:T(8,128)(2,1)S(1)}, u32[]{:S(2)}, u32[]{:S(2)}) collective-permute-start(bf16[2,640,256]{2,1,0:T(8,128)(2,1)S(1)} %collective-permute-done.2.refs_2_.refs_3_), channel_id=1, source_target_pairs={{0,16},{16,0},{1,17},{17,1},{2,18},{18,2},{3,19},{19,3},{4,20},{20... | collective-permute-start | bytes 1966088 | tf_op jit(solution)/shard_map/ppermute | solution.py:192
  69.1 0.9 copy-start.8
  69.9 0.8 copy-start.12
  70.8 14.0 %collective-permute-start.9 = (bf16[2,640,256]{2,1,0:T(8,128)(2,1)S(1)}, bf16[2,640,256]{2,1,0:T(8,128)(2,1)S(1)}, u32[]{:S(2)}, u32[]{:S(2)}) collective-permute-start(bf16[2,640,256]{2,1,0:T(8,128)(2,1)S(1)} %collective-permute-done.5.refs_1_.refs_5_), channel_id=1, source_target_pairs={{0,32},{16,240},{32,64},{48,16},{64,96},{80,48},{96,128},{112,80},... | collective-permute-start | bytes 1966088 | tf_op jit(solution)/shard_map/ppermute | solution.py:206
  75.0 9.8 %collective-permute-start.7 = (bf16[2,640,256]{2,1,0:T(8,128)(2,1)S(1)}, bf16[2,640,256]{2,1,0:T(8,128)(2,1)S(1)}, u32[]{:S(2)}, u32[]{:S(2)}) collective-permute-start(bf16[2,640,256]{2,1,0:T(8,128)(2,1)S(1)} %collective-permute-done.5.refs_1_.refs_5_), channel_id=1, source_target_pairs={{0,16},{16,0},{1,17},{17,1},{2,18},{18,2},{3,19},{19,3},{4,20},{20... | collective-permute-start | bytes 1966088 | tf_op jit(solution)/shard_map/ppermute | solution.py:192
  76.9 0.9 copy-start.10
  77.8 0.8 copy-start.16
  78.7 12.8 %collective-permute-start.11 = (bf16[2,640,256]{2,1,0:T(8,128)(2,1)S(1)}, bf16[2,640,256]{2,1,0:T(8,128)(2,1)S(1)}, u32[]{:S(2)}, u32[]{:S(2)}) collective-permute-start(bf16[2,640,256]{2,1,0:T(8,128)(2,1)S(1)} %collective-permute-done.6.refs_2_.refs_7_), channel_id=1, source_target_pairs={{0,32},{16,240},{32,64},{48,16},{64,96},{80,48},{96,128},{112,80},... | collective-permute-start | bytes 1966088 | tf_op jit(solution)/shard_map/ppermute | solution.py:206
  82.0 9.5 %collective-permute-start.8 = (bf16[2,640,256]{2,1,0:T(8,128)(2,1)S(1)}, bf16[2,640,256]{2,1,0:T(8,128)(2,1)S(1)}, u32[]{:S(2)}, u32[]{:S(2)}) collective-permute-start(bf16[2,640,256]{2,1,0:T(8,128)(2,1)S(1)} %collective-permute-done.6.refs_2_.refs_7_), channel_id=1, source_target_pairs={{0,16},{16,0},{1,17},{17,1},{2,18},{18,2},{3,19},{19,3},{4,20},{20... | collective-permute-start | bytes 1966088 | tf_op jit(solution)/shard_map/ppermute | solution.py:192
  84.0 0.9 copy-start.14
  84.8 0.9 copy-start.18
  85.7 11.7 %collective-permute-start.13 = (bf16[2,640,256]{2,1,0:T(8,128)(2,1)S(1)}, bf16[2,640,256]{2,1,0:T(8,128)(2,1)}, u32[]{:S(2)}, u32[]{:S(2)}) collective-permute-start(bf16[2,640,256]{2,1,0:T(8,128)(2,1)S(1)} %collective-permute-done.9.refs_1_.refs_9_), channel_id=1, source_target_pairs={{0,32},{16,240},{32,64},{48,16},{64,96},{80,48},{96,128},{112,80},... | collective-permute-start | bytes 1966088 | tf_op jit(solution)/shard_map/ppermute | solution.py:206
  89.5 7.9 %collective-permute-start.10 = (bf16[2,640,256]{2,1,0:T(8,128)(2,1)S(1)}, bf16[2,640,256]{2,1,0:T(8,128)(2,1)S(1)}, u32[]{:S(2)}, u32[]{:S(2)}) collective-permute-start(bf16[2,640,256]{2,1,0:T(8,128)(2,1)S(1)} %collective-permute-done.9.refs_1_.refs_9_), channel_id=1, source_target_pairs={{0,16},{16,0},{1,17},{17,1},{2,18},{18,2},{3,19},{19,3},{4,20},{20... | collective-permute-start | bytes 1966088 | tf_op jit(solution)/shard_map/ppermute | solution.py:192
  91.5 0.8 copy-start.20
  92.3 21.1 %collective-permute-start.12 = (bf16[2,640,256]{2,1,0:T(8,128)(2,1)S(1)}, bf16[2,640,256]{2,1,0:T(8,128)(2,1)}, u32[]{:S(2)}, u32[]{:S(2)}) collective-permute-start(bf16[2,640,256]{2,1,0:T(8,128)(2,1)S(1)} %collective-permute-done.11.refs_3_.refs_11_), channel_id=1, source_target_pairs={{0,16},{16,0},{1,17},{17,1},{2,18},{18,2},{3,19},{19,3},{4,20},{20... | collective-permute-start | bytes 1966088 | tf_op jit(solution)/shard_map/ppermute | solution.py:192
  97.4 0.9 copy-start.1
  98.3 17.8 %collective-permute-start.14 = (bf16[2,640,256]{2,1,0:T(8,128)(2,1)}, bf16[2,640,256]{2,1,0:T(8,128)(2,1)}, u32[]{:S(2)}, u32[]{:S(2)}) collective-permute-start(bf16[2,640,256]{2,1,0:T(8,128)(2,1)} %collective-permute-done.13.refs_2_.refs_13_), channel_id=1, source_target_pairs={{0,16},{16,0},{1,17},{17,1},{2,18},{18,2},{3,19},{19,3},{4,20},{20... | collective-permute-start | bytes 1966088 | tf_op jit(solution)/shard_map/ppermute | solution.py:192
  102.8 1.1 copy-start.4
  103.9 1.7 %copy-start.7 = (bf16[2,640,256]{2,1,0:T(8,128)(2,1)S(1)}, bf16[2,640,256]{2,1,0:T(8,128)(2,1)}, u32[]{:S(2)}) copy-start(bf16[2,640,256]{2,1,0:T(8,128)(2,1)} %copy-done.6) | copy-start | bytes 1966084
  103.9 1.7 %copy-start.9 = (bf16[2,640,256]{2,1,0:T(8,128)(2,1)S(1)}, bf16[2,640,256]{2,1,0:T(8,128)(2,1)}, u32[]{:S(2)}) copy-start(bf16[2,640,256]{2,1,0:T(8,128)(2,1)} %copy-done.8) | copy-start | bytes 1966084
  103.9 1.7 %copy-start.13 = (bf16[2,640,256]{2,1,0:T(8,128)(2,1)S(1)}, bf16[2,640,256]{2,1,0:T(8,128)(2,1)}, u32[]{:S(2)}) copy-start(bf16[2,640,256]{2,1,0:T(8,128)(2,1)} %copy-done.12) | copy-start | bytes 1966084
  103.9 1.7 %copy-start.17 = (bf16[2,640,256]{2,1,0:T(8,128)(2,1)S(1)}, bf16[2,640,256]{2,1,0:T(8,128)(2,1)}, u32[]{:S(2)}) copy-start(bf16[2,640,256]{2,1,0:T(8,128)(2,1)} %copy-done.16) | copy-start | bytes 1966084
  105.6 2.8 %copy-start.11 = (bf16[2,640,256]{2,1,0:T(8,128)(2,1)S(1)}, bf16[2,640,256]{2,1,0:T(8,128)(2,1)}, u32[]{:S(2)}) copy-start(bf16[2,640,256]{2,1,0:T(8,128)(2,1)} %copy-done.10) | copy-start | bytes 1966084
  105.6 2.8 %copy-start.15 = (bf16[2,640,256]{2,1,0:T(8,128)(2,1)S(1)}, bf16[2,640,256]{2,1,0:T(8,128)(2,1)}, u32[]{:S(2)}) copy-start(bf16[2,640,256]{2,1,0:T(8,128)(2,1)} %copy-done.14) | copy-start | bytes 1966084
  105.6 2.8 %copy-start.19 = (bf16[2,640,256]{2,1,0:T(8,128)(2,1)S(1)}, bf16[2,640,256]{2,1,0:T(8,128)(2,1)}, u32[]{:S(2)}) copy-start(bf16[2,640,256]{2,1,0:T(8,128)(2,1)} %copy-done.18) | copy-start | bytes 1966084
  105.6 2.8 %copy-start.21 = (bf16[2,640,256]{2,1,0:T(8,128)(2,1)S(1)}, bf16[2,640,256]{2,1,0:T(8,128)(2,1)}, u32[]{:S(2)}) copy-start(bf16[2,640,256]{2,1,0:T(8,128)(2,1)} %copy-done.20) | copy-start | bytes 1966084
  108.4 2.7 %copy-start.2 = (bf16[2,640,256]{2,1,0:T(8,128)(2,1)S(1)}, bf16[2,640,256]{2,1,0:T(8,128)(2,1)}, u32[]{:S(2)}) copy-start(bf16[2,640,256]{2,1,0:T(8,128)(2,1)} %copy-done.1) | copy-start | bytes 1966084
  113.4 2.7 %copy-start.5 = (bf16[2,640,256]{2,1,0:T(8,128)(2,1)S(1)}, bf16[2,640,256]{2,1,0:T(8,128)(2,1)}, u32[]{:S(2)}) copy-start(bf16[2,640,256]{2,1,0:T(8,128)(2,1)} %copy-done.3) | copy-start | bytes 1966084

commit v3 on v2

--- a/solution.py
+++ b/solution.py
@@ -14,7 +14,7 @@
 EARLY_VMEM = 8 << 20
 GRADS_VMEM = 16 << 20
 FORWARD_GROUP = 4
-GRADS_GROUP = 4
+GRADS_GROUP = 2
 
 
 def pack_kernel(routes_ref, gates_ref, tokens_ref, cotangent_ref, out_ref):
@@ -49,15 +49,6 @@
         out_ref[j, :, width // 2 :] = scaled
 
 
-def fetch(sources, buffers, sems):
-    copies = []
-    for n, (source, place) in enumerate(zip(sources, buffers)):
-        copy = pltpu.make_async_copy(source, place, sems.at[n])
-        copy.start()
-        copies.append(copy)
-    return copies
-
-
 def column(index_ref, ring_size, half, block, j):
     step, chain, turned = block
     ring, core = index_ref[0], index_ref[1]
@@ -76,24 +67,19 @@
     )
 
 
-def weight_copies(index_ref, ring_size, weights_ref, weights_buf, blocks):
-    halves, half = weights_buf.shape[1], weights_buf.shape[4]
-    sources, places = [], []
-    for k, block in enumerate(blocks):
-        for j in range(halves):
-            cols = pl.ds(column(index_ref, ring_size, half, block, j), half)
-            sources.append(weights_ref.at[0, :, :, cols])
-            places.append(weights_buf.at[k, j])
-    return sources, places
-
-
-def add_forward(weights_buf, total, pieces, numbers):
-    halves, hidden_units = weights_buf.shape[1], weights_buf.shape[3]
+def add_forward(ring_size, index_ref, weights_ref, total, pieces, blocks):
+    halves, half = pieces[0].shape[0], pieces[0].shape[2] // 2
+    hidden_units = weights_ref.shape[2]
     along = (((1,), (1,)), ((), ()))
 
     def weight_block(m):
         return jnp.concatenate(
-            [weights_buf[k, j, m] for k in numbers for j in range(halves)], axis=1
+            [
+                weights_ref[0, m, :, pl.ds(column(index_ref, ring_size, half, block, j), half)]
+                for block in blocks
+                for j in range(halves)
+            ],
+            axis=1,
         )
 
     pair = jnp.concatenate([weight_block(0), weight_block(1)], axis=0)
@@ -108,44 +94,23 @@
 def forward_kernel(ring_size, blocks, chained, index_ref, weights_ref, *refs):
     count = len(blocks)
     partials, sources, total = refs[:chained], refs[chained : chained + count], refs[chained + count]
-    pieces_buf, weights_buf, sems = refs[chained + count + 1 :]
-    slices, homes = weight_copies(index_ref, ring_size, weights_ref, weights_buf, blocks)
-    copies = fetch(
-        list(partials) + slices + list(sources),
-        [total] * chained + homes + [pieces_buf.at[k] for k in range(count)],
-        sems,
-    )
-    if not chained:
-        total[...] = jnp.zeros_like(total)
-    base = chained + len(slices)
-    for copy in copies[:base]:
-        copy.wait()
+    total[...] = partials[0][...] if chained else jnp.zeros_like(total)
     for k in range(0, count, FORWARD_GROUP):
         chosen = range(k, min(k + FORWARD_GROUP, count))
-        for n in chosen:
-            copies[base + n].wait()
-        add_forward(weights_buf, total, [pieces_buf.at[n] for n in chosen], chosen)
+        add_forward(
+            ring_size, index_ref, weights_ref, total,
+            [sources[n] for n in chosen], [blocks[n] for n in chosen],
+        )
 
 
 def grads_kernel(ring_size, blocks, late, index_ref, weights_ref, partial_ref, *refs):
     count = len(blocks)
-    sources, out_ref = refs[:count], refs[count]
-    pieces_buf, weights_buf, total, sems = refs[count + 1 :]
-    half = pieces_buf.shape[3] // 2
-    halves = pieces_buf.shape[1]
-    hidden_units = weights_buf.shape[3]
+    sources, out_ref, total = refs[:count], refs[count], refs[count + 1]
+    halves, half = sources[0].shape[0], sources[0].shape[2] // 2
+    hidden_units = weights_ref.shape[2]
     last = [blocks.index(block) for block in late]
-    order = last + [k for k in range(count) if k not in last]
-    slices, homes = weight_copies(index_ref, ring_size, weights_ref, weights_buf, late)
-    copies = fetch(
-        [partial_ref] + slices + [sources[k] for k in order],
-        [total] + homes + [pieces_buf.at[k] for k in order],
-        sems,
-    )
-    base = 1 + len(slices)
-    for copy in copies[: base + len(last)]:
-        copy.wait()
-    add_forward(weights_buf, total, [pieces_buf.at[k] for k in last], range(len(last)))
+    total[...] = partial_ref[...]
+    add_forward(ring_size, index_ref, weights_ref, total, [sources[k] for k in last], late)
     gate_part = total[:, :hidden_units]
     up_part = total[:, hidden_units : 2 * hidden_units]
     back_hidden = total[:, 2 * hidden_units :]
@@ -158,11 +123,8 @@
     both = jnp.concatenate([pre_gate, pre_up], axis=1).T
     hidden_t = hidden.T
     for n in range(0, count, GRADS_GROUP):
-        chosen = order[n : n + GRADS_GROUP]
-        for m in range(len(chosen)):
-            if n + m >= len(last):
-                copies[base + n + m].wait()
-        pieces = [pieces_buf.at[k] for k in chosen]
+        chosen = range(n, min(n + GRADS_GROUP, count))
+        pieces = [sources[k] for k in chosen]
         ins = jnp.dot(both, joined(pieces, 0), preferred_element_type=F32).astype(BF16)
         outs = jnp.dot(hidden_t, joined(pieces, 1), preferred_element_type=F32).astype(BF16)
         for m, k in enumerate(chosen):
@@ -217,7 +179,7 @@
     index = jnp.stack([lax.axis_index("ring"), lax.axis_index("core")]).astype(jnp.int32)
     hidden_units = expert_weights.shape[2]
     features = expert_weights.shape[3]
-    any_spec = pl.BlockSpec(memory_space=pl.ANY)
+    vmem_spec = pl.BlockSpec(memory_space=pltpu.VMEM)
     smem_spec = pl.BlockSpec(memory_space=pltpu.SMEM)
     piece_bytes = 8 * slots * width
     weight_bytes = 6 * hidden_units * features
@@ -232,9 +194,6 @@
     late = [(far, 0, 1)]
     sums = jax.ShapeDtypeStruct((slots, 3 * hidden_units), F32)
 
-    def weight_scratch(count):
-        return pltpu.VMEM((count, 2, 3, hidden_units, width), BF16)
-
     partials = []
     for chosen in early.values():
         chained = len(partials)
@@ -242,13 +201,8 @@
             pl.pallas_call(
                 functools.partial(forward_kernel, ring_size, chosen, chained),
                 out_shape=sums,
-                in_specs=[smem_spec, any_spec] + [any_spec] * (chained + len(chosen)),
+                in_specs=[smem_spec, vmem_spec] + [vmem_spec] * (chained + len(chosen)),
                 out_specs=pl.BlockSpec(memory_space=pltpu.VMEM),
-                scratch_shapes=[
-                    pltpu.VMEM((len(chosen), 2, slots, 2 * width), BF16),
-                    weight_scratch(len(chosen)),
-                    pltpu.SemaphoreType.DMA((chained + 3 * len(chosen),)),
-                ],
                 cost_estimate=pl.CostEstimate(
                     flops=len(chosen) * block_flops,
                     bytes_accessed=len(chosen) * piece_bytes,
@@ -260,14 +214,9 @@
     return pl.pallas_call(
         functools.partial(grads_kernel, ring_size, blocks, late),
         out_shape=jax.ShapeDtypeStruct(expert_weights.shape, BF16),
-        in_specs=[smem_spec, any_spec, any_spec] + [any_spec] * len(blocks),
+        in_specs=[smem_spec, vmem_spec, vmem_spec] + [vmem_spec] * len(blocks),
         out_specs=pl.BlockSpec(memory_space=pltpu.VMEM),
-        scratch_shapes=[
-            pltpu.VMEM((len(blocks), 2, slots, 2 * width), BF16),
-            weight_scratch(len(late)),
-            pltpu.VMEM(sums.shape, F32),
-            pltpu.SemaphoreType.DMA((1 + 2 * len(late) + len(blocks),)),
-        ],
+        scratch_shapes=[pltpu.VMEM(sums.shape, F32)],
         cost_estimate=pl.CostEstimate(
             flops=len(blocks) * block_flops,
             bytes_accessed=len(blocks) * piece_bytes + weight_bytes,

time: 125 us -> 118 us (0.944)
  Pallas kernels: 22.1 us -> 14.7 us
    pallas_call x5, Pallas kernels: 12 us -> 7.06 us  [device_step(): pl.pallas_call(functools.partial(forward_kernel, ring_size, chosen, chain...]
    pallas_call x1, Pallas kernels: 7.85 us -> 5.43 us  [device_step(): pl.pallas_call(functools.partial(grads_kernel, ring_size, blocks, late),...]
  transfers between devices with their start and end apart: 15 -> 15, of which waited for: 2 -> 2; matrix products, arithmetic and copies ran while one was open for 0% -> 0% of each run, Pallas kernels for 10% -> 6%
where the time goes in v3:
time: 118 us; the launch traced here: 117 us
  starting transfers between devices  55 us (47%)
  blocking collectives  30.5 us (26%)
  Pallas kernels  14.7 us (12%)
  local copies, waits for them, and re-layouts  10.4 us (9%)
  waiting for transfers between devices  6.32 us (5%)
    ppermute x7, starting transfers between devices, device_step(): piece = lax.ppermute(held[step - 1, chain, 0], ('ring', 'core'), around)  33.6 us
    all_to_all x1, blocking collectives, device_step(): lax.all_to_all(send.reshape(2 * groups, CAP, 2 * width), ('half', 'expert...  30.5 us
    ppermute x8, starting transfers between devices, swapped(): return lax.ppermute(x, 'core', [(0, 1), (1, 0)])  21.5 us
    unnamed x44, local copies, waits for them, and re-layouts  10.4 us
    pallas_call x5, Pallas kernels, device_step(): pl.pallas_call(functools.partial(forward_kernel, ring_size, chosen, chain...  7.06 us
    ppermute x7, waiting for transfers between devices, device_step(): piece = lax.ppermute(held[step - 1, chain, 0], ('ring', 'core'), around)  6.3 us
    pallas_call x1, Pallas kernels, device_step(): pl.pallas_call(functools.partial(grads_kernel, ring_size, blocks, late),...  5.43 us
  transfers between devices with their start and end apart: 15, of which 2 were waited for; matrix products, arithmetic and copies ran while one was open for 0% of the time, Pallas kernels for 6%

profile of v3, /device:TPU:1, one launch (start us, length us, event | category | flops | bytes accessed | tf_op | source)
XLA Modules:
  0.0 117.3 jit_solution(13480243010546927623)
XLA Ops:
  0.0 2.2 %shard_map.55 = bf16[2,640,256]{2,1,0:T(8,128)(2,1)} custom-call(s32[2,128]{1,0:T(2,128)} %bitcast.11, f32[2,128]{1,0:T(2,128)} %bitcast.12, bf16[128,128]{1,0:T(8,128)(2,1)} %tokens_ref.1, bf16[128,128]{1,0:T(8,128)(2,1)} %cotangent_ref.1), custom_call_target="tpu_custom_call" | custom-call | tf_op jit(solution)/shard_map/pallas_call | solution.py:144
  2.2 30.5 %all_to_all.5 = bf16[32,40,256]{2,1,0:T(8,128)(2,1)S(1)} all-to-all(bf16[32,40,256]{2,1,0:T(8,128)(2,1)} %bitcast.10), channel_id=1, replica_groups=mesh['half'=2,'ring'=8,'core'=2,'expert'=16] {'half','expert'}, dimensions={0} | all-to-all | bytes 1310720 | tf_op jit(solution)/shard_map/all_to_all | solution.py:156
  32.8 4.2 %collective-permute-start = (bf16[2,640,256]{2,1,0:T(8,128)(2,1)S(1)}, bf16[2,640,256]{2,1,0:T(8,128)(2,1)S(1)}, u32[]{:S(2)}, u32[]{:S(2)}) collective-permute-start(bf16[2,640,256]{2,1,0:T(8,128)(2,1)S(1)} %bitcast.6), channel_id=1, source_target_pairs={{0,16},{16,0},{1,17},{17,1},{2,18},{18,2},{3,19},{19,3},{4,20},{20... | collective-permute-start | bytes 1966088 | tf_op jit(solution)/shard_map/ppermute | solution.py:154
  36.9 10.7 %collective-permute-start.1 = (bf16[2,640,256]{2,1,0:T(8,128)(2,1)S(1)}, bf16[2,640,256]{2,1,0:T(8,128)(2,1)S(1)}, u32[]{:S(2)}, u32[]{:S(2)}) collective-permute-start(bf16[2,640,256]{2,1,0:T(8,128)(2,1)S(1)} %bitcast.7), channel_id=1, source_target_pairs={{0,32},{16,240},{32,64},{48,16},{64,96},{80,48},{96,128},{112,80},... | collective-permute-start | bytes 1966088 | tf_op jit(solution)/shard_map/ppermute | solution.py:168
  47.6 0.0 collective-permute-done.refs_1_
  47.6 2.2 %collective-permute-start.2 = (bf16[2,640,256]{2,1,0:T(8,128)(2,1)S(1)}, bf16[2,640,256]{2,1,0:T(8,128)(2,1)S(1)}, u32[]{:S(2)}, u32[]{:S(2)}) collective-permute-start(bf16[2,640,256]{2,1,0:T(8,128)(2,1)S(1)} %collective-permute-done.refs_1_), channel_id=1, source_target_pairs={{0,32},{16,240},{32,64},{48,16},{64,96},{80,48},{96,128},{112,80},... | collective-permute-start | bytes 1966088 | tf_op jit(solution)/shard_map/ppermute | solution.py:168
  49.8 0.0 copy-start.3
  49.8 0.8 copy-done.3
  50.6 4.5 %collective-permute-done.1.refs_1_.refs_2_ = bf16[2,640,256]{2,1,0:T(8,128)(2,1)S(1)} collective-permute-done((bf16[2,640,256]{2,1,0:T(8,128)(2,1)S(1)}, bf16[2,640,256]{2,1,0:T(8,128)(2,1)S(1)}, u32[]{:S(2)}, u32[]{:S(2)}) %collective-permute-start.1) | collective-permute-done | bytes 655392 | tf_op jit(solution)/shard_map/ppermute | solution.py:168
  55.1 5.0 %collective-permute-start.5 = (bf16[2,640,256]{2,1,0:T(8,128)(2,1)S(1)}, bf16[2,640,256]{2,1,0:T(8,128)(2,1)S(1)}, u32[]{:S(2)}, u32[]{:S(2)}) collective-permute-start(bf16[2,640,256]{2,1,0:T(8,128)(2,1)S(1)} %collective-permute-done.1.refs_1_.refs_2_), channel_id=1, source_target_pairs={{0,32},{16,240},{32,64},{48,16},{64,96},{80,48},{96,128},{112,80},... | collective-permute-start | bytes 1966088 | tf_op jit(solution)/shard_map/ppermute | solution.py:168
  60.1 1.9 %collective-permute-start.3 = (bf16[2,640,256]{2,1,0:T(8,128)(2,1)S(1)}, bf16[2,640,256]{2,1,0:T(8,128)(2,1)S(1)}, u32[]{:S(2)}, u32[]{:S(2)}) collective-permute-start(bf16[2,640,256]{2,1,0:T(8,128)(2,1)S(1)} %collective-permute-done.1.refs_1_.refs_2_), channel_id=1, source_target_pairs={{0,16},{16,0},{1,17},{17,1},{2,18},{18,2},{3,19},{19,3},{4,20},{20... | collective-permute-start | bytes 1966088 | tf_op jit(solution)/shard_map/ppermute | solution.py:154
  62.1 0.8 copy-done.6
  62.9 0.0 collective-permute-done.2.refs_2_.refs_3_
  62.9 4.2 %collective-permute-start.6 = (bf16[2,640,256]{2,1,0:T(8,128)(2,1)S(1)}, bf16[2,640,256]{2,1,0:T(8,128)(2,1)S(1)}, u32[]{:S(2)}, u32[]{:S(2)}) collective-permute-start(bf16[2,640,256]{2,1,0:T(8,128)(2,1)S(1)} %collective-permute-done.2.refs_2_.refs_3_), channel_id=1, source_target_pairs={{0,32},{16,240},{32,64},{48,16},{64,96},{80,48},{96,128},{112,80},... | collective-permute-start | bytes 1966088 | tf_op jit(solution)/shard_map/ppermute | solution.py:168
  67.1 1.9 %collective-permute-start.4 = (bf16[2,640,256]{2,1,0:T(8,128)(2,1)S(1)}, bf16[2,640,256]{2,1,0:T(8,128)(2,1)S(1)}, u32[]{:S(2)}, u32[]{:S(2)}) collective-permute-start(bf16[2,640,256]{2,1,0:T(8,128)(2,1)S(1)} %collective-permute-done.2.refs_2_.refs_3_), channel_id=1, source_target_pairs={{0,16},{16,0},{1,17},{17,1},{2,18},{18,2},{3,19},{19,3},{4,20},{20... | collective-permute-start | bytes 1966088 | tf_op jit(solution)/shard_map/ppermute | solution.py:154
  69.1 0.8 copy-done.8
  69.9 0.8 copy-done.12
  70.8 4.2 %collective-permute-start.9 = (bf16[2,640,256]{2,1,0:T(8,128)(2,1)S(1)}, bf16[2,640,256]{2,1,0:T(8,128)(2,1)S(1)}, u32[]{:S(2)}, u32[]{:S(2)}) collective-permute-start(bf16[2,640,256]{2,1,0:T(8,128)(2,1)S(1)} %collective-permute-done.5.refs_1_.refs_5_), channel_id=1, source_target_pairs={{0,32},{16,240},{32,64},{48,16},{64,96},{80,48},{96,128},{112,80},... | collective-permute-start | bytes 1966088 | tf_op jit(solution)/shard_map/ppermute | solution.py:168
  75.0 1.9 %collective-permute-start.7 = (bf16[2,640,256]{2,1,0:T(8,128)(2,1)S(1)}, bf16[2,640,256]{2,1,0:T(8,128)(2,1)S(1)}, u32[]{:S(2)}, u32[]{:S(2)}) collective-permute-start(bf16[2,640,256]{2,1,0:T(8,128)(2,1)S(1)} %collective-permute-done.5.refs_1_.refs_5_), channel_id=1, source_target_pairs={{0,16},{16,0},{1,17},{17,1},{2,18},{18,2},{3,19},{19,3},{4,20},{20... | collective-permute-start | bytes 1966088 | tf_op jit(solution)/shard_map/ppermute | solution.py:154
  76.9 0.9 copy-done.10
  77.8 0.0 collective-permute-done.6.refs_2_.refs_7_
  77.8 0.8 copy-done.16
  78.7 3.4 %collective-permute-start.11 = (bf16[2,640,256]{2,1,0:T(8,128)(2,1)S(1)}, bf16[2,640,256]{2,1,0:T(8,128)(2,1)S(1)}, u32[]{:S(2)}, u32[]{:S(2)}) collective-permute-start(bf16[2,640,256]{2,1,0:T(8,128)(2,1)S(1)} %collective-permute-done.6.refs_2_.refs_7_), channel_id=1, source_target_pairs={{0,32},{16,240},{32,64},{48,16},{64,96},{80,48},{96,128},{112,80},... | collective-permute-start | bytes 1966088 | tf_op jit(solution)/shard_map/ppermute | solution.py:168
  82.0 1.9 %collective-permute-start.8 = (bf16[2,640,256]{2,1,0:T(8,128)(2,1)S(1)}, bf16[2,640,256]{2,1,0:T(8,128)(2,1)S(1)}, u32[]{:S(2)}, u32[]{:S(2)}) collective-permute-start(bf16[2,640,256]{2,1,0:T(8,128)(2,1)S(1)} %collective-permute-done.6.refs_2_.refs_7_), channel_id=1, source_target_pairs={{0,16},{16,0},{1,17},{17,1},{2,18},{18,2},{3,19},{19,3},{4,20},{20... | collective-permute-start | bytes 1966088 | tf_op jit(solution)/shard_map/ppermute | solution.py:154
  84.0 0.8 copy-done.14
  84.8 0.8 copy-done.18
  85.7 3.9 %collective-permute-start.13 = (bf16[2,640,256]{2,1,0:T(8,128)(2,1)S(1)}, bf16[2,640,256]{2,1,0:T(8,128)(2,1)}, u32[]{:S(2)}, u32[]{:S(2)}) collective-permute-start(bf16[2,640,256]{2,1,0:T(8,128)(2,1)S(1)} %collective-permute-done.9.refs_1_.refs_9_), channel_id=1, source_target_pairs={{0,32},{16,240},{32,64},{48,16},{64,96},{80,48},{96,128},{112,80},... | collective-permute-start | bytes 1966088 | tf_op jit(solution)/shard_map/ppermute | solution.py:168
  89.5 1.9 %collective-permute-start.10 = (bf16[2,640,256]{2,1,0:T(8,128)(2,1)S(1)}, bf16[2,640,256]{2,1,0:T(8,128)(2,1)S(1)}, u32[]{:S(2)}, u32[]{:S(2)}) collective-permute-start(bf16[2,640,256]{2,1,0:T(8,128)(2,1)S(1)} %collective-permute-done.9.refs_1_.refs_9_), channel_id=1, source_target_pairs={{0,16},{16,0},{1,17},{17,1},{2,18},{18,2},{3,19},{19,3},{4,20},{20... | collective-permute-start | bytes 1966088 | tf_op jit(solution)/shard_map/ppermute | solution.py:154
  91.5 0.0 collective-permute-done.11.refs_3_.refs_11_
  91.5 0.8 copy-done.20
  92.3 3.2 %collective-permute-start.12 = (bf16[2,640,256]{2,1,0:T(8,128)(2,1)S(1)}, bf16[2,640,256]{2,1,0:T(8,128)(2,1)}, u32[]{:S(2)}, u32[]{:S(2)}) collective-permute-start(bf16[2,640,256]{2,1,0:T(8,128)(2,1)S(1)} %collective-permute-done.11.refs_3_.refs_11_), channel_id=1, source_target_pairs={{0,16},{16,0},{1,17},{17,1},{2,18},{18,2},{3,19},{19,3},{4,20},{20... | collective-permute-start | bytes 1966088 | tf_op jit(solution)/shard_map/ppermute | solution.py:154
  95.6 1.8 %collective-permute-done.13.refs_2_.refs_13_ = bf16[2,640,256]{2,1,0:T(8,128)(2,1)} collective-permute-done((bf16[2,640,256]{2,1,0:T(8,128)(2,1)S(1)}, bf16[2,640,256]{2,1,0:T(8,128)(2,1)}, u32[]{:S(2)}, u32[]{:S(2)}) %collective-permute-start.13) | collective-permute-done | bytes 655392 | tf_op jit(solution)/shard_map/ppermute | solution.py:168
  97.4 0.9 copy-done.1
  98.3 4.5 %collective-permute-start.14 = (bf16[2,640,256]{2,1,0:T(8,128)(2,1)}, bf16[2,640,256]{2,1,0:T(8,128)(2,1)}, u32[]{:S(2)}, u32[]{:S(2)}) collective-permute-start(bf16[2,640,256]{2,1,0:T(8,128)(2,1)} %collective-permute-done.13.refs_2_.refs_13_), channel_id=1, source_target_pairs={{0,16},{16,0},{1,17},{17,1},{2,18},{18,2},{3,19},{19,3},{4,20},{20... | collective-permute-start | bytes 1966088 | tf_op jit(solution)/shard_map/ppermute | solution.py:154
  102.8 0.1 pad_add_fusion.index_ref
  102.8 1.1 copy-done.4
  103.9 1.1 shard_map.56.refs_0_
  105.0 0.2 copy-done.9
  105.2 0.2 copy-done.13
  105.4 0.2 copy-done.17
  105.6 1.4 %shard_map.57.refs_0_ = f32[640,192]{1,0:T(8,128)S(1)} custom-call(s32[2]{0:T(128)S(1)} %pad_add_fusion.index_ref, bf16[1,3,64,4096]{3,2,1,0:T(8,128)(2,1)S(1)} %copy-done, f32[640,192]{1,0:T(8,128)S(1)} %shard_map.56.refs_0_, bf16[2,640,256]{2,1,0:T(8,128)(2,1)S(1)} %copy-done.7, bf16[2,640,256]{2,1,0:T(8,128)(2,1)S(1)} %copy-done.9, ...), custom_call_target="tpu_custom_call" | custom-call | flops 251658240 | bytes 2621440 | tf_op jit(solution)/shard_map/pallas_call | solution.py:201
  107.1 0.0 copy-done.19
  107.1 0.2 copy-done.21
  107.3 1.4 %shard_map.58.refs_0_ = f32[640,192]{1,0:T(8,128)S(1)} custom-call(s32[2]{0:T(128)S(1)} %pad_add_fusion.index_ref, bf16[1,3,64,4096]{3,2,1,0:T(8,128)(2,1)S(1)} %copy-done, f32[640,192]{1,0:T(8,128)S(1)} %shard_map.57.refs_0_, bf16[2,640,256]{2,1,0:T(8,128)(2,1)S(1)} %copy-done.11, bf16[2,640,256]{2,1,0:T(8,128)(2,1)S(1)} %copy-done.15, ...), custom_call_target="tpu_custom_call" | custom-call | flops 251658240 | bytes 2621440 | tf_op jit(solution)/shard_map/pallas_call | solution.py:201
  108.7 1.2 %shard_map.59.refs_0_ = f32[640,192]{1,0:T(8,128)S(1)} custom-call(s32[2]{0:T(128)S(1)} %pad_add_fusion.index_ref, bf16[1,3,64,4096]{3,2,1,0:T(8,128)(2,1)S(1)} %copy-done, f32[640,192]{1,0:T(8,128)S(1)} %shard_map.58.refs_0_, bf16[2,640,256]{2,1,0:T(8,128)(2,1)S(1)} %collective-permute-done.9.refs_1_.refs_9_, bf16[2,640,256]{2,1,0:T(8,128)(2,1)S(1)} %copy-done.2, ...), custom_call_target="tpu_custom_call" | custom-call | flops 188743680 | bytes 1966080 | tf_op jit(solution)/shard_map/pallas_call | solution.py:201
  110.0 0.0 copy-start.5
  110.0 1.9 %shard_map.60.partial_ref = f32[640,192]{1,0:T(8,128)S(1)} custom-call(s32[2]{0:T(128)S(1)} %pad_add_fusion.index_ref, bf16[1,3,64,4096]{3,2,1,0:T(8,128)(2,1)S(1)} %copy-done, f32[640,192]{1,0:T(8,128)S(1)} %shard_map.59.refs_0_, bf16[2,640,256]{2,1,0:T(8,128)(2,1)} %collective-permute-done.12.refs_1_.refs_14_, ...), custom_call_target="tpu_custom_call" | custom-call | flops 125829120 | bytes 1310720 | tf_op jit(solution)/shard_map/pallas_call | solution.py:201
  111.9 5.4 %shard_map.61 = bf16[1,3,64,4096]{3,2,1,0:T(8,128)(2,1)} custom-call(s32[2]{0:T(128)S(1)} %pad_add_fusion.index_ref, bf16[1,3,64,4096]{3,2,1,0:T(8,128)(2,1)S(1)} %copy-done, f32[640,192]{1,0:T(8,128)S(1)} %shard_map.60.partial_ref, bf16[2,640,256]{2,1,0:T(8,128)(2,1)S(1)} %bitcast.9, bf16[2,640,256]{2,1,0:T(8,128)(2,1)S(1)} %copy-done.5, ...), custom_call_target="tpu_custom_call" | custom-call | flops 1006632960 | bytes 12058624 | tf_op jit(solution)/shard_map/pallas_call | solution.py:214
  (35 shorter events, 0.1 us)
Async XLA Ops:
  0.0 102.8 %copy-start = (bf16[1,3,64,4096]{3,2,1,0:T(8,128)(2,1)S(1)}, bf16[1,3,64,4096]{3,2,1,0:T(8,128)(2,1)}, u32[]{:S(2)}) copy-start(bf16[1,3,64,4096]{3,2,1,0:T(8,128)(2,1)} %weights_ref.11) | copy-start | bytes 4718596
  32.8 14.8 %collective-permute-start = (bf16[2,640,256]{2,1,0:T(8,128)(2,1)S(1)}, bf16[2,640,256]{2,1,0:T(8,128)(2,1)S(1)}, u32[]{:S(2)}, u32[]{:S(2)}) collective-permute-start(bf16[2,640,256]{2,1,0:T(8,128)(2,1)S(1)} %bitcast.6), channel_id=1, source_target_pairs={{0,16},{16,0},{1,17},{17,1},{2,18},{18,2},{3,19},{19,3},{4,20},{20... | collective-permute-start | bytes 1966088 | tf_op jit(solution)/shard_map/ppermute | solution.py:154
  36.9 18.2 %collective-permute-start.1 = (bf16[2,640,256]{2,1,0:T(8,128)(2,1)S(1)}, bf16[2,640,256]{2,1,0:T(8,128)(2,1)S(1)}, u32[]{:S(2)}, u32[]{:S(2)}) collective-permute-start(bf16[2,640,256]{2,1,0:T(8,128)(2,1)S(1)} %bitcast.7), channel_id=1, source_target_pairs={{0,32},{16,240},{32,64},{48,16},{64,96},{80,48},{96,128},{112,80},... | collective-permute-start | bytes 1966088 | tf_op jit(solution)/shard_map/ppermute | solution.py:168
  47.6 15.3 %collective-permute-start.2 = (bf16[2,640,256]{2,1,0:T(8,128)(2,1)S(1)}, bf16[2,640,256]{2,1,0:T(8,128)(2,1)S(1)}, u32[]{:S(2)}, u32[]{:S(2)}) collective-permute-start(bf16[2,640,256]{2,1,0:T(8,128)(2,1)S(1)} %collective-permute-done.refs_1_), channel_id=1, source_target_pairs={{0,32},{16,240},{32,64},{48,16},{64,96},{80,48},{96,128},{112,80},... | collective-permute-start | bytes 1966088 | tf_op jit(solution)/shard_map/ppermute | solution.py:168
  49.8 0.8 copy-start.3
  55.1 14.8 %collective-permute-start.5 = (bf16[2,640,256]{2,1,0:T(8,128)(2,1)S(1)}, bf16[2,640,256]{2,1,0:T(8,128)(2,1)S(1)}, u32[]{:S(2)}, u32[]{:S(2)}) collective-permute-start(bf16[2,640,256]{2,1,0:T(8,128)(2,1)S(1)} %collective-permute-done.1.refs_1_.refs_2_), channel_id=1, source_target_pairs={{0,32},{16,240},{32,64},{48,16},{64,96},{80,48},{96,128},{112,80},... | collective-permute-start | bytes 1966088 | tf_op jit(solution)/shard_map/ppermute | solution.py:168
  60.1 9.8 %collective-permute-start.3 = (bf16[2,640,256]{2,1,0:T(8,128)(2,1)S(1)}, bf16[2,640,256]{2,1,0:T(8,128)(2,1)S(1)}, u32[]{:S(2)}, u32[]{:S(2)}) collective-permute-start(bf16[2,640,256]{2,1,0:T(8,128)(2,1)S(1)} %collective-permute-done.1.refs_1_.refs_2_), channel_id=1, source_target_pairs={{0,16},{16,0},{1,17},{17,1},{2,18},{18,2},{3,19},{19,3},{4,20},{20... | collective-permute-start | bytes 1966088 | tf_op jit(solution)/shard_map/ppermute | solution.py:154
  62.1 0.8 copy-start.6
  62.9 14.9 %collective-permute-start.6 = (bf16[2,640,256]{2,1,0:T(8,128)(2,1)S(1)}, bf16[2,640,256]{2,1,0:T(8,128)(2,1)S(1)}, u32[]{:S(2)}, u32[]{:S(2)}) collective-permute-start(bf16[2,640,256]{2,1,0:T(8,128)(2,1)S(1)} %collective-permute-done.2.refs_2_.refs_3_), channel_id=1, source_target_pairs={{0,32},{16,240},{32,64},{48,16},{64,96},{80,48},{96,128},{112,80},... | collective-permute-start | bytes 1966088 | tf_op jit(solution)/shard_map/ppermute | solution.py:168
  67.1 10.7 %collective-permute-start.4 = (bf16[2,640,256]{2,1,0:T(8,128)(2,1)S(1)}, bf16[2,640,256]{2,1,0:T(8,128)(2,1)S(1)}, u32[]{:S(2)}, u32[]{:S(2)}) collective-permute-start(bf16[2,640,256]{2,1,0:T(8,128)(2,1)S(1)} %collective-permute-done.2.refs_2_.refs_3_), channel_id=1, source_target_pairs={{0,16},{16,0},{1,17},{17,1},{2,18},{18,2},{3,19},{19,3},{4,20},{20... | collective-permute-start | bytes 1966088 | tf_op jit(solution)/shard_map/ppermute | solution.py:154
  69.1 0.9 copy-start.8
  69.9 0.8 copy-start.12
  70.8 14.0 %collective-permute-start.9 = (bf16[2,640,256]{2,1,0:T(8,128)(2,1)S(1)}, bf16[2,640,256]{2,1,0:T(8,128)(2,1)S(1)}, u32[]{:S(2)}, u32[]{:S(2)}) collective-permute-start(bf16[2,640,256]{2,1,0:T(8,128)(2,1)S(1)} %collective-permute-done.5.refs_1_.refs_5_), channel_id=1, source_target_pairs={{0,32},{16,240},{32,64},{48,16},{64,96},{80,48},{96,128},{112,80},... | collective-permute-start | bytes 1966088 | tf_op jit(solution)/shard_map/ppermute | solution.py:168
  75.0 9.8 %collective-permute-start.7 = (bf16[2,640,256]{2,1,0:T(8,128)(2,1)S(1)}, bf16[2,640,256]{2,1,0:T(8,128)(2,1)S(1)}, u32[]{:S(2)}, u32[]{:S(2)}) collective-permute-start(bf16[2,640,256]{2,1,0:T(8,128)(2,1)S(1)} %collective-permute-done.5.refs_1_.refs_5_), channel_id=1, source_target_pairs={{0,16},{16,0},{1,17},{17,1},{2,18},{18,2},{3,19},{19,3},{4,20},{20... | collective-permute-start | bytes 1966088 | tf_op jit(solution)/shard_map/ppermute | solution.py:154
  76.9 0.9 copy-start.10
  77.8 0.8 copy-start.16
  78.7 12.8 %collective-permute-start.11 = (bf16[2,640,256]{2,1,0:T(8,128)(2,1)S(1)}, bf16[2,640,256]{2,1,0:T(8,128)(2,1)S(1)}, u32[]{:S(2)}, u32[]{:S(2)}) collective-permute-start(bf16[2,640,256]{2,1,0:T(8,128)(2,1)S(1)} %collective-permute-done.6.refs_2_.refs_7_), channel_id=1, source_target_pairs={{0,32},{16,240},{32,64},{48,16},{64,96},{80,48},{96,128},{112,80},... | collective-permute-start | bytes 1966088 | tf_op jit(solution)/shard_map/ppermute | solution.py:168
  82.0 9.5 %collective-permute-start.8 = (bf16[2,640,256]{2,1,0:T(8,128)(2,1)S(1)}, bf16[2,640,256]{2,1,0:T(8,128)(2,1)S(1)}, u32[]{:S(2)}, u32[]{:S(2)}) collective-permute-start(bf16[2,640,256]{2,1,0:T(8,128)(2,1)S(1)} %collective-permute-done.6.refs_2_.refs_7_), channel_id=1, source_target_pairs={{0,16},{16,0},{1,17},{17,1},{2,18},{18,2},{3,19},{19,3},{4,20},{20... | collective-permute-start | bytes 1966088 | tf_op jit(solution)/shard_map/ppermute | solution.py:154
  84.0 0.9 copy-start.14
  84.8 0.9 copy-start.18
  85.7 11.7 %collective-permute-start.13 = (bf16[2,640,256]{2,1,0:T(8,128)(2,1)S(1)}, bf16[2,640,256]{2,1,0:T(8,128)(2,1)}, u32[]{:S(2)}, u32[]{:S(2)}) collective-permute-start(bf16[2,640,256]{2,1,0:T(8,128)(2,1)S(1)} %collective-permute-done.9.refs_1_.refs_9_), channel_id=1, source_target_pairs={{0,32},{16,240},{32,64},{48,16},{64,96},{80,48},{96,128},{112,80},... | collective-permute-start | bytes 1966088 | tf_op jit(solution)/shard_map/ppermute | solution.py:168
  89.5 7.9 %collective-permute-start.10 = (bf16[2,640,256]{2,1,0:T(8,128)(2,1)S(1)}, bf16[2,640,256]{2,1,0:T(8,128)(2,1)S(1)}, u32[]{:S(2)}, u32[]{:S(2)}) collective-permute-start(bf16[2,640,256]{2,1,0:T(8,128)(2,1)S(1)} %collective-permute-done.9.refs_1_.refs_9_), channel_id=1, source_target_pairs={{0,16},{16,0},{1,17},{17,1},{2,18},{18,2},{3,19},{19,3},{4,20},{20... | collective-permute-start | bytes 1966088 | tf_op jit(solution)/shard_map/ppermute | solution.py:154
  91.5 0.8 copy-start.20
  92.3 17.6 %collective-permute-start.12 = (bf16[2,640,256]{2,1,0:T(8,128)(2,1)S(1)}, bf16[2,640,256]{2,1,0:T(8,128)(2,1)}, u32[]{:S(2)}, u32[]{:S(2)}) collective-permute-start(bf16[2,640,256]{2,1,0:T(8,128)(2,1)S(1)} %collective-permute-done.11.refs_3_.refs_11_), channel_id=1, source_target_pairs={{0,16},{16,0},{1,17},{17,1},{2,18},{18,2},{3,19},{19,3},{4,20},{20... | collective-permute-start | bytes 1966088 | tf_op jit(solution)/shard_map/ppermute | solution.py:154
  97.4 0.9 copy-start.1
  98.3 13.6 %collective-permute-start.14 = (bf16[2,640,256]{2,1,0:T(8,128)(2,1)}, bf16[2,640,256]{2,1,0:T(8,128)(2,1)}, u32[]{:S(2)}, u32[]{:S(2)}) collective-permute-start(bf16[2,640,256]{2,1,0:T(8,128)(2,1)} %collective-permute-done.13.refs_2_.refs_13_), channel_id=1, source_target_pairs={{0,16},{16,0},{1,17},{17,1},{2,18},{18,2},{3,19},{19,3},{4,20},{20... | collective-permute-start | bytes 1966088 | tf_op jit(solution)/shard_map/ppermute | solution.py:154
  102.8 1.1 copy-start.4
  103.9 1.1 copy-start.7
  103.9 1.3 %copy-start.9 = (bf16[2,640,256]{2,1,0:T(8,128)(2,1)S(1)}, bf16[2,640,256]{2,1,0:T(8,128)(2,1)}, u32[]{:S(2)}) copy-start(bf16[2,640,256]{2,1,0:T(8,128)(2,1)} %copy-done.8) | copy-start | bytes 1966084
  103.9 1.5 %copy-start.13 = (bf16[2,640,256]{2,1,0:T(8,128)(2,1)S(1)}, bf16[2,640,256]{2,1,0:T(8,128)(2,1)}, u32[]{:S(2)}) copy-start(bf16[2,640,256]{2,1,0:T(8,128)(2,1)} %copy-done.12) | copy-start | bytes 1966084
  103.9 1.7 %copy-start.17 = (bf16[2,640,256]{2,1,0:T(8,128)(2,1)S(1)}, bf16[2,640,256]{2,1,0:T(8,128)(2,1)}, u32[]{:S(2)}) copy-start(bf16[2,640,256]{2,1,0:T(8,128)(2,1)} %copy-done.16) | copy-start | bytes 1966084
  105.6 1.4 %copy-start.11 = (bf16[2,640,256]{2,1,0:T(8,128)(2,1)S(1)}, bf16[2,640,256]{2,1,0:T(8,128)(2,1)}, u32[]{:S(2)}) copy-start(bf16[2,640,256]{2,1,0:T(8,128)(2,1)} %copy-done.10) | copy-start | bytes 1966084
  105.6 1.4 %copy-start.15 = (bf16[2,640,256]{2,1,0:T(8,128)(2,1)S(1)}, bf16[2,640,256]{2,1,0:T(8,128)(2,1)}, u32[]{:S(2)}) copy-start(bf16[2,640,256]{2,1,0:T(8,128)(2,1)} %copy-done.14) | copy-start | bytes 1966084
  105.6 1.5 %copy-start.19 = (bf16[2,640,256]{2,1,0:T(8,128)(2,1)S(1)}, bf16[2,640,256]{2,1,0:T(8,128)(2,1)}, u32[]{:S(2)}) copy-start(bf16[2,640,256]{2,1,0:T(8,128)(2,1)} %copy-done.18) | copy-start | bytes 1966084
  105.6 1.7 %copy-start.21 = (bf16[2,640,256]{2,1,0:T(8,128)(2,1)S(1)}, bf16[2,640,256]{2,1,0:T(8,128)(2,1)}, u32[]{:S(2)}) copy-start(bf16[2,640,256]{2,1,0:T(8,128)(2,1)} %copy-done.20) | copy-start | bytes 1966084
  107.3 1.4 %copy-start.2 = (bf16[2,640,256]{2,1,0:T(8,128)(2,1)S(1)}, bf16[2,640,256]{2,1,0:T(8,128)(2,1)}, u32[]{:S(2)}) copy-start(bf16[2,640,256]{2,1,0:T(8,128)(2,1)} %copy-done.1) | copy-start | bytes 1966084
  110.0 1.9 %copy-start.5 = (bf16[2,640,256]{2,1,0:T(8,128)(2,1)S(1)}, bf16[2,640,256]{2,1,0:T(8,128)(2,1)}, u32[]{:S(2)}) copy-start(bf16[2,640,256]{2,1,0:T(8,128)(2,1)} %copy-done.3) | copy-start | bytes 1966084

commit v4 on v3

--- a/solution.py
+++ b/solution.py
@@ -105,7 +105,8 @@
 
 def grads_kernel(ring_size, blocks, late, index_ref, weights_ref, partial_ref, *refs):
     count = len(blocks)
-    sources, out_ref, total = refs[:count], refs[count], refs[count + 1]
+    sources, out_ref = refs[:count], refs[count]
+    total, out_buf, sems = refs[count + 1 :]
     halves, half = sources[0].shape[0], sources[0].shape[2] // 2
     hidden_units = weights_ref.shape[2]
     last = [blocks.index(block) for block in late]
@@ -122,6 +123,7 @@
     pre_up = (back_hidden * silu).astype(BF16)
     both = jnp.concatenate([pre_gate, pre_up], axis=1).T
     hidden_t = hidden.T
+    copies = []
     for n in range(0, count, GRADS_GROUP):
         chosen = range(n, min(n + GRADS_GROUP, count))
         pieces = [sources[k] for k in chosen]
@@ -129,11 +131,18 @@
         outs = jnp.dot(hidden_t, joined(pieces, 1), preferred_element_type=F32).astype(BF16)
         for m, k in enumerate(chosen):
             for j in range(halves):
+                cut = slice((m * halves + j) * half, (m * halves + j + 1) * half)
+                out_buf[k, j, 0] = ins[:hidden_units, cut]
+                out_buf[k, j, 1] = ins[hidden_units:, cut]
+                out_buf[k, j, 2] = outs[:, cut]
                 cols = pl.ds(column(index_ref, ring_size, half, blocks[k], j), half)
-                cut = slice((m * halves + j) * half, (m * halves + j + 1) * half)
-                out_ref[0, 0, :, cols] = ins[:hidden_units, cut]
-                out_ref[0, 1, :, cols] = ins[hidden_units:, cut]
-                out_ref[0, 2, :, cols] = outs[:, cut]
+                copy = pltpu.make_async_copy(
+                    out_buf.at[k, j], out_ref.at[0, :, :, cols], sems.at[k, j]
+                )
+                copy.start()
+                copies.append(copy)
+    for copy in copies:
+        copy.wait()
 
 
 def device_step(tokens, cotangent, routes, gates, expert_weights):
@@ -142,7 +151,8 @@
     slots = groups * CAP
     width = tokens.shape[1]
     send = pl.pallas_call(
-        pack_kernel, out_shape=jax.ShapeDtypeStruct((2, slots, 2 * width), BF16)
+        pack_kernel,
+        out_shape=jax.ShapeDtypeStruct((2, slots, 2 * width), BF16),
     )(routes.T, gates.T, tokens, cotangent)
     around = [
         (z * 2 + c, ((z + 1 - 2 * c) % ring_size) * 2 + c)
@@ -215,8 +225,12 @@
         functools.partial(grads_kernel, ring_size, blocks, late),
         out_shape=jax.ShapeDtypeStruct(expert_weights.shape, BF16),
         in_specs=[smem_spec, vmem_spec, vmem_spec] + [vmem_spec] * len(blocks),
-        out_specs=pl.BlockSpec(memory_space=pltpu.VMEM),
-        scratch_shapes=[pltpu.VMEM(sums.shape, F32)],
+        out_specs=pl.BlockSpec(memory_space=pl.ANY),
+        scratch_shapes=[
+            pltpu.VMEM(sums.shape, F32),
+            pltpu.VMEM((len(blocks), 2, 3, hidden_units, width), BF16),
+            pltpu.SemaphoreType.DMA((len(blocks), 2)),
+        ],
         cost_estimate=pl.CostEstimate(
             flops=len(blocks) * block_flops,
             bytes_accessed=len(blocks) * piece_bytes + weight_bytes,

time: 118 us -> 118 us (level)
  no operation moved by 1% of the time
where the time goes in v4:
time: 118 us; the launch traced here: 117 us
  starting transfers between devices  55 us (47%)
  blocking collectives  30.5 us (26%)
  Pallas kernels  14.2 us (12%)
  local copies, waits for them, and re-layouts  10.4 us (9%)
  waiting for transfers between devices  6.32 us (5%)
    ppermute x7, starting transfers between devices, device_step(): piece = lax.ppermute(held[step - 1, chain, 0], ('ring', 'core'), around)  33.6 us
    all_to_all x1, blocking collectives, device_step(): lax.all_to_all(send.reshape(2 * groups, CAP, 2 * width), ('half', 'expert...  30.5 us
    ppermute x8, starting transfers between devices, swapped(): return lax.ppermute(x, 'core', [(0, 1), (1, 0)])  21.5 us
    unnamed x44, local copies, waits for them, and re-layouts  10.4 us
    pallas_call x5, Pallas kernels, device_step(): pl.pallas_call(functools.partial(forward_kernel, ring_size, chosen, chain...  7.06 us
    ppermute x7, waiting for transfers between devices, device_step(): piece = lax.ppermute(held[step - 1, chain, 0], ('ring', 'core'), around)  6.3 us
    pallas_call x1, Pallas kernels, device_step(): pl.pallas_call(functools.partial(grads_kernel, ring_size, blocks, late),...  4.91 us
  transfers between devices with their start and end apart: 15, of which 2 were waited for; matrix products, arithmetic and copies ran while one was open for 0% of the time, Pallas kernels for 6%

profile of v4, /device:TPU:1, one launch (start us, length us, event | category | flops | bytes accessed | tf_op | source)
XLA Modules:
  0.0 116.8 jit_solution(10605759850914701272)
XLA Ops:
  0.0 2.2 %shard_map.55 = bf16[2,640,256]{2,1,0:T(8,128)(2,1)} custom-call(s32[2,128]{1,0:T(2,128)} %bitcast.11, f32[2,128]{1,0:T(2,128)} %bitcast.12, bf16[128,128]{1,0:T(8,128)(2,1)} %tokens_ref.1, bf16[128,128]{1,0:T(8,128)(2,1)} %cotangent_ref.1), custom_call_target="tpu_custom_call" | custom-call | tf_op jit(solution)/shard_map/pallas_call | solution.py:153
  2.2 30.5 %all_to_all.5 = bf16[32,40,256]{2,1,0:T(8,128)(2,1)S(1)} all-to-all(bf16[32,40,256]{2,1,0:T(8,128)(2,1)} %bitcast.10), channel_id=1, replica_groups=mesh['half'=2,'ring'=8,'core'=2,'expert'=16] {'half','expert'}, dimensions={0} | all-to-all | bytes 1310720 | tf_op jit(solution)/shard_map/all_to_all | solution.py:166
  32.8 4.2 %collective-permute-start = (bf16[2,640,256]{2,1,0:T(8,128)(2,1)S(1)}, bf16[2,640,256]{2,1,0:T(8,128)(2,1)S(1)}, u32[]{:S(2)}, u32[]{:S(2)}) collective-permute-start(bf16[2,640,256]{2,1,0:T(8,128)(2,1)S(1)} %bitcast.6), channel_id=1, source_target_pairs={{0,16},{16,0},{1,17},{17,1},{2,18},{18,2},{3,19},{19,3},{4,20},{20... | collective-permute-start | bytes 1966088 | tf_op jit(solution)/shard_map/ppermute | solution.py:164
  36.9 10.7 %collective-permute-start.1 = (bf16[2,640,256]{2,1,0:T(8,128)(2,1)S(1)}, bf16[2,640,256]{2,1,0:T(8,128)(2,1)S(1)}, u32[]{:S(2)}, u32[]{:S(2)}) collective-permute-start(bf16[2,640,256]{2,1,0:T(8,128)(2,1)S(1)} %bitcast.7), channel_id=1, source_target_pairs={{0,32},{16,240},{32,64},{48,16},{64,96},{80,48},{96,128},{112,80},... | collective-permute-start | bytes 1966088 | tf_op jit(solution)/shard_map/ppermute | solution.py:178
  47.6 0.0 collective-permute-done.refs_1_
  47.6 2.2 %collective-permute-start.2 = (bf16[2,640,256]{2,1,0:T(8,128)(2,1)S(1)}, bf16[2,640,256]{2,1,0:T(8,128)(2,1)S(1)}, u32[]{:S(2)}, u32[]{:S(2)}) collective-permute-start(bf16[2,640,256]{2,1,0:T(8,128)(2,1)S(1)} %collective-permute-done.refs_1_), channel_id=1, source_target_pairs={{0,32},{16,240},{32,64},{48,16},{64,96},{80,48},{96,128},{112,80},... | collective-permute-start | bytes 1966088 | tf_op jit(solution)/shard_map/ppermute | solution.py:178
  49.8 0.0 copy-start.3
  49.8 0.8 copy-done.3
  50.6 4.5 %collective-permute-done.1.refs_1_.refs_2_ = bf16[2,640,256]{2,1,0:T(8,128)(2,1)S(1)} collective-permute-done((bf16[2,640,256]{2,1,0:T(8,128)(2,1)S(1)}, bf16[2,640,256]{2,1,0:T(8,128)(2,1)S(1)}, u32[]{:S(2)}, u32[]{:S(2)}) %collective-permute-start.1) | collective-permute-done | bytes 655392 | tf_op jit(solution)/shard_map/ppermute | solution.py:178
  55.1 5.0 %collective-permute-start.5 = (bf16[2,640,256]{2,1,0:T(8,128)(2,1)S(1)}, bf16[2,640,256]{2,1,0:T(8,128)(2,1)S(1)}, u32[]{:S(2)}, u32[]{:S(2)}) collective-permute-start(bf16[2,640,256]{2,1,0:T(8,128)(2,1)S(1)} %collective-permute-done.1.refs_1_.refs_2_), channel_id=1, source_target_pairs={{0,32},{16,240},{32,64},{48,16},{64,96},{80,48},{96,128},{112,80},... | collective-permute-start | bytes 1966088 | tf_op jit(solution)/shard_map/ppermute | solution.py:178
  60.1 1.9 %collective-permute-start.3 = (bf16[2,640,256]{2,1,0:T(8,128)(2,1)S(1)}, bf16[2,640,256]{2,1,0:T(8,128)(2,1)S(1)}, u32[]{:S(2)}, u32[]{:S(2)}) collective-permute-start(bf16[2,640,256]{2,1,0:T(8,128)(2,1)S(1)} %collective-permute-done.1.refs_1_.refs_2_), channel_id=1, source_target_pairs={{0,16},{16,0},{1,17},{17,1},{2,18},{18,2},{3,19},{19,3},{4,20},{20... | collective-permute-start | bytes 1966088 | tf_op jit(solution)/shard_map/ppermute | solution.py:164
  62.1 0.8 copy-done.6
  62.9 0.0 collective-permute-done.2.refs_2_.refs_3_
  62.9 4.2 %collective-permute-start.6 = (bf16[2,640,256]{2,1,0:T(8,128)(2,1)S(1)}, bf16[2,640,256]{2,1,0:T(8,128)(2,1)S(1)}, u32[]{:S(2)}, u32[]{:S(2)}) collective-permute-start(bf16[2,640,256]{2,1,0:T(8,128)(2,1)S(1)} %collective-permute-done.2.refs_2_.refs_3_), channel_id=1, source_target_pairs={{0,32},{16,240},{32,64},{48,16},{64,96},{80,48},{96,128},{112,80},... | collective-permute-start | bytes 1966088 | tf_op jit(solution)/shard_map/ppermute | solution.py:178
  67.1 1.9 %collective-permute-start.4 = (bf16[2,640,256]{2,1,0:T(8,128)(2,1)S(1)}, bf16[2,640,256]{2,1,0:T(8,128)(2,1)S(1)}, u32[]{:S(2)}, u32[]{:S(2)}) collective-permute-start(bf16[2,640,256]{2,1,0:T(8,128)(2,1)S(1)} %collective-permute-done.2.refs_2_.refs_3_), channel_id=1, source_target_pairs={{0,16},{16,0},{1,17},{17,1},{2,18},{18,2},{3,19},{19,3},{4,20},{20... | collective-permute-start | bytes 1966088 | tf_op jit(solution)/shard_map/ppermute | solution.py:164
  69.1 0.8 copy-done.8
  69.9 0.8 copy-done.12
  70.8 4.2 %collective-permute-start.9 = (bf16[2,640,256]{2,1,0:T(8,128)(2,1)S(1)}, bf16[2,640,256]{2,1,0:T(8,128)(2,1)S(1)}, u32[]{:S(2)}, u32[]{:S(2)}) collective-permute-start(bf16[2,640,256]{2,1,0:T(8,128)(2,1)S(1)} %collective-permute-done.5.refs_1_.refs_5_), channel_id=1, source_target_pairs={{0,32},{16,240},{32,64},{48,16},{64,96},{80,48},{96,128},{112,80},... | collective-permute-start | bytes 1966088 | tf_op jit(solution)/shard_map/ppermute | solution.py:178
  75.0 1.9 %collective-permute-start.7 = (bf16[2,640,256]{2,1,0:T(8,128)(2,1)S(1)}, bf16[2,640,256]{2,1,0:T(8,128)(2,1)S(1)}, u32[]{:S(2)}, u32[]{:S(2)}) collective-permute-start(bf16[2,640,256]{2,1,0:T(8,128)(2,1)S(1)} %collective-permute-done.5.refs_1_.refs_5_), channel_id=1, source_target_pairs={{0,16},{16,0},{1,17},{17,1},{2,18},{18,2},{3,19},{19,3},{4,20},{20... | collective-permute-start | bytes 1966088 | tf_op jit(solution)/shard_map/ppermute | solution.py:164
  76.9 0.9 copy-done.10
  77.8 0.0 collective-permute-done.6.refs_2_.refs_7_
  77.8 0.8 copy-done.16
  78.7 3.4 %collective-permute-start.11 = (bf16[2,640,256]{2,1,0:T(8,128)(2,1)S(1)}, bf16[2,640,256]{2,1,0:T(8,128)(2,1)S(1)}, u32[]{:S(2)}, u32[]{:S(2)}) collective-permute-start(bf16[2,640,256]{2,1,0:T(8,128)(2,1)S(1)} %collective-permute-done.6.refs_2_.refs_7_), channel_id=1, source_target_pairs={{0,32},{16,240},{32,64},{48,16},{64,96},{80,48},{96,128},{112,80},... | collective-permute-start | bytes 1966088 | tf_op jit(solution)/shard_map/ppermute | solution.py:178
  82.0 1.9 %collective-permute-start.8 = (bf16[2,640,256]{2,1,0:T(8,128)(2,1)S(1)}, bf16[2,640,256]{2,1,0:T(8,128)(2,1)S(1)}, u32[]{:S(2)}, u32[]{:S(2)}) collective-permute-start(bf16[2,640,256]{2,1,0:T(8,128)(2,1)S(1)} %collective-permute-done.6.refs_2_.refs_7_), channel_id=1, source_target_pairs={{0,16},{16,0},{1,17},{17,1},{2,18},{18,2},{3,19},{19,3},{4,20},{20... | collective-permute-start | bytes 1966088 | tf_op jit(solution)/shard_map/ppermute | solution.py:164
  84.0 0.8 copy-done.14
  84.8 0.8 copy-done.18
  85.7 3.9 %collective-permute-start.13 = (bf16[2,640,256]{2,1,0:T(8,128)(2,1)S(1)}, bf16[2,640,256]{2,1,0:T(8,128)(2,1)}, u32[]{:S(2)}, u32[]{:S(2)}) collective-permute-start(bf16[2,640,256]{2,1,0:T(8,128)(2,1)S(1)} %collective-permute-done.9.refs_1_.refs_9_), channel_id=1, source_target_pairs={{0,32},{16,240},{32,64},{48,16},{64,96},{80,48},{96,128},{112,80},... | collective-permute-start | bytes 1966088 | tf_op jit(solution)/shard_map/ppermute | solution.py:178
  89.5 1.9 %collective-permute-start.10 = (bf16[2,640,256]{2,1,0:T(8,128)(2,1)S(1)}, bf16[2,640,256]{2,1,0:T(8,128)(2,1)S(1)}, u32[]{:S(2)}, u32[]{:S(2)}) collective-permute-start(bf16[2,640,256]{2,1,0:T(8,128)(2,1)S(1)} %collective-permute-done.9.refs_1_.refs_9_), channel_id=1, source_target_pairs={{0,16},{16,0},{1,17},{17,1},{2,18},{18,2},{3,19},{19,3},{4,20},{20... | collective-permute-start | bytes 1966088 | tf_op jit(solution)/shard_map/ppermute | solution.py:164
  91.5 0.0 collective-permute-done.11.refs_3_.refs_11_
  91.5 0.8 copy-done.20
  92.3 3.2 %collective-permute-start.12 = (bf16[2,640,256]{2,1,0:T(8,128)(2,1)S(1)}, bf16[2,640,256]{2,1,0:T(8,128)(2,1)}, u32[]{:S(2)}, u32[]{:S(2)}) collective-permute-start(bf16[2,640,256]{2,1,0:T(8,128)(2,1)S(1)} %collective-permute-done.11.refs_3_.refs_11_), channel_id=1, source_target_pairs={{0,16},{16,0},{1,17},{17,1},{2,18},{18,2},{3,19},{19,3},{4,20},{20... | collective-permute-start | bytes 1966088 | tf_op jit(solution)/shard_map/ppermute | solution.py:164
  95.6 1.8 %collective-permute-done.13.refs_2_.refs_13_ = bf16[2,640,256]{2,1,0:T(8,128)(2,1)} collective-permute-done((bf16[2,640,256]{2,1,0:T(8,128)(2,1)S(1)}, bf16[2,640,256]{2,1,0:T(8,128)(2,1)}, u32[]{:S(2)}, u32[]{:S(2)}) %collective-permute-start.13) | collective-permute-done | bytes 655392 | tf_op jit(solution)/shard_map/ppermute | solution.py:178
  97.4 0.9 copy-done.1
  98.3 4.5 %collective-permute-start.14 = (bf16[2,640,256]{2,1,0:T(8,128)(2,1)}, bf16[2,640,256]{2,1,0:T(8,128)(2,1)}, u32[]{:S(2)}, u32[]{:S(2)}) collective-permute-start(bf16[2,640,256]{2,1,0:T(8,128)(2,1)} %collective-permute-done.13.refs_2_.refs_13_), channel_id=1, source_target_pairs={{0,16},{16,0},{1,17},{17,1},{2,18},{18,2},{3,19},{19,3},{4,20},{20... | collective-permute-start | bytes 1966088 | tf_op jit(solution)/shard_map/ppermute | solution.py:164
  102.8 0.1 pad_add_fusion.index_ref
  102.8 1.1 copy-done.4
  103.9 1.1 shard_map.56.refs_0_
  105.0 0.2 copy-done.9
  105.2 0.2 copy-done.13
  105.4 0.2 copy-done.17
  105.6 1.4 %shard_map.57.refs_0_ = f32[640,192]{1,0:T(8,128)S(1)} custom-call(s32[2]{0:T(128)S(1)} %pad_add_fusion.index_ref, bf16[1,3,64,4096]{3,2,1,0:T(8,128)(2,1)S(1)} %copy-done, f32[640,192]{1,0:T(8,128)S(1)} %shard_map.56.refs_0_, bf16[2,640,256]{2,1,0:T(8,128)(2,1)S(1)} %copy-done.7, bf16[2,640,256]{2,1,0:T(8,128)(2,1)S(1)} %copy-done.9, ...), custom_call_target="tpu_custom_call" | custom-call | flops 251658240 | bytes 2621440 | tf_op jit(solution)/shard_map/pallas_call | solution.py:211
  107.1 0.0 copy-done.19
  107.1 0.2 copy-done.21
  107.3 1.4 %shard_map.58.refs_0_ = f32[640,192]{1,0:T(8,128)S(1)} custom-call(s32[2]{0:T(128)S(1)} %pad_add_fusion.index_ref, bf16[1,3,64,4096]{3,2,1,0:T(8,128)(2,1)S(1)} %copy-done, f32[640,192]{1,0:T(8,128)S(1)} %shard_map.57.refs_0_, bf16[2,640,256]{2,1,0:T(8,128)(2,1)S(1)} %copy-done.11, bf16[2,640,256]{2,1,0:T(8,128)(2,1)S(1)} %copy-done.15, ...), custom_call_target="tpu_custom_call" | custom-call | flops 251658240 | bytes 2621440 | tf_op jit(solution)/shard_map/pallas_call | solution.py:211
  108.7 1.2 %shard_map.59.refs_0_ = f32[640,192]{1,0:T(8,128)S(1)} custom-call(s32[2]{0:T(128)S(1)} %pad_add_fusion.index_ref, bf16[1,3,64,4096]{3,2,1,0:T(8,128)(2,1)S(1)} %copy-done, f32[640,192]{1,0:T(8,128)S(1)} %shard_map.58.refs_0_, bf16[2,640,256]{2,1,0:T(8,128)(2,1)S(1)} %collective-permute-done.9.refs_1_.refs_9_, bf16[2,640,256]{2,1,0:T(8,128)(2,1)S(1)} %copy-done.2, ...), custom_call_target="tpu_custom_call" | custom-call | flops 188743680 | bytes 1966080 | tf_op jit(solution)/shard_map/pallas_call | solution.py:211
  110.0 0.0 copy-start.5
  110.0 1.9 %shard_map.60.partial_ref = f32[640,192]{1,0:T(8,128)S(1)} custom-call(s32[2]{0:T(128)S(1)} %pad_add_fusion.index_ref, bf16[1,3,64,4096]{3,2,1,0:T(8,128)(2,1)S(1)} %copy-done, f32[640,192]{1,0:T(8,128)S(1)} %shard_map.59.refs_0_, bf16[2,640,256]{2,1,0:T(8,128)(2,1)} %collective-permute-done.12.refs_1_.refs_14_, ...), custom_call_target="tpu_custom_call" | custom-call | flops 125829120 | bytes 1310720 | tf_op jit(solution)/shard_map/pallas_call | solution.py:211
  111.9 4.9 %shard_map.61 = bf16[1,3,64,4096]{3,2,1,0:T(8,128)(2,1)} custom-call(s32[2]{0:T(128)S(1)} %pad_add_fusion.index_ref, bf16[1,3,64,4096]{3,2,1,0:T(8,128)(2,1)S(1)} %copy-done, f32[640,192]{1,0:T(8,128)S(1)} %shard_map.60.partial_ref, bf16[2,640,256]{2,1,0:T(8,128)(2,1)S(1)} %bitcast.9, bf16[2,640,256]{2,1,0:T(8,128)(2,1)S(1)} %copy-done.5, ...), custom_call_target="tpu_custom_call" | custom-call | flops 1006632960 | bytes 12058624 | tf_op jit(solution)/shard_map/pallas_call | solution.py:224
  (35 shorter events, 0.1 us)
Async XLA Ops:
  0.0 102.8 %copy-start = (bf16[1,3,64,4096]{3,2,1,0:T(8,128)(2,1)S(1)}, bf16[1,3,64,4096]{3,2,1,0:T(8,128)(2,1)}, u32[]{:S(2)}) copy-start(bf16[1,3,64,4096]{3,2,1,0:T(8,128)(2,1)} %weights_ref.11) | copy-start | bytes 4718596
  32.8 14.8 %collective-permute-start = (bf16[2,640,256]{2,1,0:T(8,128)(2,1)S(1)}, bf16[2,640,256]{2,1,0:T(8,128)(2,1)S(1)}, u32[]{:S(2)}, u32[]{:S(2)}) collective-permute-start(bf16[2,640,256]{2,1,0:T(8,128)(2,1)S(1)} %bitcast.6), channel_id=1, source_target_pairs={{0,16},{16,0},{1,17},{17,1},{2,18},{18,2},{3,19},{19,3},{4,20},{20... | collective-permute-start | bytes 1966088 | tf_op jit(solution)/shard_map/ppermute | solution.py:164
  36.9 18.2 %collective-permute-start.1 = (bf16[2,640,256]{2,1,0:T(8,128)(2,1)S(1)}, bf16[2,640,256]{2,1,0:T(8,128)(2,1)S(1)}, u32[]{:S(2)}, u32[]{:S(2)}) collective-permute-start(bf16[2,640,256]{2,1,0:T(8,128)(2,1)S(1)} %bitcast.7), channel_id=1, source_target_pairs={{0,32},{16,240},{32,64},{48,16},{64,96},{80,48},{96,128},{112,80},... | collective-permute-start | bytes 1966088 | tf_op jit(solution)/shard_map/ppermute | solution.py:178
  47.6 15.3 %collective-permute-start.2 = (bf16[2,640,256]{2,1,0:T(8,128)(2,1)S(1)}, bf16[2,640,256]{2,1,0:T(8,128)(2,1)S(1)}, u32[]{:S(2)}, u32[]{:S(2)}) collective-permute-start(bf16[2,640,256]{2,1,0:T(8,128)(2,1)S(1)} %collective-permute-done.refs_1_), channel_id=1, source_target_pairs={{0,32},{16,240},{32,64},{48,16},{64,96},{80,48},{96,128},{112,80},... | collective-permute-start | bytes 1966088 | tf_op jit(solution)/shard_map/ppermute | solution.py:178
  49.8 0.8 copy-start.3
  55.1 14.8 %collective-permute-start.5 = (bf16[2,640,256]{2,1,0:T(8,128)(2,1)S(1)}, bf16[2,640,256]{2,1,0:T(8,128)(2,1)S(1)}, u32[]{:S(2)}, u32[]{:S(2)}) collective-permute-start(bf16[2,640,256]{2,1,0:T(8,128)(2,1)S(1)} %collective-permute-done.1.refs_1_.refs_2_), channel_id=1, source_target_pairs={{0,32},{16,240},{32,64},{48,16},{64,96},{80,48},{96,128},{112,80},... | collective-permute-start | bytes 1966088 | tf_op jit(solution)/shard_map/ppermute | solution.py:178
  60.1 9.8 %collective-permute-start.3 = (bf16[2,640,256]{2,1,0:T(8,128)(2,1)S(1)}, bf16[2,640,256]{2,1,0:T(8,128)(2,1)S(1)}, u32[]{:S(2)}, u32[]{:S(2)}) collective-permute-start(bf16[2,640,256]{2,1,0:T(8,128)(2,1)S(1)} %collective-permute-done.1.refs_1_.refs_2_), channel_id=1, source_target_pairs={{0,16},{16,0},{1,17},{17,1},{2,18},{18,2},{3,19},{19,3},{4,20},{20... | collective-permute-start | bytes 1966088 | tf_op jit(solution)/shard_map/ppermute | solution.py:164
  62.1 0.8 copy-start.6
  62.9 14.9 %collective-permute-start.6 = (bf16[2,640,256]{2,1,0:T(8,128)(2,1)S(1)}, bf16[2,640,256]{2,1,0:T(8,128)(2,1)S(1)}, u32[]{:S(2)}, u32[]{:S(2)}) collective-permute-start(bf16[2,640,256]{2,1,0:T(8,128)(2,1)S(1)} %collective-permute-done.2.refs_2_.refs_3_), channel_id=1, source_target_pairs={{0,32},{16,240},{32,64},{48,16},{64,96},{80,48},{96,128},{112,80},... | collective-permute-start | bytes 1966088 | tf_op jit(solution)/shard_map/ppermute | solution.py:178
  67.1 10.7 %collective-permute-start.4 = (bf16[2,640,256]{2,1,0:T(8,128)(2,1)S(1)}, bf16[2,640,256]{2,1,0:T(8,128)(2,1)S(1)}, u32[]{:S(2)}, u32[]{:S(2)}) collective-permute-start(bf16[2,640,256]{2,1,0:T(8,128)(2,1)S(1)} %collective-permute-done.2.refs_2_.refs_3_), channel_id=1, source_target_pairs={{0,16},{16,0},{1,17},{17,1},{2,18},{18,2},{3,19},{19,3},{4,20},{20... | collective-permute-start | bytes 1966088 | tf_op jit(solution)/shard_map/ppermute | solution.py:164
  69.1 0.9 copy-start.8
  69.9 0.8 copy-start.12
  70.8 14.0 %collective-permute-start.9 = (bf16[2,640,256]{2,1,0:T(8,128)(2,1)S(1)}, bf16[2,640,256]{2,1,0:T(8,128)(2,1)S(1)}, u32[]{:S(2)}, u32[]{:S(2)}) collective-permute-start(bf16[2,640,256]{2,1,0:T(8,128)(2,1)S(1)} %collective-permute-done.5.refs_1_.refs_5_), channel_id=1, source_target_pairs={{0,32},{16,240},{32,64},{48,16},{64,96},{80,48},{96,128},{112,80},... | collective-permute-start | bytes 1966088 | tf_op jit(solution)/shard_map/ppermute | solution.py:178
  75.0 9.8 %collective-permute-start.7 = (bf16[2,640,256]{2,1,0:T(8,128)(2,1)S(1)}, bf16[2,640,256]{2,1,0:T(8,128)(2,1)S(1)}, u32[]{:S(2)}, u32[]{:S(2)}) collective-permute-start(bf16[2,640,256]{2,1,0:T(8,128)(2,1)S(1)} %collective-permute-done.5.refs_1_.refs_5_), channel_id=1, source_target_pairs={{0,16},{16,0},{1,17},{17,1},{2,18},{18,2},{3,19},{19,3},{4,20},{20... | collective-permute-start | bytes 1966088 | tf_op jit(solution)/shard_map/ppermute | solution.py:164
  76.9 0.9 copy-start.10
  77.8 0.8 copy-start.16
  78.7 12.8 %collective-permute-start.11 = (bf16[2,640,256]{2,1,0:T(8,128)(2,1)S(1)}, bf16[2,640,256]{2,1,0:T(8,128)(2,1)S(1)}, u32[]{:S(2)}, u32[]{:S(2)}) collective-permute-start(bf16[2,640,256]{2,1,0:T(8,128)(2,1)S(1)} %collective-permute-done.6.refs_2_.refs_7_), channel_id=1, source_target_pairs={{0,32},{16,240},{32,64},{48,16},{64,96},{80,48},{96,128},{112,80},... | collective-permute-start | bytes 1966088 | tf_op jit(solution)/shard_map/ppermute | solution.py:178
  82.0 9.5 %collective-permute-start.8 = (bf16[2,640,256]{2,1,0:T(8,128)(2,1)S(1)}, bf16[2,640,256]{2,1,0:T(8,128)(2,1)S(1)}, u32[]{:S(2)}, u32[]{:S(2)}) collective-permute-start(bf16[2,640,256]{2,1,0:T(8,128)(2,1)S(1)} %collective-permute-done.6.refs_2_.refs_7_), channel_id=1, source_target_pairs={{0,16},{16,0},{1,17},{17,1},{2,18},{18,2},{3,19},{19,3},{4,20},{20... | collective-permute-start | bytes 1966088 | tf_op jit(solution)/shard_map/ppermute | solution.py:164
  84.0 0.9 copy-start.14
  84.8 0.9 copy-start.18
  85.7 11.7 %collective-permute-start.13 = (bf16[2,640,256]{2,1,0:T(8,128)(2,1)S(1)}, bf16[2,640,256]{2,1,0:T(8,128)(2,1)}, u32[]{:S(2)}, u32[]{:S(2)}) collective-permute-start(bf16[2,640,256]{2,1,0:T(8,128)(2,1)S(1)} %collective-permute-done.9.refs_1_.refs_9_), channel_id=1, source_target_pairs={{0,32},{16,240},{32,64},{48,16},{64,96},{80,48},{96,128},{112,80},... | collective-permute-start | bytes 1966088 | tf_op jit(solution)/shard_map/ppermute | solution.py:178
  89.5 7.9 %collective-permute-start.10 = (bf16[2,640,256]{2,1,0:T(8,128)(2,1)S(1)}, bf16[2,640,256]{2,1,0:T(8,128)(2,1)S(1)}, u32[]{:S(2)}, u32[]{:S(2)}) collective-permute-start(bf16[2,640,256]{2,1,0:T(8,128)(2,1)S(1)} %collective-permute-done.9.refs_1_.refs_9_), channel_id=1, source_target_pairs={{0,16},{16,0},{1,17},{17,1},{2,18},{18,2},{3,19},{19,3},{4,20},{20... | collective-permute-start | bytes 1966088 | tf_op jit(solution)/shard_map/ppermute | solution.py:164
  91.5 0.8 copy-start.20
  92.3 17.6 %collective-permute-start.12 = (bf16[2,640,256]{2,1,0:T(8,128)(2,1)S(1)}, bf16[2,640,256]{2,1,0:T(8,128)(2,1)}, u32[]{:S(2)}, u32[]{:S(2)}) collective-permute-start(bf16[2,640,256]{2,1,0:T(8,128)(2,1)S(1)} %collective-permute-done.11.refs_3_.refs_11_), channel_id=1, source_target_pairs={{0,16},{16,0},{1,17},{17,1},{2,18},{18,2},{3,19},{19,3},{4,20},{20... | collective-permute-start | bytes 1966088 | tf_op jit(solution)/shard_map/ppermute | solution.py:164
  97.4 0.9 copy-start.1
  98.3 13.6 %collective-permute-start.14 = (bf16[2,640,256]{2,1,0:T(8,128)(2,1)}, bf16[2,640,256]{2,1,0:T(8,128)(2,1)}, u32[]{:S(2)}, u32[]{:S(2)}) collective-permute-start(bf16[2,640,256]{2,1,0:T(8,128)(2,1)} %collective-permute-done.13.refs_2_.refs_13_), channel_id=1, source_target_pairs={{0,16},{16,0},{1,17},{17,1},{2,18},{18,2},{3,19},{19,3},{4,20},{20... | collective-permute-start | bytes 1966088 | tf_op jit(solution)/shard_map/ppermute | solution.py:164
  102.8 1.1 copy-start.4
  103.9 1.1 copy-start.7
  103.9 1.3 %copy-start.9 = (bf16[2,640,256]{2,1,0:T(8,128)(2,1)S(1)}, bf16[2,640,256]{2,1,0:T(8,128)(2,1)}, u32[]{:S(2)}) copy-start(bf16[2,640,256]{2,1,0:T(8,128)(2,1)} %copy-done.8) | copy-start | bytes 1966084
  103.9 1.5 %copy-start.13 = (bf16[2,640,256]{2,1,0:T(8,128)(2,1)S(1)}, bf16[2,640,256]{2,1,0:T(8,128)(2,1)}, u32[]{:S(2)}) copy-start(bf16[2,640,256]{2,1,0:T(8,128)(2,1)} %copy-done.12) | copy-start | bytes 1966084
  103.9 1.7 %copy-start.17 = (bf16[2,640,256]{2,1,0:T(8,128)(2,1)S(1)}, bf16[2,640,256]{2,1,0:T(8,128)(2,1)}, u32[]{:S(2)}) copy-start(bf16[2,640,256]{2,1,0:T(8,128)(2,1)} %copy-done.16) | copy-start | bytes 1966084
  105.6 1.4 %copy-start.11 = (bf16[2,640,256]{2,1,0:T(8,128)(2,1)S(1)}, bf16[2,640,256]{2,1,0:T(8,128)(2,1)}, u32[]{:S(2)}) copy-start(bf16[2,640,256]{2,1,0:T(8,128)(2,1)} %copy-done.10) | copy-start | bytes 1966084
  105.6 1.4 %copy-start.15 = (bf16[2,640,256]{2,1,0:T(8,128)(2,1)S(1)}, bf16[2,640,256]{2,1,0:T(8,128)(2,1)}, u32[]{:S(2)}) copy-start(bf16[2,640,256]{2,1,0:T(8,128)(2,1)} %copy-done.14) | copy-start | bytes 1966084
  105.6 1.5 %copy-start.19 = (bf16[2,640,256]{2,1,0:T(8,128)(2,1)S(1)}, bf16[2,640,256]{2,1,0:T(8,128)(2,1)}, u32[]{:S(2)}) copy-start(bf16[2,640,256]{2,1,0:T(8,128)(2,1)} %copy-done.18) | copy-start | bytes 1966084
  105.6 1.7 %copy-start.21 = (bf16[2,640,256]{2,1,0:T(8,128)(2,1)S(1)}, bf16[2,640,256]{2,1,0:T(8,128)(2,1)}, u32[]{:S(2)}) copy-start(bf16[2,640,256]{2,1,0:T(8,128)(2,1)} %copy-done.20) | copy-start | bytes 1966084
  107.3 1.4 %copy-start.2 = (bf16[2,640,256]{2,1,0:T(8,128)(2,1)S(1)}, bf16[2,640,256]{2,1,0:T(8,128)(2,1)}, u32[]{:S(2)}) copy-start(bf16[2,640,256]{2,1,0:T(8,128)(2,1)} %copy-done.1) | copy-start | bytes 1966084
  110.0 1.9 %copy-start.5 = (bf16[2,640,256]{2,1,0:T(8,128)(2,1)S(1)}, bf16[2,640,256]{2,1,0:T(8,128)(2,1)}, u32[]{:S(2)}) copy-start(bf16[2,640,256]{2,1,0:T(8,128)(2,1)} %copy-done.3) | copy-start | bytes 1966084

commit v5 on v4

--- a/solution.py
+++ b/solution.py
@@ -13,13 +13,28 @@
 F32 = jnp.float32
 EARLY_VMEM = 8 << 20
 GRADS_VMEM = 16 << 20
-FORWARD_GROUP = 4
+FORWARD_GROUP = 2
 GRADS_GROUP = 2
 
 
-def pack_kernel(routes_ref, gates_ref, tokens_ref, cotangent_ref, out_ref):
+def pack_kernel(routes_in, gates_in, tokens_in, cotangent_in, out_ref, *scratch):
+    routes_ref, gates_ref, tokens_ref, cotangent_ref, packed, in_sems, out_sems = scratch
+    loads = []
+    for n, (source, place) in enumerate(
+        (
+            (routes_in, routes_ref),
+            (gates_in, gates_ref),
+            (tokens_in, tokens_ref),
+            (cotangent_in, cotangent_ref),
+        )
+    ):
+        load = pltpu.make_async_copy(source, place, in_sems.at[n])
+        load.start()
+        loads.append(load)
     tokens = routes_ref.shape[1]
     copies, slots, width = out_ref.shape
+    for load in loads:
+        load.wait()
     experts = slots // CAP
     ids = lax.broadcasted_iota(jnp.int32, (experts, tokens), 0)
     named = jnp.zeros((experts, tokens), F32)
@@ -41,22 +56,35 @@
         weights.append(jnp.sum(jnp.where(hit, weight[e : e + 1, :], 0.0), axis=1, keepdims=True))
     select = jnp.concatenate(select, axis=0).astype(BF16)
     weights = jnp.concatenate(weights, axis=0)
-    rows = jnp.dot(select, tokens_ref[...], preferred_element_type=F32).astype(BF16)
+    half = width // 2
+    stores = []
+
+    def store(part):
+        for j in range(copies):
+            copy = pltpu.make_async_copy(
+                packed.at[part], out_ref.at[j, :, pl.ds(part * half, half)], out_sems.at[part, j]
+            )
+            copy.start()
+            stores.append(copy)
+
+    rows = jnp.dot(select, tokens_ref[...], preferred_element_type=F32)
+    packed[0] = rows.astype(BF16)
+    store(0)
     scaled = jnp.dot(select, cotangent_ref[...], preferred_element_type=F32)
-    scaled = (scaled * weights).astype(BF16)
-    for j in range(copies):
-        out_ref[j, :, : width // 2] = rows
-        out_ref[j, :, width // 2 :] = scaled
+    packed[1] = (scaled * weights).astype(BF16)
+    store(1)
+    for copy in stores:
+        copy.wait()
 
 
 def column(index_ref, ring_size, half, block, j):
-    step, chain, turned = block
+    step, chain, turned, sides = block
     ring, core = index_ref[0], index_ref[1]
     way = (1 - 2 * core) * (1 - 2 * turned)
     z = lax.rem(ring - way * step + 2 * ring_size, ring_size)
     other = chain ^ turned
     c = core + other - 2 * core * other
-    return pl.multiple_of(((j * ring_size + z) * 2 + c) * half, half)
+    return pl.multiple_of(((sides[j] * ring_size + z) * 2 + c) * half, half)
 
 
 def joined(pieces, part):
@@ -68,8 +96,7 @@
 
 
 def add_forward(ring_size, index_ref, weights_ref, total, pieces, blocks):
-    halves, half = pieces[0].shape[0], pieces[0].shape[2] // 2
-    hidden_units = weights_ref.shape[2]
+    half = pieces[0].shape[2] // 2
     along = (((1,), (1,)), ((), ()))
 
     def weight_block(m):
@@ -77,17 +104,18 @@
             [
                 weights_ref[0, m, :, pl.ds(column(index_ref, ring_size, half, block, j), half)]
                 for block in blocks
-                for j in range(halves)
+                for j in range(len(block[3]))
             ],
             axis=1,
         )
 
+    hidden_units = weights_ref.shape[2]
     pair = jnp.concatenate([weight_block(0), weight_block(1)], axis=0)
-    total[:, : 2 * hidden_units] += lax.dot_general(
-        joined(pieces, 0), pair, along, preferred_element_type=F32
-    )
-    total[:, 2 * hidden_units :] += lax.dot_general(
-        joined(pieces, 1), weight_block(2), along, preferred_element_type=F32
+    total[: 2 * hidden_units] += lax.dot_general(
+        pair, joined(pieces, 0), along, preferred_element_type=F32
+    )
+    total[2 * hidden_units :] += lax.dot_general(
+        weight_block(2), joined(pieces, 1), along, preferred_element_type=F32
     )
 
 
@@ -107,31 +135,32 @@
     count = len(blocks)
     sources, out_ref = refs[:count], refs[count]
     total, out_buf, sems = refs[count + 1 :]
-    halves, half = sources[0].shape[0], sources[0].shape[2] // 2
+    half = sources[0].shape[2] // 2
     hidden_units = weights_ref.shape[2]
     last = [blocks.index(block) for block in late]
     total[...] = partial_ref[...]
     add_forward(ring_size, index_ref, weights_ref, total, [sources[k] for k in last], late)
-    gate_part = total[:, :hidden_units]
-    up_part = total[:, hidden_units : 2 * hidden_units]
-    back_hidden = total[:, 2 * hidden_units :]
+    gate_part = total[:hidden_units]
+    up_part = total[hidden_units : 2 * hidden_units]
+    back_hidden = total[2 * hidden_units :]
     sigmoid_part = jax.nn.sigmoid(gate_part)
     silu = gate_part * sigmoid_part
     hidden = (silu * up_part).astype(BF16)
     derivative = sigmoid_part * (1.0 + gate_part * (1.0 - sigmoid_part))
     pre_gate = (back_hidden * up_part * derivative).astype(BF16)
     pre_up = (back_hidden * silu).astype(BF16)
-    both = jnp.concatenate([pre_gate, pre_up], axis=1).T
-    hidden_t = hidden.T
+    both = jnp.concatenate([pre_gate, pre_up], axis=0)
     copies = []
     for n in range(0, count, GRADS_GROUP):
         chosen = range(n, min(n + GRADS_GROUP, count))
         pieces = [sources[k] for k in chosen]
         ins = jnp.dot(both, joined(pieces, 0), preferred_element_type=F32).astype(BF16)
-        outs = jnp.dot(hidden_t, joined(pieces, 1), preferred_element_type=F32).astype(BF16)
-        for m, k in enumerate(chosen):
-            for j in range(halves):
-                cut = slice((m * halves + j) * half, (m * halves + j + 1) * half)
+        outs = jnp.dot(hidden, joined(pieces, 1), preferred_element_type=F32).astype(BF16)
+        at = 0
+        for k in chosen:
+            for j in range(len(blocks[k][3])):
+                cut = slice(at, at + half)
+                at += half
                 out_buf[k, j, 0] = ins[:hidden_units, cut]
                 out_buf[k, j, 1] = ins[hidden_units:, cut]
                 out_buf[k, j, 2] = outs[:, cut]
@@ -153,6 +182,17 @@
     send = pl.pallas_call(
         pack_kernel,
         out_shape=jax.ShapeDtypeStruct((2, slots, 2 * width), BF16),
+        in_specs=[pl.BlockSpec(memory_space=pl.ANY)] * 4,
+        out_specs=pl.BlockSpec(memory_space=pl.ANY),
+        scratch_shapes=[
+            pltpu.VMEM(routes.shape[::-1], routes.dtype),
+            pltpu.VMEM(gates.shape[::-1], F32),
+            pltpu.VMEM(tokens.shape, BF16),
+            pltpu.VMEM(cotangent.shape, BF16),
+            pltpu.VMEM((2, slots, width), BF16),
+            pltpu.SemaphoreType.DMA((4,)),
+            pltpu.SemaphoreType.DMA((2, 2)),
+        ],
     )(routes.T, gates.T, tokens, cotangent)
     around = [
         (z * 2 + c, ((z + 1 - 2 * c) % ring_size) * 2 + c)
@@ -171,20 +211,29 @@
         tiled=True,
     ).reshape(2, slots, 2 * width)
     far = ring_size // 2
-    held = {(0, 0, 0): own, (0, 1, 0): swapped(own)}
+    both = (0, 1)
+    held = {(0, 0, 0, both): own, (0, 1, 0, both): swapped(own)}
     raw = {}
-    for step in range(1, far + 1):
-        for chain in range(2 if step < far else 1):
-            piece = lax.ppermute(held[step - 1, chain, 0], ("ring", "core"), around)
-            raw[step, chain, 0] = piece
-            if step > 1:
-                crossed = swapped(held[step - 1, chain, 0])
-                raw[step - 1, chain, 1] = crossed
-                piece, crossed = lax.optimization_barrier((piece, crossed))
-                held[step - 1, chain, 1] = crossed
-            held[step, chain, 0] = piece
-    held[far - 1, 1, 1] = swapped(held[far - 1, 1, 0])
-    held[far, 0, 1] = swapped(held[far, 0, 0])
+    ring = ("ring", "core")
+
+    def cross(step, chain, piece):
+        key = (step - 1, chain, 1, both)
+        raw[key] = swapped(held[step - 1, chain, 0, both])
+        piece, held[key] = lax.optimization_barrier((piece, raw[key]))
+        return piece
+
+    for step in range(1, far):
+        for chain in range(2):
+            piece = lax.ppermute(held[step - 1, chain, 0, both], ring, around)
+            raw[step, chain, 0, both] = piece
+            held[step, chain, 0, both] = cross(step, chain, piece) if step > 1 else piece
+    for side in both:
+        piece = held[far - 1, 0, 0, both][side : side + 1]
+        held[far, 0, 0, (side,)] = lax.ppermute(piece, ring, around)
+    for chain in range(2):
+        held[far - 1, chain, 1, both] = swapped(held[far - 1, chain, 0, both])
+    for side in both:
+        held[far, 0, 1, (side,)] = swapped(held[far, 0, 0, (side,)])
     blocks = list(held)
     index = jnp.stack([lax.axis_index("ring"), lax.axis_index("core")]).astype(jnp.int32)
     hidden_units = expert_weights.shape[2]
@@ -195,14 +244,14 @@
     weight_bytes = 6 * hidden_units * features
     block_flops = 12 * slots * width * hidden_units
     early = {
-        "early_0": [(0, 0, 0), (0, 1, 0)],
-        "early_1": [(1, c, t) for t in range(2) for c in range(2)],
-        "early_2": [(s, c, t) for s in range(2, far - 1) for t in range(2) for c in range(2)],
-        "early_3": [(far - 1, 0, 0), (far - 1, 0, 1), (far - 1, 1, 0)],
-        "early_4": [(far - 1, 1, 1), (far, 0, 0)],
+        "early_0": [(0, 0, 0, both), (0, 1, 0, both)],
+        "early_1": [(1, c, t, both) for t in range(2) for c in range(2)],
+        "early_2": [(s, c, t, both) for s in range(2, far - 1) for t in range(2) for c in range(2)],
+        "early_3": [(far - 1, 0, 0, both), (far - 1, 0, 1, both), (far - 1, 1, 0, both)],
+        "early_4": [(far - 1, 1, 1, both), (far, 0, 0, (0,)), (far, 0, 0, (1,)), (far, 0, 1, (0,))],
     }
-    late = [(far, 0, 1)]
-    sums = jax.ShapeDtypeStruct((slots, 3 * hidden_units), F32)
+    late = [(far, 0, 1, (1,))]
+    sums = jax.ShapeDtypeStruct((3 * hidden_units, slots), F32)
 
     partials = []
     for chosen in early.values():

time: 118 us -> 124 us (1.051)
  starting transfers between devices: 55 us -> 59.7 us
  waiting for transfers between devices: 6.32 us -> 8.29 us
  local copies, waits for them, and re-layouts: 10.4 us -> 8.62 us
    ppermute x8 -> x9, starting transfers between devices: 21.5 us -> 24.3 us  [swapped(): return lax.ppermute(x, 'core', [(0, 1), (1, 0)])]
    ppermute x7 -> x8, waiting for transfers between devices: 6.3 us -> 8.27 us  [the longest x6 4.48 us: device_step(): piece = lax.ppermute(held[step - 1, chain, 0, both], ring, around)]
    ppermute x7 -> x8, starting transfers between devices: 33.6 us -> 35.4 us  [the longest x6 29.7 us: device_step(): piece = lax.ppermute(held[step - 1, chain, 0, both], ring, around)]
    unnamed x44 -> x40, local copies, waits for them, and re-layouts: 10.4 us -> 8.58 us
  transfers between devices with their start and end apart: 15 -> 17, of which waited for: 2 -> 2; matrix products, arithmetic and copies ran while one was open for 0% -> 0% of each run, Pallas kernels for 6% -> 6%
where the time goes in v5:
time: 124 us; the launch traced here: 123 us
  starting transfers between devices  59.7 us (48%)
  blocking collectives  30.5 us (25%)
  Pallas kernels  15 us (12%)
  local copies, waits for them, and re-layouts  8.62 us (7%)
  waiting for transfers between devices  8.29 us (7%)
    all_to_all x1, blocking collectives, device_step(): lax.all_to_all(send.reshape(2 * groups, CAP, 2 * width), ('half', 'expert...  30.5 us
    ppermute x6, starting transfers between devices, device_step(): piece = lax.ppermute(held[step - 1, chain, 0, both], ring, around)  29.7 us
    ppermute x9, starting transfers between devices, swapped(): return lax.ppermute(x, 'core', [(0, 1), (1, 0)])  24.3 us
    unnamed x40, local copies, waits for them, and re-layouts  8.58 us
    pallas_call x5, Pallas kernels, device_step(): pl.pallas_call(functools.partial(forward_kernel, ring_size, chosen, chain...  7.85 us
    ppermute x2, starting transfers between devices, device_step(): held[far, 0, 0, (side,)] = lax.ppermute(piece, ring, around)  5.66 us
    pallas_call x1, Pallas kernels, device_step(): pl.pallas_call(functools.partial(grads_kernel, ring_size, blocks, late),...  4.88 us
    ppermute x6, waiting for transfers between devices, device_step(): piece = lax.ppermute(held[step - 1, chain, 0, both], ring, around)  4.48 us
  transfers between devices with their start and end apart: 17, of which 2 were waited for; matrix products, arithmetic and copies ran while one was open for 0% of the time, Pallas kernels for 6%

profile of v5, /device:TPU:1, one launch (start us, length us, event | category | flops | bytes accessed | tf_op | source)
XLA Modules:
  0.0 122.6 jit_solution(13614123122322008691)
XLA Ops:
  0.0 2.2 %shard_map.55 = bf16[2,640,256]{2,1,0:T(8,128)(2,1)} custom-call(s32[2,128]{1,0:T(2,128)} %bitcast.11, f32[2,128]{1,0:T(2,128)} %bitcast.12, bf16[128,128]{1,0:T(8,128)(2,1)} %tokens_in.1, bf16[128,128]{1,0:T(8,128)(2,1)} %cotangent_in.1), custom_call_target="tpu_custom_call" | custom-call | tf_op jit(solution)/shard_map/pallas_call | solution.py:182
  2.2 30.5 %all_to_all.5 = bf16[32,40,256]{2,1,0:T(8,128)(2,1)S(1)} all-to-all(bf16[32,40,256]{2,1,0:T(8,128)(2,1)} %bitcast.10), channel_id=1, replica_groups=mesh['half'=2,'ring'=8,'core'=2,'expert'=16] {'half','expert'}, dimensions={0} | all-to-all | bytes 1310720 | tf_op jit(solution)/shard_map/all_to_all | solution.py:206
  32.8 4.2 %collective-permute-start = (bf16[2,640,256]{2,1,0:T(8,128)(2,1)S(1)}, bf16[2,640,256]{2,1,0:T(8,128)(2,1)S(1)}, u32[]{:S(2)}, u32[]{:S(2)}) collective-permute-start(bf16[2,640,256]{2,1,0:T(8,128)(2,1)S(1)} %bitcast.6), channel_id=1, source_target_pairs={{0,16},{16,0},{1,17},{17,1},{2,18},{18,2},{3,19},{19,3},{4,20},{20... | collective-permute-start | bytes 1966088 | tf_op jit(solution)/shard_map/ppermute | solution.py:204
  36.9 10.7 %collective-permute-start.1 = (bf16[2,640,256]{2,1,0:T(8,128)(2,1)S(1)}, bf16[2,640,256]{2,1,0:T(8,128)(2,1)S(1)}, u32[]{:S(2)}, u32[]{:S(2)}) collective-permute-start(bf16[2,640,256]{2,1,0:T(8,128)(2,1)S(1)} %bitcast.7), channel_id=1, source_target_pairs={{0,32},{16,240},{32,64},{48,16},{64,96},{80,48},{96,128},{112,80},... | collective-permute-start | bytes 1966088 | tf_op jit(solution)/shard_map/ppermute | solution.py:227
  47.6 0.0 collective-permute-done.refs_1_
  47.6 2.2 %collective-permute-start.2 = (bf16[2,640,256]{2,1,0:T(8,128)(2,1)S(1)}, bf16[2,640,256]{2,1,0:T(8,128)(2,1)S(1)}, u32[]{:S(2)}, u32[]{:S(2)}) collective-permute-start(bf16[2,640,256]{2,1,0:T(8,128)(2,1)S(1)} %collective-permute-done.refs_1_), channel_id=1, source_target_pairs={{0,32},{16,240},{32,64},{48,16},{64,96},{80,48},{96,128},{112,80},... | collective-permute-start | bytes 1966088 | tf_op jit(solution)/shard_map/ppermute | solution.py:227
  49.8 0.0 copy-start.1
  49.8 0.8 copy-done.1
  50.7 4.5 %collective-permute-done.1.refs_1_.refs_2_ = bf16[2,640,256]{2,1,0:T(8,128)(2,1)S(1)} collective-permute-done((bf16[2,640,256]{2,1,0:T(8,128)(2,1)S(1)}, bf16[2,640,256]{2,1,0:T(8,128)(2,1)S(1)}, u32[]{:S(2)}, u32[]{:S(2)}) %collective-permute-start.1) | collective-permute-done | bytes 655392 | tf_op jit(solution)/shard_map/ppermute | solution.py:227
  55.1 5.0 %collective-permute-start.5 = (bf16[2,640,256]{2,1,0:T(8,128)(2,1)S(1)}, bf16[2,640,256]{2,1,0:T(8,128)(2,1)S(1)}, u32[]{:S(2)}, u32[]{:S(2)}) collective-permute-start(bf16[2,640,256]{2,1,0:T(8,128)(2,1)S(1)} %collective-permute-done.1.refs_1_.refs_2_), channel_id=1, source_target_pairs={{0,32},{16,240},{32,64},{48,16},{64,96},{80,48},{96,128},{112,80},... | collective-permute-start | bytes 1966088 | tf_op jit(solution)/shard_map/ppermute | solution.py:227
  60.1 1.9 %collective-permute-start.3 = (bf16[2,640,256]{2,1,0:T(8,128)(2,1)S(1)}, bf16[2,640,256]{2,1,0:T(8,128)(2,1)S(1)}, u32[]{:S(2)}, u32[]{:S(2)}) collective-permute-start(bf16[2,640,256]{2,1,0:T(8,128)(2,1)S(1)} %collective-permute-done.1.refs_1_.refs_2_), channel_id=1, source_target_pairs={{0,16},{16,0},{1,17},{17,1},{2,18},{18,2},{3,19},{19,3},{4,20},{20... | collective-permute-start | bytes 1966088 | tf_op jit(solution)/shard_map/ppermute | solution.py:204
  62.1 0.8 copy-done.4
  62.9 4.2 %collective-permute-start.6 = (bf16[2,640,256]{2,1,0:T(8,128)(2,1)S(1)}, bf16[2,640,256]{2,1,0:T(8,128)(2,1)S(1)}, u32[]{:S(2)}, u32[]{:S(2)}) collective-permute-start(bf16[2,640,256]{2,1,0:T(8,128)(2,1)S(1)} %collective-permute-done.2.refs_2_.refs_3_), channel_id=1, source_target_pairs={{0,32},{16,240},{32,64},{48,16},{64,96},{80,48},{96,128},{112,80},... | collective-permute-start | bytes 1966088 | tf_op jit(solution)/shard_map/ppermute | solution.py:227
  67.2 1.9 %collective-permute-start.4 = (bf16[2,640,256]{2,1,0:T(8,128)(2,1)S(1)}, bf16[2,640,256]{2,1,0:T(8,128)(2,1)S(1)}, u32[]{:S(2)}, u32[]{:S(2)}) collective-permute-start(bf16[2,640,256]{2,1,0:T(8,128)(2,1)S(1)} %collective-permute-done.2.refs_2_.refs_3_), channel_id=1, source_target_pairs={{0,16},{16,0},{1,17},{17,1},{2,18},{18,2},{3,19},{19,3},{4,20},{20... | collective-permute-start | bytes 1966088 | tf_op jit(solution)/shard_map/ppermute | solution.py:204
  69.1 0.8 copy-done.6
  70.0 0.8 copy-done.10
  70.8 4.2 %collective-permute-start.9 = (bf16[2,640,256]{2,1,0:T(8,128)(2,1)S(1)}, bf16[2,640,256]{2,1,0:T(8,128)(2,1)S(1)}, u32[]{:S(2)}, u32[]{:S(2)}) collective-permute-start(bf16[2,640,256]{2,1,0:T(8,128)(2,1)S(1)} %collective-permute-done.5.refs_1_.refs_5_), channel_id=1, source_target_pairs={{0,32},{16,240},{32,64},{48,16},{64,96},{80,48},{96,128},{112,80},... | collective-permute-start | bytes 1966088 | tf_op jit(solution)/shard_map/ppermute | solution.py:227
  75.0 1.9 %collective-permute-start.7 = (bf16[2,640,256]{2,1,0:T(8,128)(2,1)S(1)}, bf16[2,640,256]{2,1,0:T(8,128)(2,1)S(1)}, u32[]{:S(2)}, u32[]{:S(2)}) collective-permute-start(bf16[2,640,256]{2,1,0:T(8,128)(2,1)S(1)} %collective-permute-done.5.refs_1_.refs_5_), channel_id=1, source_target_pairs={{0,16},{16,0},{1,17},{17,1},{2,18},{18,2},{3,19},{19,3},{4,20},{20... | collective-permute-start | bytes 1966088 | tf_op jit(solution)/shard_map/ppermute | solution.py:204
  77.0 0.8 copy-done.8
  77.8 0.0 collective-permute-done.6.refs_2_.refs_7_
  77.8 0.8 copy-done.14
  78.7 3.4 %collective-permute-start.11 = (bf16[2,640,256]{2,1,0:T(8,128)(2,1)S(1)}, bf16[2,640,256]{2,1,0:T(8,128)(2,1)S(1)}, u32[]{:S(2)}, u32[]{:S(2)}) collective-permute-start(bf16[2,640,256]{2,1,0:T(8,128)(2,1)S(1)} %collective-permute-done.6.refs_2_.refs_7_), channel_id=1, source_target_pairs={{0,32},{16,240},{32,64},{48,16},{64,96},{80,48},{96,128},{112,80},... | collective-permute-start | bytes 1966088 | tf_op jit(solution)/shard_map/ppermute | solution.py:227
  82.1 1.9 %collective-permute-start.8 = (bf16[2,640,256]{2,1,0:T(8,128)(2,1)S(1)}, bf16[2,640,256]{2,1,0:T(8,128)(2,1)S(1)}, u32[]{:S(2)}, u32[]{:S(2)}) collective-permute-start(bf16[2,640,256]{2,1,0:T(8,128)(2,1)S(1)} %collective-permute-done.6.refs_2_.refs_7_), channel_id=1, source_target_pairs={{0,16},{16,0},{1,17},{17,1},{2,18},{18,2},{3,19},{19,3},{4,20},{20... | collective-permute-start | bytes 1966088 | tf_op jit(solution)/shard_map/ppermute | solution.py:204
  84.0 0.0 collective-permute-done.9.refs_1_.refs_9_
  84.0 0.0 collective-permute-done.7.refs_3_.refs_8_
  84.0 0.8 copy-done.16
  84.9 2.9 %collective-permute-start.10 = (bf16[2,640,256]{2,1,0:T(8,128)(2,1)S(1)}, bf16[2,640,256]{2,1,0:T(8,128)(2,1)}, u32[]{:S(2)}, u32[]{:S(2)}) collective-permute-start(bf16[2,640,256]{2,1,0:T(8,128)(2,1)S(1)} %collective-permute-done.9.refs_1_.refs_9_), channel_id=1, source_target_pairs={{0,16},{16,0},{1,17},{17,1},{2,18},{18,2},{3,19},{19,3},{4,20},{20... | collective-permute-start | bytes 1966088 | tf_op jit(solution)/shard_map/ppermute | solution.py:204
  87.8 3.2 %collective-permute-start.13 = (bf16[1,640,256]{2,1,0:T(8,128)(2,1)S(1)}, bf16[1,640,256]{2,1,0:T(8,128)(2,1)}, u32[]{:S(2)}, u32[]{:S(2)}) collective-permute-start(bf16[1,640,256]{2,1,0:T(8,128)(2,1)S(1)} %get-tuple-element.22), channel_id=1, source_target_pairs={{0,32},{16,240},{32,64},{48,16},{64,96},{80,48},{96,128},{112,80},... | collective-permute-start | bytes 983048 | tf_op jit(solution)/shard_map/ppermute | solution.py:232
  91.1 0.0 collective-permute-done.11.refs_3_.refs_11_
  91.1 0.8 copy-done.18
  91.9 3.7 %collective-permute-start.12 = (bf16[2,640,256]{2,1,0:T(8,128)(2,1)S(1)}, bf16[2,640,256]{2,1,0:T(8,128)(2,1)}, u32[]{:S(2)}, u32[]{:S(2)}) collective-permute-start(bf16[2,640,256]{2,1,0:T(8,128)(2,1)S(1)} %collective-permute-done.11.refs_3_.refs_11_), channel_id=1, source_target_pairs={{0,16},{16,0},{1,17},{17,1},{2,18},{18,2},{3,19},{19,3},{4,20},{20... | collective-permute-start | bytes 1966088 | tf_op jit(solution)/shard_map/ppermute | solution.py:204
  95.6 2.4 %collective-permute-start.14 = (bf16[1,640,256]{2,1,0:T(8,128)(2,1)S(1)}, bf16[1,640,256]{2,1,0:T(8,128)(2,1)}, u32[]{:S(2)}, u32[]{:S(2)}) collective-permute-start(bf16[1,640,256]{2,1,0:T(8,128)(2,1)S(1)} %get-tuple-element.21), channel_id=1, source_target_pairs={{0,32},{16,240},{32,64},{48,16},{64,96},{80,48},{96,128},{112,80},... | collective-permute-start | bytes 983048 | tf_op jit(solution)/shard_map/ppermute | solution.py:232
  98.0 2.0 %collective-permute-start.15 = (bf16[1,640,256]{2,1,0:T(8,128)(2,1)}, bf16[1,640,256]{2,1,0:T(8,128)(2,1)}, u32[]{:S(2)}, u32[]{:S(2)}) collective-permute-start(bf16[1,640,256]{2,1,0:T(8,128)(2,1)} %collective-permute-done.13.refs_2_.refs_12_), channel_id=1, source_target_pairs={{0,16},{16,0},{1,17},{17,1},{2,18},{18,2},{3,19},{19,3},{4,20},{20... | collective-permute-start | bytes 983048 | tf_op jit(solution)/shard_map/ppermute | solution.py:204
  100.0 3.8 %collective-permute-done.14.refs_3_.refs_13_ = bf16[1,640,256]{2,1,0:T(8,128)(2,1)} collective-permute-done((bf16[1,640,256]{2,1,0:T(8,128)(2,1)S(1)}, bf16[1,640,256]{2,1,0:T(8,128)(2,1)}, u32[]{:S(2)}, u32[]{:S(2)}) %collective-permute-start.14) | collective-permute-done | bytes 327712 | tf_op jit(solution)/shard_map/ppermute | solution.py:232
  103.8 4.0 %collective-permute-start.16 = (bf16[1,640,256]{2,1,0:T(8,128)(2,1)}, bf16[1,640,256]{2,1,0:T(8,128)(2,1)}, u32[]{:S(2)}, u32[]{:S(2)}) collective-permute-start(bf16[1,640,256]{2,1,0:T(8,128)(2,1)} %collective-permute-done.14.refs_3_.refs_13_), channel_id=1, source_target_pairs={{0,16},{16,0},{1,17},{17,1},{2,18},{18,2},{3,19},{19,3},{4,20},{20... | collective-permute-start | bytes 983048 | tf_op jit(solution)/shard_map/ppermute | solution.py:204
  107.8 0.1 pad_add_fusion.index_ref
  107.9 1.1 copy-done.2
  109.0 1.1 shard_map.56.refs_0_
  110.1 0.2 copy-done.7
  110.3 0.2 copy-done.11
  110.5 0.2 copy-done.15
  110.7 1.5 %shard_map.57.refs_0_ = f32[192,640]{1,0:T(8,128)S(1)} custom-call(s32[2]{0:T(128)S(1)} %pad_add_fusion.index_ref, bf16[1,3,64,4096]{3,2,1,0:T(8,128)(2,1)S(1)} %copy-done, f32[192,640]{1,0:T(8,128)S(1)} %shard_map.56.refs_0_, bf16[2,640,256]{2,1,0:T(8,128)(2,1)S(1)} %copy-done.5, bf16[2,640,256]{2,1,0:T(8,128)(2,1)S(1)} %copy-done.7, ...), custom_call_target="tpu_custom_call" | custom-call | flops 251658240 | bytes 2621440 | tf_op jit(solution)/shard_map/pallas_call | solution.py:260
  112.2 0.2 copy-done.19
  112.3 1.4 %shard_map.58.refs_0_ = f32[192,640]{1,0:T(8,128)S(1)} custom-call(s32[2]{0:T(128)S(1)} %pad_add_fusion.index_ref, bf16[1,3,64,4096]{3,2,1,0:T(8,128)(2,1)S(1)} %copy-done, f32[192,640]{1,0:T(8,128)S(1)} %shard_map.57.refs_0_, bf16[2,640,256]{2,1,0:T(8,128)(2,1)S(1)} %copy-done.9, bf16[2,640,256]{2,1,0:T(8,128)(2,1)S(1)} %copy-done.13, ...), custom_call_target="tpu_custom_call" | custom-call | flops 251658240 | bytes 2621440 | tf_op jit(solution)/shard_map/pallas_call | solution.py:260
  113.8 1.8 %shard_map.59.refs_0_ = f32[192,640]{1,0:T(8,128)S(1)} custom-call(s32[2]{0:T(128)S(1)} %pad_add_fusion.index_ref, bf16[1,3,64,4096]{3,2,1,0:T(8,128)(2,1)S(1)} %copy-done, f32[192,640]{1,0:T(8,128)S(1)} %shard_map.58.refs_0_, bf16[2,640,256]{2,1,0:T(8,128)(2,1)S(1)} %collective-permute-done.9.refs_1_.refs_9_, ...), custom_call_target="tpu_custom_call" | custom-call | flops 188743680 | bytes 1966080 | tf_op jit(solution)/shard_map/pallas_call | solution.py:260
  115.6 0.0 copy-start.3
  115.6 2.1 %shard_map.60.partial_ref = f32[192,640]{1,0:T(8,128)S(1)} custom-call(s32[2]{0:T(128)S(1)} %pad_add_fusion.index_ref, bf16[1,3,64,4096]{3,2,1,0:T(8,128)(2,1)S(1)} %copy-done, f32[192,640]{1,0:T(8,128)S(1)} %shard_map.59.refs_0_, bf16[2,640,256]{2,1,0:T(8,128)(2,1)} %collective-permute-done.12.refs_1_.refs_15_, ...), custom_call_target="tpu_custom_call" | custom-call | flops 251658240 | bytes 2621440 | tf_op jit(solution)/shard_map/pallas_call | solution.py:260
  117.8 4.9 %shard_map.61 = bf16[1,3,64,4096]{3,2,1,0:T(8,128)(2,1)} custom-call(s32[2]{0:T(128)S(1)} %pad_add_fusion.index_ref, bf16[1,3,64,4096]{3,2,1,0:T(8,128)(2,1)S(1)} %copy-done, f32[192,640]{1,0:T(8,128)S(1)} %shard_map.60.partial_ref, bf16[2,640,256]{2,1,0:T(8,128)(2,1)S(1)} %bitcast.9, bf16[2,640,256]{2,1,0:T(8,128)(2,1)S(1)} %copy-done.3, ...), custom_call_target="tpu_custom_call" | custom-call | flops 1132462080 | bytes 13369344 | tf_op jit(solution)/shard_map/pallas_call | solution.py:273
  (36 shorter events, 0.1 us)
Async XLA Ops:
  0.0 107.9 %copy-start = (bf16[1,3,64,4096]{3,2,1,0:T(8,128)(2,1)S(1)}, bf16[1,3,64,4096]{3,2,1,0:T(8,128)(2,1)}, u32[]{:S(2)}) copy-start(bf16[1,3,64,4096]{3,2,1,0:T(8,128)(2,1)} %weights_ref.11) | copy-start | bytes 4718596
  32.8 14.8 %collective-permute-start = (bf16[2,640,256]{2,1,0:T(8,128)(2,1)S(1)}, bf16[2,640,256]{2,1,0:T(8,128)(2,1)S(1)}, u32[]{:S(2)}, u32[]{:S(2)}) collective-permute-start(bf16[2,640,256]{2,1,0:T(8,128)(2,1)S(1)} %bitcast.6), channel_id=1, source_target_pairs={{0,16},{16,0},{1,17},{17,1},{2,18},{18,2},{3,19},{19,3},{4,20},{20... | collective-permute-start | bytes 1966088 | tf_op jit(solution)/shard_map/ppermute | solution.py:204
  36.9 18.2 %collective-permute-start.1 = (bf16[2,640,256]{2,1,0:T(8,128)(2,1)S(1)}, bf16[2,640,256]{2,1,0:T(8,128)(2,1)S(1)}, u32[]{:S(2)}, u32[]{:S(2)}) collective-permute-start(bf16[2,640,256]{2,1,0:T(8,128)(2,1)S(1)} %bitcast.7), channel_id=1, source_target_pairs={{0,32},{16,240},{32,64},{48,16},{64,96},{80,48},{96,128},{112,80},... | collective-permute-start | bytes 1966088 | tf_op jit(solution)/shard_map/ppermute | solution.py:227
  47.6 15.3 %collective-permute-start.2 = (bf16[2,640,256]{2,1,0:T(8,128)(2,1)S(1)}, bf16[2,640,256]{2,1,0:T(8,128)(2,1)S(1)}, u32[]{:S(2)}, u32[]{:S(2)}) collective-permute-start(bf16[2,640,256]{2,1,0:T(8,128)(2,1)S(1)} %collective-permute-done.refs_1_), channel_id=1, source_target_pairs={{0,32},{16,240},{32,64},{48,16},{64,96},{80,48},{96,128},{112,80},... | collective-permute-start | bytes 1966088 | tf_op jit(solution)/shard_map/ppermute | solution.py:227
  49.8 0.8 copy-start.1
  55.1 14.8 %collective-permute-start.5 = (bf16[2,640,256]{2,1,0:T(8,128)(2,1)S(1)}, bf16[2,640,256]{2,1,0:T(8,128)(2,1)S(1)}, u32[]{:S(2)}, u32[]{:S(2)}) collective-permute-start(bf16[2,640,256]{2,1,0:T(8,128)(2,1)S(1)} %collective-permute-done.1.refs_1_.refs_2_), channel_id=1, source_target_pairs={{0,32},{16,240},{32,64},{48,16},{64,96},{80,48},{96,128},{112,80},... | collective-permute-start | bytes 1966088 | tf_op jit(solution)/shard_map/ppermute | solution.py:227
  60.1 9.8 %collective-permute-start.3 = (bf16[2,640,256]{2,1,0:T(8,128)(2,1)S(1)}, bf16[2,640,256]{2,1,0:T(8,128)(2,1)S(1)}, u32[]{:S(2)}, u32[]{:S(2)}) collective-permute-start(bf16[2,640,256]{2,1,0:T(8,128)(2,1)S(1)} %collective-permute-done.1.refs_1_.refs_2_), channel_id=1, source_target_pairs={{0,16},{16,0},{1,17},{17,1},{2,18},{18,2},{3,19},{19,3},{4,20},{20... | collective-permute-start | bytes 1966088 | tf_op jit(solution)/shard_map/ppermute | solution.py:204
  62.1 0.8 copy-start.4
  62.9 14.9 %collective-permute-start.6 = (bf16[2,640,256]{2,1,0:T(8,128)(2,1)S(1)}, bf16[2,640,256]{2,1,0:T(8,128)(2,1)S(1)}, u32[]{:S(2)}, u32[]{:S(2)}) collective-permute-start(bf16[2,640,256]{2,1,0:T(8,128)(2,1)S(1)} %collective-permute-done.2.refs_2_.refs_3_), channel_id=1, source_target_pairs={{0,32},{16,240},{32,64},{48,16},{64,96},{80,48},{96,128},{112,80},... | collective-permute-start | bytes 1966088 | tf_op jit(solution)/shard_map/ppermute | solution.py:227
  67.2 10.6 %collective-permute-start.4 = (bf16[2,640,256]{2,1,0:T(8,128)(2,1)S(1)}, bf16[2,640,256]{2,1,0:T(8,128)(2,1)S(1)}, u32[]{:S(2)}, u32[]{:S(2)}) collective-permute-start(bf16[2,640,256]{2,1,0:T(8,128)(2,1)S(1)} %collective-permute-done.2.refs_2_.refs_3_), channel_id=1, source_target_pairs={{0,16},{16,0},{1,17},{17,1},{2,18},{18,2},{3,19},{19,3},{4,20},{20... | collective-permute-start | bytes 1966088 | tf_op jit(solution)/shard_map/ppermute | solution.py:204
  69.1 0.9 copy-start.6
  70.0 0.8 copy-start.10
  70.8 13.2 %collective-permute-start.9 = (bf16[2,640,256]{2,1,0:T(8,128)(2,1)S(1)}, bf16[2,640,256]{2,1,0:T(8,128)(2,1)S(1)}, u32[]{:S(2)}, u32[]{:S(2)}) collective-permute-start(bf16[2,640,256]{2,1,0:T(8,128)(2,1)S(1)} %collective-permute-done.5.refs_1_.refs_5_), channel_id=1, source_target_pairs={{0,32},{16,240},{32,64},{48,16},{64,96},{80,48},{96,128},{112,80},... | collective-permute-start | bytes 1966088 | tf_op jit(solution)/shard_map/ppermute | solution.py:227
  75.0 9.0 %collective-permute-start.7 = (bf16[2,640,256]{2,1,0:T(8,128)(2,1)S(1)}, bf16[2,640,256]{2,1,0:T(8,128)(2,1)S(1)}, u32[]{:S(2)}, u32[]{:S(2)}) collective-permute-start(bf16[2,640,256]{2,1,0:T(8,128)(2,1)S(1)} %collective-permute-done.5.refs_1_.refs_5_), channel_id=1, source_target_pairs={{0,16},{16,0},{1,17},{17,1},{2,18},{18,2},{3,19},{19,3},{4,20},{20... | collective-permute-start | bytes 1966088 | tf_op jit(solution)/shard_map/ppermute | solution.py:204
  77.0 0.8 copy-start.8
  77.8 13.3 %copy-start.12 = (bf16[2,640,256]{2,1,0:T(8,128)(2,1)}, bf16[2,640,256]{2,1,0:T(8,128)(2,1)S(1)}, u32[]{:S(2)}) copy-start(bf16[2,640,256]{2,1,0:T(8,128)(2,1)S(1)} %collective-permute-done.6.refs_2_.refs_7_) | copy-start | bytes 1966084
  77.8 0.9 copy-start.14
  78.7 12.4 %collective-permute-start.11 = (bf16[2,640,256]{2,1,0:T(8,128)(2,1)S(1)}, bf16[2,640,256]{2,1,0:T(8,128)(2,1)S(1)}, u32[]{:S(2)}, u32[]{:S(2)}) collective-permute-start(bf16[2,640,256]{2,1,0:T(8,128)(2,1)S(1)} %collective-permute-done.6.refs_2_.refs_7_), channel_id=1, source_target_pairs={{0,32},{16,240},{32,64},{48,16},{64,96},{80,48},{96,128},{112,80},... | collective-permute-start | bytes 1966088 | tf_op jit(solution)/shard_map/ppermute | solution.py:227
  82.1 9.0 %collective-permute-start.8 = (bf16[2,640,256]{2,1,0:T(8,128)(2,1)S(1)}, bf16[2,640,256]{2,1,0:T(8,128)(2,1)S(1)}, u32[]{:S(2)}, u32[]{:S(2)}) collective-permute-start(bf16[2,640,256]{2,1,0:T(8,128)(2,1)S(1)} %collective-permute-done.6.refs_2_.refs_7_), channel_id=1, source_target_pairs={{0,16},{16,0},{1,17},{17,1},{2,18},{18,2},{3,19},{19,3},{4,20},{20... | collective-permute-start | bytes 1966088 | tf_op jit(solution)/shard_map/ppermute | solution.py:204
  84.0 0.8 copy-start.16
  84.9 28.9 %collective-permute-start.10 = (bf16[2,640,256]{2,1,0:T(8,128)(2,1)S(1)}, bf16[2,640,256]{2,1,0:T(8,128)(2,1)}, u32[]{:S(2)}, u32[]{:S(2)}) collective-permute-start(bf16[2,640,256]{2,1,0:T(8,128)(2,1)S(1)} %collective-permute-done.9.refs_1_.refs_9_), channel_id=1, source_target_pairs={{0,16},{16,0},{1,17},{17,1},{2,18},{18,2},{3,19},{19,3},{4,20},{20... | collective-permute-start | bytes 1966088 | tf_op jit(solution)/shard_map/ppermute | solution.py:204
  87.8 10.2 %collective-permute-start.13 = (bf16[1,640,256]{2,1,0:T(8,128)(2,1)S(1)}, bf16[1,640,256]{2,1,0:T(8,128)(2,1)}, u32[]{:S(2)}, u32[]{:S(2)}) collective-permute-start(bf16[1,640,256]{2,1,0:T(8,128)(2,1)S(1)} %get-tuple-element.22), channel_id=1, source_target_pairs={{0,32},{16,240},{32,64},{48,16},{64,96},{80,48},{96,128},{112,80},... | collective-permute-start | bytes 983048 | tf_op jit(solution)/shard_map/ppermute | solution.py:232
  91.1 0.8 copy-start.18
  91.9 23.7 %collective-permute-start.12 = (bf16[2,640,256]{2,1,0:T(8,128)(2,1)S(1)}, bf16[2,640,256]{2,1,0:T(8,128)(2,1)}, u32[]{:S(2)}, u32[]{:S(2)}) collective-permute-start(bf16[2,640,256]{2,1,0:T(8,128)(2,1)S(1)} %collective-permute-done.11.refs_3_.refs_11_), channel_id=1, source_target_pairs={{0,16},{16,0},{1,17},{17,1},{2,18},{18,2},{3,19},{19,3},{4,20},{20... | collective-permute-start | bytes 1966088 | tf_op jit(solution)/shard_map/ppermute | solution.py:204
  95.6 8.2 %collective-permute-start.14 = (bf16[1,640,256]{2,1,0:T(8,128)(2,1)S(1)}, bf16[1,640,256]{2,1,0:T(8,128)(2,1)}, u32[]{:S(2)}, u32[]{:S(2)}) collective-permute-start(bf16[1,640,256]{2,1,0:T(8,128)(2,1)S(1)} %get-tuple-element.21), channel_id=1, source_target_pairs={{0,32},{16,240},{32,64},{48,16},{64,96},{80,48},{96,128},{112,80},... | collective-permute-start | bytes 983048 | tf_op jit(solution)/shard_map/ppermute | solution.py:232
  98.0 17.6 %collective-permute-start.15 = (bf16[1,640,256]{2,1,0:T(8,128)(2,1)}, bf16[1,640,256]{2,1,0:T(8,128)(2,1)}, u32[]{:S(2)}, u32[]{:S(2)}) collective-permute-start(bf16[1,640,256]{2,1,0:T(8,128)(2,1)} %collective-permute-done.13.refs_2_.refs_12_), channel_id=1, source_target_pairs={{0,16},{16,0},{1,17},{17,1},{2,18},{18,2},{3,19},{19,3},{4,20},{20... | collective-permute-start | bytes 983048 | tf_op jit(solution)/shard_map/ppermute | solution.py:204
  103.8 13.9 %collective-permute-start.16 = (bf16[1,640,256]{2,1,0:T(8,128)(2,1)}, bf16[1,640,256]{2,1,0:T(8,128)(2,1)}, u32[]{:S(2)}, u32[]{:S(2)}) collective-permute-start(bf16[1,640,256]{2,1,0:T(8,128)(2,1)} %collective-permute-done.14.refs_3_.refs_13_), channel_id=1, source_target_pairs={{0,16},{16,0},{1,17},{17,1},{2,18},{18,2},{3,19},{19,3},{4,20},{20... | collective-permute-start | bytes 983048 | tf_op jit(solution)/shard_map/ppermute | solution.py:204
  107.9 1.1 copy-start.2
  109.0 1.1 copy-start.5
  109.0 1.3 %copy-start.7 = (bf16[2,640,256]{2,1,0:T(8,128)(2,1)S(1)}, bf16[2,640,256]{2,1,0:T(8,128)(2,1)}, u32[]{:S(2)}) copy-start(bf16[2,640,256]{2,1,0:T(8,128)(2,1)} %copy-done.6) | copy-start | bytes 1966084
  109.0 1.5 %copy-start.11 = (bf16[2,640,256]{2,1,0:T(8,128)(2,1)S(1)}, bf16[2,640,256]{2,1,0:T(8,128)(2,1)}, u32[]{:S(2)}) copy-start(bf16[2,640,256]{2,1,0:T(8,128)(2,1)} %copy-done.10) | copy-start | bytes 1966084
  109.0 1.7 %copy-start.15 = (bf16[2,640,256]{2,1,0:T(8,128)(2,1)S(1)}, bf16[2,640,256]{2,1,0:T(8,128)(2,1)}, u32[]{:S(2)}) copy-start(bf16[2,640,256]{2,1,0:T(8,128)(2,1)} %copy-done.14) | copy-start | bytes 1966084
  110.7 1.5 %copy-start.9 = (bf16[2,640,256]{2,1,0:T(8,128)(2,1)S(1)}, bf16[2,640,256]{2,1,0:T(8,128)(2,1)}, u32[]{:S(2)}) copy-start(bf16[2,640,256]{2,1,0:T(8,128)(2,1)} %copy-done.8) | copy-start | bytes 1966084
  110.7 1.5 %copy-start.13 = (bf16[2,640,256]{2,1,0:T(8,128)(2,1)S(1)}, bf16[2,640,256]{2,1,0:T(8,128)(2,1)}, u32[]{:S(2)}) copy-start(bf16[2,640,256]{2,1,0:T(8,128)(2,1)} %copy-done.12) | copy-start | bytes 1966084
  110.7 1.5 %copy-start.17 = (bf16[2,640,256]{2,1,0:T(8,128)(2,1)S(1)}, bf16[2,640,256]{2,1,0:T(8,128)(2,1)}, u32[]{:S(2)}) copy-start(bf16[2,640,256]{2,1,0:T(8,128)(2,1)} %copy-done.16) | copy-start | bytes 1966084
  110.7 1.7 %copy-start.19 = (bf16[2,640,256]{2,1,0:T(8,128)(2,1)S(1)}, bf16[2,640,256]{2,1,0:T(8,128)(2,1)}, u32[]{:S(2)}) copy-start(bf16[2,640,256]{2,1,0:T(8,128)(2,1)} %copy-done.18) | copy-start | bytes 1966084
  115.6 2.1 %copy-start.3 = (bf16[2,640,256]{2,1,0:T(8,128)(2,1)S(1)}, bf16[2,640,256]{2,1,0:T(8,128)(2,1)}, u32[]{:S(2)}) copy-start(bf16[2,640,256]{2,1,0:T(8,128)(2,1)} %copy-done.1) | copy-start | bytes 1966084

commit v6 on v4

--- a/solution.py
+++ b/solution.py
@@ -13,7 +13,7 @@
 F32 = jnp.float32
 EARLY_VMEM = 8 << 20
 GRADS_VMEM = 16 << 20
-FORWARD_GROUP = 4
+FORWARD_GROUP = 2
 GRADS_GROUP = 2
 
 
@@ -83,11 +83,11 @@
         )
 
     pair = jnp.concatenate([weight_block(0), weight_block(1)], axis=0)
-    total[:, : 2 * hidden_units] += lax.dot_general(
-        joined(pieces, 0), pair, along, preferred_element_type=F32
-    )
-    total[:, 2 * hidden_units :] += lax.dot_general(
-        joined(pieces, 1), weight_block(2), along, preferred_element_type=F32
+    total[: 2 * hidden_units] += lax.dot_general(
+        pair, joined(pieces, 0), along, preferred_element_type=F32
+    )
+    total[2 * hidden_units :] += lax.dot_general(
+        weight_block(2), joined(pieces, 1), along, preferred_element_type=F32
     )
 
 
@@ -103,32 +103,40 @@
         )
 
 
-def grads_kernel(ring_size, blocks, late, index_ref, weights_ref, partial_ref, *refs):
+def grads_kernel(ring_size, blocks, late, moved, index_ref, weights_ref, partial_ref, *refs):
     count = len(blocks)
-    sources, out_ref = refs[:count], refs[count]
-    total, out_buf, sems = refs[count + 1 :]
+    sources, out_ref = list(refs[:count]), refs[count]
+    total, out_buf, sems, moved_buf, moved_sems = refs[count + 1 :]
+    loads = []
+    for n, block in enumerate(moved):
+        k = blocks.index(block)
+        load = pltpu.make_async_copy(sources[k], moved_buf.at[n], moved_sems.at[n])
+        load.start()
+        loads.append(load)
+        sources[k] = moved_buf.at[n]
     halves, half = sources[0].shape[0], sources[0].shape[2] // 2
     hidden_units = weights_ref.shape[2]
     last = [blocks.index(block) for block in late]
     total[...] = partial_ref[...]
     add_forward(ring_size, index_ref, weights_ref, total, [sources[k] for k in last], late)
-    gate_part = total[:, :hidden_units]
-    up_part = total[:, hidden_units : 2 * hidden_units]
-    back_hidden = total[:, 2 * hidden_units :]
+    for load in loads:
+        load.wait()
+    gate_part = total[:hidden_units]
+    up_part = total[hidden_units : 2 * hidden_units]
+    back_hidden = total[2 * hidden_units :]
     sigmoid_part = jax.nn.sigmoid(gate_part)
     silu = gate_part * sigmoid_part
     hidden = (silu * up_part).astype(BF16)
     derivative = sigmoid_part * (1.0 + gate_part * (1.0 - sigmoid_part))
     pre_gate = (back_hidden * up_part * derivative).astype(BF16)
     pre_up = (back_hidden * silu).astype(BF16)
-    both = jnp.concatenate([pre_gate, pre_up], axis=1).T
-    hidden_t = hidden.T
+    both = jnp.concatenate([pre_gate, pre_up], axis=0)
     copies = []
     for n in range(0, count, GRADS_GROUP):
         chosen = range(n, min(n + GRADS_GROUP, count))
         pieces = [sources[k] for k in chosen]
         ins = jnp.dot(both, joined(pieces, 0), preferred_element_type=F32).astype(BF16)
-        outs = jnp.dot(hidden_t, joined(pieces, 1), preferred_element_type=F32).astype(BF16)
+        outs = jnp.dot(hidden, joined(pieces, 1), preferred_element_type=F32).astype(BF16)
         for m, k in enumerate(chosen):
             for j in range(halves):
                 cut = slice((m * halves + j) * half, (m * halves + j + 1) * half)
@@ -202,7 +210,8 @@
         "early_4": [(far - 1, 1, 1), (far, 0, 0)],
     }
     late = [(far, 0, 1)]
-    sums = jax.ShapeDtypeStruct((slots, 3 * hidden_units), F32)
+    from_hbm = [(1, 1, 0), (1, 0, 1), (2, 0, 0)]
+    sums = jax.ShapeDtypeStruct((3 * hidden_units, slots), F32)
 
     partials = []
     for chosen in early.values():
@@ -222,14 +231,17 @@
             )(index, expert_weights, *partials, *[raw.get(k, held[k]) for k in chosen])
         ]
     return pl.pallas_call(
-        functools.partial(grads_kernel, ring_size, blocks, late),
+        functools.partial(grads_kernel, ring_size, blocks, late, from_hbm),
         out_shape=jax.ShapeDtypeStruct(expert_weights.shape, BF16),
-        in_specs=[smem_spec, vmem_spec, vmem_spec] + [vmem_spec] * len(blocks),
+        in_specs=[smem_spec, vmem_spec, vmem_spec]
+        + [pl.BlockSpec(memory_space=pl.ANY) if k in from_hbm else vmem_spec for k in blocks],
         out_specs=pl.BlockSpec(memory_space=pl.ANY),
         scratch_shapes=[
             pltpu.VMEM(sums.shape, F32),
             pltpu.VMEM((len(blocks), 2, 3, hidden_units, width), BF16),
             pltpu.SemaphoreType.DMA((len(blocks), 2)),
+            pltpu.VMEM((len(from_hbm), 2, slots, 2 * width), BF16),
+            pltpu.SemaphoreType.DMA((len(from_hbm),)),
         ],
         cost_estimate=pl.CostEstimate(
             flops=len(blocks) * block_flops,

time: 118 us -> 118 us (level)
  no operation moved by 1% of the time
where the time goes in v6:
time: 118 us; the launch traced here: 117 us
  starting transfers between devices  55 us (47%)
  blocking collectives  30.5 us (26%)
  Pallas kernels  14.8 us (13%)
  local copies, waits for them, and re-layouts  10.3 us (9%)
  waiting for transfers between devices  6.32 us (5%)
    ppermute x7, starting transfers between devices, device_step(): piece = lax.ppermute(held[step - 1, chain, 0], ('ring', 'core'), around)  33.6 us
    all_to_all x1, blocking collectives, device_step(): lax.all_to_all(send.reshape(2 * groups, CAP, 2 * width), ('half', 'expert...  30.5 us
    ppermute x8, starting transfers between devices, swapped(): return lax.ppermute(x, 'core', [(0, 1), (1, 0)])  21.5 us
    unnamed x44, local copies, waits for them, and re-layouts  10.3 us
    pallas_call x5, Pallas kernels, device_step(): pl.pallas_call(functools.partial(forward_kernel, ring_size, chosen, chain...  7.08 us
    ppermute x7, waiting for transfers between devices, device_step(): piece = lax.ppermute(held[step - 1, chain, 0], ('ring', 'core'), around)  6.3 us
    pallas_call x1, Pallas kernels, device_step(): pl.pallas_call(functools.partial(grads_kernel, ring_size, blocks, late, f...  5.5 us
  transfers between devices with their start and end apart: 15, of which 2 were waited for; matrix products, arithmetic and copies ran while one was open for 0% of the time, Pallas kernels for 6%

profile of v6, /device:TPU:1, one launch (start us, length us, event | category | flops | bytes accessed | tf_op | source)
XLA Modules:
  0.0 117.4 jit_solution(10068179079833221615)
XLA Ops:
  0.0 2.2 %shard_map.55 = bf16[2,640,256]{2,1,0:T(8,128)(2,1)} custom-call(s32[2,128]{1,0:T(2,128)} %bitcast.11, f32[2,128]{1,0:T(2,128)} %bitcast.12, bf16[128,128]{1,0:T(8,128)(2,1)} %tokens_ref.1, bf16[128,128]{1,0:T(8,128)(2,1)} %cotangent_ref.1), custom_call_target="tpu_custom_call" | custom-call | tf_op jit(solution)/shard_map/pallas_call | solution.py:161
  2.2 30.5 %all_to_all.5 = bf16[32,40,256]{2,1,0:T(8,128)(2,1)S(1)} all-to-all(bf16[32,40,256]{2,1,0:T(8,128)(2,1)} %bitcast.10), channel_id=1, replica_groups=mesh['half'=2,'ring'=8,'core'=2,'expert'=16] {'half','expert'}, dimensions={0} | all-to-all | bytes 1310720 | tf_op jit(solution)/shard_map/all_to_all | solution.py:174
  32.8 4.2 %collective-permute-start = (bf16[2,640,256]{2,1,0:T(8,128)(2,1)S(1)}, bf16[2,640,256]{2,1,0:T(8,128)(2,1)S(1)}, u32[]{:S(2)}, u32[]{:S(2)}) collective-permute-start(bf16[2,640,256]{2,1,0:T(8,128)(2,1)S(1)} %bitcast.6), channel_id=1, source_target_pairs={{0,16},{16,0},{1,17},{17,1},{2,18},{18,2},{3,19},{19,3},{4,20},{20... | collective-permute-start | bytes 1966088 | tf_op jit(solution)/shard_map/ppermute | solution.py:172
  36.9 10.7 %collective-permute-start.1 = (bf16[2,640,256]{2,1,0:T(8,128)(2,1)S(1)}, bf16[2,640,256]{2,1,0:T(8,128)(2,1)S(1)}, u32[]{:S(2)}, u32[]{:S(2)}) collective-permute-start(bf16[2,640,256]{2,1,0:T(8,128)(2,1)S(1)} %bitcast.7), channel_id=1, source_target_pairs={{0,32},{16,240},{32,64},{48,16},{64,96},{80,48},{96,128},{112,80},... | collective-permute-start | bytes 1966088 | tf_op jit(solution)/shard_map/ppermute | solution.py:186
  47.6 0.0 collective-permute-done.refs_1_
  47.6 2.2 %collective-permute-start.2 = (bf16[2,640,256]{2,1,0:T(8,128)(2,1)S(1)}, bf16[2,640,256]{2,1,0:T(8,128)(2,1)S(1)}, u32[]{:S(2)}, u32[]{:S(2)}) collective-permute-start(bf16[2,640,256]{2,1,0:T(8,128)(2,1)S(1)} %collective-permute-done.refs_1_), channel_id=1, source_target_pairs={{0,32},{16,240},{32,64},{48,16},{64,96},{80,48},{96,128},{112,80},... | collective-permute-start | bytes 1966088 | tf_op jit(solution)/shard_map/ppermute | solution.py:186
  49.8 0.0 copy-start.3
  49.8 0.8 copy-done.3
  50.6 4.5 %collective-permute-done.1.refs_1_.refs_2_ = bf16[2,640,256]{2,1,0:T(8,128)(2,1)S(1)} collective-permute-done((bf16[2,640,256]{2,1,0:T(8,128)(2,1)S(1)}, bf16[2,640,256]{2,1,0:T(8,128)(2,1)S(1)}, u32[]{:S(2)}, u32[]{:S(2)}) %collective-permute-start.1) | collective-permute-done | bytes 655392 | tf_op jit(solution)/shard_map/ppermute | solution.py:186
  55.1 5.0 %collective-permute-start.5 = (bf16[2,640,256]{2,1,0:T(8,128)(2,1)S(1)}, bf16[2,640,256]{2,1,0:T(8,128)(2,1)S(1)}, u32[]{:S(2)}, u32[]{:S(2)}) collective-permute-start(bf16[2,640,256]{2,1,0:T(8,128)(2,1)S(1)} %collective-permute-done.1.refs_1_.refs_2_), channel_id=1, source_target_pairs={{0,32},{16,240},{32,64},{48,16},{64,96},{80,48},{96,128},{112,80},... | collective-permute-start | bytes 1966088 | tf_op jit(solution)/shard_map/ppermute | solution.py:186
  60.1 1.9 %collective-permute-start.3 = (bf16[2,640,256]{2,1,0:T(8,128)(2,1)S(1)}, bf16[2,640,256]{2,1,0:T(8,128)(2,1)S(1)}, u32[]{:S(2)}, u32[]{:S(2)}) collective-permute-start(bf16[2,640,256]{2,1,0:T(8,128)(2,1)S(1)} %collective-permute-done.1.refs_1_.refs_2_), channel_id=1, source_target_pairs={{0,16},{16,0},{1,17},{17,1},{2,18},{18,2},{3,19},{19,3},{4,20},{20... | collective-permute-start | bytes 1966088 | tf_op jit(solution)/shard_map/ppermute | solution.py:172
  62.1 0.8 copy-done.6
  62.9 0.0 collective-permute-done.2.refs_2_.refs_3_
  62.9 4.2 %collective-permute-start.6 = (bf16[2,640,256]{2,1,0:T(8,128)(2,1)S(1)}, bf16[2,640,256]{2,1,0:T(8,128)(2,1)S(1)}, u32[]{:S(2)}, u32[]{:S(2)}) collective-permute-start(bf16[2,640,256]{2,1,0:T(8,128)(2,1)S(1)} %collective-permute-done.2.refs_2_.refs_3_), channel_id=1, source_target_pairs={{0,32},{16,240},{32,64},{48,16},{64,96},{80,48},{96,128},{112,80},... | collective-permute-start | bytes 1966088 | tf_op jit(solution)/shard_map/ppermute | solution.py:186
  67.1 1.9 %collective-permute-start.4 = (bf16[2,640,256]{2,1,0:T(8,128)(2,1)S(1)}, bf16[2,640,256]{2,1,0:T(8,128)(2,1)S(1)}, u32[]{:S(2)}, u32[]{:S(2)}) collective-permute-start(bf16[2,640,256]{2,1,0:T(8,128)(2,1)S(1)} %collective-permute-done.2.refs_2_.refs_3_), channel_id=1, source_target_pairs={{0,16},{16,0},{1,17},{17,1},{2,18},{18,2},{3,19},{19,3},{4,20},{20... | collective-permute-start | bytes 1966088 | tf_op jit(solution)/shard_map/ppermute | solution.py:172
  69.1 0.8 copy-done.8
  69.9 0.8 copy-done.12
  70.8 4.2 %collective-permute-start.9 = (bf16[2,640,256]{2,1,0:T(8,128)(2,1)S(1)}, bf16[2,640,256]{2,1,0:T(8,128)(2,1)S(1)}, u32[]{:S(2)}, u32[]{:S(2)}) collective-permute-start(bf16[2,640,256]{2,1,0:T(8,128)(2,1)S(1)} %collective-permute-done.5.refs_1_.refs_5_), channel_id=1, source_target_pairs={{0,32},{16,240},{32,64},{48,16},{64,96},{80,48},{96,128},{112,80},... | collective-permute-start | bytes 1966088 | tf_op jit(solution)/shard_map/ppermute | solution.py:186
  75.0 1.9 %collective-permute-start.7 = (bf16[2,640,256]{2,1,0:T(8,128)(2,1)S(1)}, bf16[2,640,256]{2,1,0:T(8,128)(2,1)S(1)}, u32[]{:S(2)}, u32[]{:S(2)}) collective-permute-start(bf16[2,640,256]{2,1,0:T(8,128)(2,1)S(1)} %collective-permute-done.5.refs_1_.refs_5_), channel_id=1, source_target_pairs={{0,16},{16,0},{1,17},{17,1},{2,18},{18,2},{3,19},{19,3},{4,20},{20... | collective-permute-start | bytes 1966088 | tf_op jit(solution)/shard_map/ppermute | solution.py:172
  76.9 0.9 copy-done.10
  77.8 0.0 collective-permute-done.6.refs_2_.refs_7_
  77.8 0.8 copy-done.16
  78.7 3.4 %collective-permute-start.11 = (bf16[2,640,256]{2,1,0:T(8,128)(2,1)S(1)}, bf16[2,640,256]{2,1,0:T(8,128)(2,1)S(1)}, u32[]{:S(2)}, u32[]{:S(2)}) collective-permute-start(bf16[2,640,256]{2,1,0:T(8,128)(2,1)S(1)} %collective-permute-done.6.refs_2_.refs_7_), channel_id=1, source_target_pairs={{0,32},{16,240},{32,64},{48,16},{64,96},{80,48},{96,128},{112,80},... | collective-permute-start | bytes 1966088 | tf_op jit(solution)/shard_map/ppermute | solution.py:186
  82.0 1.9 %collective-permute-start.8 = (bf16[2,640,256]{2,1,0:T(8,128)(2,1)S(1)}, bf16[2,640,256]{2,1,0:T(8,128)(2,1)S(1)}, u32[]{:S(2)}, u32[]{:S(2)}) collective-permute-start(bf16[2,640,256]{2,1,0:T(8,128)(2,1)S(1)} %collective-permute-done.6.refs_2_.refs_7_), channel_id=1, source_target_pairs={{0,16},{16,0},{1,17},{17,1},{2,18},{18,2},{3,19},{19,3},{4,20},{20... | collective-permute-start | bytes 1966088 | tf_op jit(solution)/shard_map/ppermute | solution.py:172
  84.0 0.8 copy-done.14
  84.8 0.8 copy-done.18
  85.7 3.9 %collective-permute-start.13 = (bf16[2,640,256]{2,1,0:T(8,128)(2,1)S(1)}, bf16[2,640,256]{2,1,0:T(8,128)(2,1)}, u32[]{:S(2)}, u32[]{:S(2)}) collective-permute-start(bf16[2,640,256]{2,1,0:T(8,128)(2,1)S(1)} %collective-permute-done.9.refs_1_.refs_9_), channel_id=1, source_target_pairs={{0,32},{16,240},{32,64},{48,16},{64,96},{80,48},{96,128},{112,80},... | collective-permute-start | bytes 1966088 | tf_op jit(solution)/shard_map/ppermute | solution.py:186
  89.5 1.9 %collective-permute-start.10 = (bf16[2,640,256]{2,1,0:T(8,128)(2,1)S(1)}, bf16[2,640,256]{2,1,0:T(8,128)(2,1)S(1)}, u32[]{:S(2)}, u32[]{:S(2)}) collective-permute-start(bf16[2,640,256]{2,1,0:T(8,128)(2,1)S(1)} %collective-permute-done.9.refs_1_.refs_9_), channel_id=1, source_target_pairs={{0,16},{16,0},{1,17},{17,1},{2,18},{18,2},{3,19},{19,3},{4,20},{20... | collective-permute-start | bytes 1966088 | tf_op jit(solution)/shard_map/ppermute | solution.py:172
  91.5 0.0 collective-permute-done.11.refs_3_.refs_11_
  91.5 0.8 copy-done.20
  92.3 3.2 %collective-permute-start.12 = (bf16[2,640,256]{2,1,0:T(8,128)(2,1)S(1)}, bf16[2,640,256]{2,1,0:T(8,128)(2,1)}, u32[]{:S(2)}, u32[]{:S(2)}) collective-permute-start(bf16[2,640,256]{2,1,0:T(8,128)(2,1)S(1)} %collective-permute-done.11.refs_3_.refs_11_), channel_id=1, source_target_pairs={{0,16},{16,0},{1,17},{17,1},{2,18},{18,2},{3,19},{19,3},{4,20},{20... | collective-permute-start | bytes 1966088 | tf_op jit(solution)/shard_map/ppermute | solution.py:172
  95.6 1.8 %collective-permute-done.13.refs_2_.refs_13_ = bf16[2,640,256]{2,1,0:T(8,128)(2,1)} collective-permute-done((bf16[2,640,256]{2,1,0:T(8,128)(2,1)S(1)}, bf16[2,640,256]{2,1,0:T(8,128)(2,1)}, u32[]{:S(2)}, u32[]{:S(2)}) %collective-permute-start.13) | collective-permute-done | bytes 655392 | tf_op jit(solution)/shard_map/ppermute | solution.py:186
  97.4 0.9 copy-done.1
  98.3 4.5 %collective-permute-start.14 = (bf16[2,640,256]{2,1,0:T(8,128)(2,1)}, bf16[2,640,256]{2,1,0:T(8,128)(2,1)}, u32[]{:S(2)}, u32[]{:S(2)}) collective-permute-start(bf16[2,640,256]{2,1,0:T(8,128)(2,1)} %collective-permute-done.13.refs_2_.refs_13_), channel_id=1, source_target_pairs={{0,16},{16,0},{1,17},{17,1},{2,18},{18,2},{3,19},{19,3},{4,20},{20... | collective-permute-start | bytes 1966088 | tf_op jit(solution)/shard_map/ppermute | solution.py:172
  102.8 0.1 pad_add_fusion.index_ref
  102.8 1.1 copy-done.4
  103.9 1.1 shard_map.56.refs_0_
  105.0 0.0 copy-done.7
  105.0 0.2 copy-done.9
  105.2 0.2 copy-done.13
  105.4 0.2 copy-done.17
  105.6 1.5 %shard_map.57.refs_0_ = f32[192,640]{1,0:T(8,128)S(1)} custom-call(s32[2]{0:T(128)S(1)} %pad_add_fusion.index_ref, bf16[1,3,64,4096]{3,2,1,0:T(8,128)(2,1)S(1)} %copy-done, f32[192,640]{1,0:T(8,128)S(1)} %shard_map.56.refs_0_, bf16[2,640,256]{2,1,0:T(8,128)(2,1)S(1)} %copy-done.7, bf16[2,640,256]{2,1,0:T(8,128)(2,1)S(1)} %copy-done.9, ...), custom_call_target="tpu_custom_call" | custom-call | flops 251658240 | bytes 2621440 | tf_op jit(solution)/shard_map/pallas_call | solution.py:220
  107.1 0.2 copy-done.21
  107.3 1.4 %shard_map.58.refs_0_ = f32[192,640]{1,0:T(8,128)S(1)} custom-call(s32[2]{0:T(128)S(1)} %pad_add_fusion.index_ref, bf16[1,3,64,4096]{3,2,1,0:T(8,128)(2,1)S(1)} %copy-done, f32[192,640]{1,0:T(8,128)S(1)} %shard_map.57.refs_0_, bf16[2,640,256]{2,1,0:T(8,128)(2,1)S(1)} %copy-done.11, bf16[2,640,256]{2,1,0:T(8,128)(2,1)S(1)} %copy-done.15, ...), custom_call_target="tpu_custom_call" | custom-call | flops 251658240 | bytes 2621440 | tf_op jit(solution)/shard_map/pallas_call | solution.py:220
  108.7 1.2 %shard_map.59.refs_0_ = f32[192,640]{1,0:T(8,128)S(1)} custom-call(s32[2]{0:T(128)S(1)} %pad_add_fusion.index_ref, bf16[1,3,64,4096]{3,2,1,0:T(8,128)(2,1)S(1)} %copy-done, f32[192,640]{1,0:T(8,128)S(1)} %shard_map.58.refs_0_, bf16[2,640,256]{2,1,0:T(8,128)(2,1)S(1)} %collective-permute-done.9.refs_1_.refs_9_, bf16[2,640,256]{2,1,0:T(8,128)(2,1)S(1)} %copy-done.2, ...), custom_call_target="tpu_custom_call" | custom-call | flops 188743680 | bytes 1966080 | tf_op jit(solution)/shard_map/pallas_call | solution.py:220
  110.0 0.0 copy-start.5
  110.0 1.9 %shard_map.60.partial_ref = f32[192,640]{1,0:T(8,128)S(1)} custom-call(s32[2]{0:T(128)S(1)} %pad_add_fusion.index_ref, bf16[1,3,64,4096]{3,2,1,0:T(8,128)(2,1)S(1)} %copy-done, f32[192,640]{1,0:T(8,128)S(1)} %shard_map.59.refs_0_, bf16[2,640,256]{2,1,0:T(8,128)(2,1)} %collective-permute-done.12.refs_1_.refs_14_, ...), custom_call_target="tpu_custom_call" | custom-call | flops 125829120 | bytes 1310720 | tf_op jit(solution)/shard_map/pallas_call | solution.py:220
  111.9 5.5 %shard_map.61 = bf16[1,3,64,4096]{3,2,1,0:T(8,128)(2,1)} custom-call(s32[2]{0:T(128)S(1)} %pad_add_fusion.index_ref, bf16[1,3,64,4096]{3,2,1,0:T(8,128)(2,1)S(1)} %copy-done, f32[192,640]{1,0:T(8,128)S(1)} %shard_map.60.partial_ref, bf16[2,640,256]{2,1,0:T(8,128)(2,1)S(1)} %bitcast.9, bf16[2,640,256]{2,1,0:T(8,128)(2,1)S(1)} %copy-done.5, ...), custom_call_target="tpu_custom_call" | custom-call | flops 1006632960 | bytes 12058624 | tf_op jit(solution)/shard_map/pallas_call | solution.py:233
  (35 shorter events, 0.1 us)
Async XLA Ops:
  0.0 102.8 %copy-start = (bf16[1,3,64,4096]{3,2,1,0:T(8,128)(2,1)S(1)}, bf16[1,3,64,4096]{3,2,1,0:T(8,128)(2,1)}, u32[]{:S(2)}) copy-start(bf16[1,3,64,4096]{3,2,1,0:T(8,128)(2,1)} %weights_ref.11) | copy-start | bytes 4718596
  32.8 14.8 %collective-permute-start = (bf16[2,640,256]{2,1,0:T(8,128)(2,1)S(1)}, bf16[2,640,256]{2,1,0:T(8,128)(2,1)S(1)}, u32[]{:S(2)}, u32[]{:S(2)}) collective-permute-start(bf16[2,640,256]{2,1,0:T(8,128)(2,1)S(1)} %bitcast.6), channel_id=1, source_target_pairs={{0,16},{16,0},{1,17},{17,1},{2,18},{18,2},{3,19},{19,3},{4,20},{20... | collective-permute-start | bytes 1966088 | tf_op jit(solution)/shard_map/ppermute | solution.py:172
  36.9 18.2 %collective-permute-start.1 = (bf16[2,640,256]{2,1,0:T(8,128)(2,1)S(1)}, bf16[2,640,256]{2,1,0:T(8,128)(2,1)S(1)}, u32[]{:S(2)}, u32[]{:S(2)}) collective-permute-start(bf16[2,640,256]{2,1,0:T(8,128)(2,1)S(1)} %bitcast.7), channel_id=1, source_target_pairs={{0,32},{16,240},{32,64},{48,16},{64,96},{80,48},{96,128},{112,80},... | collective-permute-start | bytes 1966088 | tf_op jit(solution)/shard_map/ppermute | solution.py:186
  47.6 15.3 %collective-permute-start.2 = (bf16[2,640,256]{2,1,0:T(8,128)(2,1)S(1)}, bf16[2,640,256]{2,1,0:T(8,128)(2,1)S(1)}, u32[]{:S(2)}, u32[]{:S(2)}) collective-permute-start(bf16[2,640,256]{2,1,0:T(8,128)(2,1)S(1)} %collective-permute-done.refs_1_), channel_id=1, source_target_pairs={{0,32},{16,240},{32,64},{48,16},{64,96},{80,48},{96,128},{112,80},... | collective-permute-start | bytes 1966088 | tf_op jit(solution)/shard_map/ppermute | solution.py:186
  49.8 0.8 copy-start.3
  55.1 14.8 %collective-permute-start.5 = (bf16[2,640,256]{2,1,0:T(8,128)(2,1)S(1)}, bf16[2,640,256]{2,1,0:T(8,128)(2,1)S(1)}, u32[]{:S(2)}, u32[]{:S(2)}) collective-permute-start(bf16[2,640,256]{2,1,0:T(8,128)(2,1)S(1)} %collective-permute-done.1.refs_1_.refs_2_), channel_id=1, source_target_pairs={{0,32},{16,240},{32,64},{48,16},{64,96},{80,48},{96,128},{112,80},... | collective-permute-start | bytes 1966088 | tf_op jit(solution)/shard_map/ppermute | solution.py:186
  60.1 9.8 %collective-permute-start.3 = (bf16[2,640,256]{2,1,0:T(8,128)(2,1)S(1)}, bf16[2,640,256]{2,1,0:T(8,128)(2,1)S(1)}, u32[]{:S(2)}, u32[]{:S(2)}) collective-permute-start(bf16[2,640,256]{2,1,0:T(8,128)(2,1)S(1)} %collective-permute-done.1.refs_1_.refs_2_), channel_id=1, source_target_pairs={{0,16},{16,0},{1,17},{17,1},{2,18},{18,2},{3,19},{19,3},{4,20},{20... | collective-permute-start | bytes 1966088 | tf_op jit(solution)/shard_map/ppermute | solution.py:172
  62.1 0.8 copy-start.6
  62.9 14.9 %collective-permute-start.6 = (bf16[2,640,256]{2,1,0:T(8,128)(2,1)S(1)}, bf16[2,640,256]{2,1,0:T(8,128)(2,1)S(1)}, u32[]{:S(2)}, u32[]{:S(2)}) collective-permute-start(bf16[2,640,256]{2,1,0:T(8,128)(2,1)S(1)} %collective-permute-done.2.refs_2_.refs_3_), channel_id=1, source_target_pairs={{0,32},{16,240},{32,64},{48,16},{64,96},{80,48},{96,128},{112,80},... | collective-permute-start | bytes 1966088 | tf_op jit(solution)/shard_map/ppermute | solution.py:186
  67.1 10.7 %collective-permute-start.4 = (bf16[2,640,256]{2,1,0:T(8,128)(2,1)S(1)}, bf16[2,640,256]{2,1,0:T(8,128)(2,1)S(1)}, u32[]{:S(2)}, u32[]{:S(2)}) collective-permute-start(bf16[2,640,256]{2,1,0:T(8,128)(2,1)S(1)} %collective-permute-done.2.refs_2_.refs_3_), channel_id=1, source_target_pairs={{0,16},{16,0},{1,17},{17,1},{2,18},{18,2},{3,19},{19,3},{4,20},{20... | collective-permute-start | bytes 1966088 | tf_op jit(solution)/shard_map/ppermute | solution.py:172
  69.1 0.9 copy-start.8
  69.9 0.8 copy-start.12
  70.8 14.0 %collective-permute-start.9 = (bf16[2,640,256]{2,1,0:T(8,128)(2,1)S(1)}, bf16[2,640,256]{2,1,0:T(8,128)(2,1)S(1)}, u32[]{:S(2)}, u32[]{:S(2)}) collective-permute-start(bf16[2,640,256]{2,1,0:T(8,128)(2,1)S(1)} %collective-permute-done.5.refs_1_.refs_5_), channel_id=1, source_target_pairs={{0,32},{16,240},{32,64},{48,16},{64,96},{80,48},{96,128},{112,80},... | collective-permute-start | bytes 1966088 | tf_op jit(solution)/shard_map/ppermute | solution.py:186
  75.0 9.8 %collective-permute-start.7 = (bf16[2,640,256]{2,1,0:T(8,128)(2,1)S(1)}, bf16[2,640,256]{2,1,0:T(8,128)(2,1)S(1)}, u32[]{:S(2)}, u32[]{:S(2)}) collective-permute-start(bf16[2,640,256]{2,1,0:T(8,128)(2,1)S(1)} %collective-permute-done.5.refs_1_.refs_5_), channel_id=1, source_target_pairs={{0,16},{16,0},{1,17},{17,1},{2,18},{18,2},{3,19},{19,3},{4,20},{20... | collective-permute-start | bytes 1966088 | tf_op jit(solution)/shard_map/ppermute | solution.py:172
  76.9 0.9 copy-start.10
  77.8 0.8 copy-start.16
  78.7 12.8 %collective-permute-start.11 = (bf16[2,640,256]{2,1,0:T(8,128)(2,1)S(1)}, bf16[2,640,256]{2,1,0:T(8,128)(2,1)S(1)}, u32[]{:S(2)}, u32[]{:S(2)}) collective-permute-start(bf16[2,640,256]{2,1,0:T(8,128)(2,1)S(1)} %collective-permute-done.6.refs_2_.refs_7_), channel_id=1, source_target_pairs={{0,32},{16,240},{32,64},{48,16},{64,96},{80,48},{96,128},{112,80},... | collective-permute-start | bytes 1966088 | tf_op jit(solution)/shard_map/ppermute | solution.py:186
  82.0 9.5 %collective-permute-start.8 = (bf16[2,640,256]{2,1,0:T(8,128)(2,1)S(1)}, bf16[2,640,256]{2,1,0:T(8,128)(2,1)S(1)}, u32[]{:S(2)}, u32[]{:S(2)}) collective-permute-start(bf16[2,640,256]{2,1,0:T(8,128)(2,1)S(1)} %collective-permute-done.6.refs_2_.refs_7_), channel_id=1, source_target_pairs={{0,16},{16,0},{1,17},{17,1},{2,18},{18,2},{3,19},{19,3},{4,20},{20... | collective-permute-start | bytes 1966088 | tf_op jit(solution)/shard_map/ppermute | solution.py:172
  84.0 0.9 copy-start.14
  84.8 0.9 copy-start.18
  85.7 11.7 %collective-permute-start.13 = (bf16[2,640,256]{2,1,0:T(8,128)(2,1)S(1)}, bf16[2,640,256]{2,1,0:T(8,128)(2,1)}, u32[]{:S(2)}, u32[]{:S(2)}) collective-permute-start(bf16[2,640,256]{2,1,0:T(8,128)(2,1)S(1)} %collective-permute-done.9.refs_1_.refs_9_), channel_id=1, source_target_pairs={{0,32},{16,240},{32,64},{48,16},{64,96},{80,48},{96,128},{112,80},... | collective-permute-start | bytes 1966088 | tf_op jit(solution)/shard_map/ppermute | solution.py:186
  89.5 7.9 %collective-permute-start.10 = (bf16[2,640,256]{2,1,0:T(8,128)(2,1)S(1)}, bf16[2,640,256]{2,1,0:T(8,128)(2,1)S(1)}, u32[]{:S(2)}, u32[]{:S(2)}) collective-permute-start(bf16[2,640,256]{2,1,0:T(8,128)(2,1)S(1)} %collective-permute-done.9.refs_1_.refs_9_), channel_id=1, source_target_pairs={{0,16},{16,0},{1,17},{17,1},{2,18},{18,2},{3,19},{19,3},{4,20},{20... | collective-permute-start | bytes 1966088 | tf_op jit(solution)/shard_map/ppermute | solution.py:172
  91.5 0.8 copy-start.20
  92.3 17.7 %collective-permute-start.12 = (bf16[2,640,256]{2,1,0:T(8,128)(2,1)S(1)}, bf16[2,640,256]{2,1,0:T(8,128)(2,1)}, u32[]{:S(2)}, u32[]{:S(2)}) collective-permute-start(bf16[2,640,256]{2,1,0:T(8,128)(2,1)S(1)} %collective-permute-done.11.refs_3_.refs_11_), channel_id=1, source_target_pairs={{0,16},{16,0},{1,17},{17,1},{2,18},{18,2},{3,19},{19,3},{4,20},{20... | collective-permute-start | bytes 1966088 | tf_op jit(solution)/shard_map/ppermute | solution.py:172
  97.4 0.9 copy-start.1
  98.3 13.6 %collective-permute-start.14 = (bf16[2,640,256]{2,1,0:T(8,128)(2,1)}, bf16[2,640,256]{2,1,0:T(8,128)(2,1)}, u32[]{:S(2)}, u32[]{:S(2)}) collective-permute-start(bf16[2,640,256]{2,1,0:T(8,128)(2,1)} %collective-permute-done.13.refs_2_.refs_13_), channel_id=1, source_target_pairs={{0,16},{16,0},{1,17},{17,1},{2,18},{18,2},{3,19},{19,3},{4,20},{20... | collective-permute-start | bytes 1966088 | tf_op jit(solution)/shard_map/ppermute | solution.py:172
  102.8 1.1 copy-start.4
  103.9 1.1 copy-start.7
  103.9 1.3 %copy-start.9 = (bf16[2,640,256]{2,1,0:T(8,128)(2,1)S(1)}, bf16[2,640,256]{2,1,0:T(8,128)(2,1)}, u32[]{:S(2)}) copy-start(bf16[2,640,256]{2,1,0:T(8,128)(2,1)} %copy-done.8) | copy-start | bytes 1966084
  103.9 1.5 %copy-start.13 = (bf16[2,640,256]{2,1,0:T(8,128)(2,1)S(1)}, bf16[2,640,256]{2,1,0:T(8,128)(2,1)}, u32[]{:S(2)}) copy-start(bf16[2,640,256]{2,1,0:T(8,128)(2,1)} %copy-done.12) | copy-start | bytes 1966084
  103.9 1.7 %copy-start.17 = (bf16[2,640,256]{2,1,0:T(8,128)(2,1)S(1)}, bf16[2,640,256]{2,1,0:T(8,128)(2,1)}, u32[]{:S(2)}) copy-start(bf16[2,640,256]{2,1,0:T(8,128)(2,1)} %copy-done.16) | copy-start | bytes 1966084
  105.6 1.5 %copy-start.11 = (bf16[2,640,256]{2,1,0:T(8,128)(2,1)S(1)}, bf16[2,640,256]{2,1,0:T(8,128)(2,1)}, u32[]{:S(2)}) copy-start(bf16[2,640,256]{2,1,0:T(8,128)(2,1)} %copy-done.10) | copy-start | bytes 1966084
  105.6 1.5 %copy-start.15 = (bf16[2,640,256]{2,1,0:T(8,128)(2,1)S(1)}, bf16[2,640,256]{2,1,0:T(8,128)(2,1)}, u32[]{:S(2)}) copy-start(bf16[2,640,256]{2,1,0:T(8,128)(2,1)} %copy-done.14) | copy-start | bytes 1966084
  105.6 1.5 %copy-start.19 = (bf16[2,640,256]{2,1,0:T(8,128)(2,1)S(1)}, bf16[2,640,256]{2,1,0:T(8,128)(2,1)}, u32[]{:S(2)}) copy-start(bf16[2,640,256]{2,1,0:T(8,128)(2,1)} %copy-done.18) | copy-start | bytes 1966084
  105.6 1.7 %copy-start.21 = (bf16[2,640,256]{2,1,0:T(8,128)(2,1)S(1)}, bf16[2,640,256]{2,1,0:T(8,128)(2,1)}, u32[]{:S(2)}) copy-start(bf16[2,640,256]{2,1,0:T(8,128)(2,1)} %copy-done.20) | copy-start | bytes 1966084
  107.3 1.5 %copy-start.2 = (bf16[2,640,256]{2,1,0:T(8,128)(2,1)S(1)}, bf16[2,640,256]{2,1,0:T(8,128)(2,1)}, u32[]{:S(2)}) copy-start(bf16[2,640,256]{2,1,0:T(8,128)(2,1)} %copy-done.1) | copy-start | bytes 1966084
  110.0 1.9 %copy-start.5 = (bf16[2,640,256]{2,1,0:T(8,128)(2,1)S(1)}, bf16[2,640,256]{2,1,0:T(8,128)(2,1)}, u32[]{:S(2)}) copy-start(bf16[2,640,256]{2,1,0:T(8,128)(2,1)} %copy-done.3) | copy-start | bytes 1966084

commit v7 on v6

--- a/solution.py
+++ b/solution.py
@@ -14,7 +14,7 @@
 EARLY_VMEM = 8 << 20
 GRADS_VMEM = 16 << 20
 FORWARD_GROUP = 2
-GRADS_GROUP = 2
+GRADS_GROUP = 4
 
 
 def pack_kernel(routes_ref, gates_ref, tokens_ref, cotangent_ref, out_ref):
@@ -103,24 +103,15 @@
         )
 
 
-def grads_kernel(ring_size, blocks, late, moved, index_ref, weights_ref, partial_ref, *refs):
+def grads_kernel(ring_size, blocks, late, index_ref, weights_ref, partial_ref, *refs):
     count = len(blocks)
-    sources, out_ref = list(refs[:count]), refs[count]
-    total, out_buf, sems, moved_buf, moved_sems = refs[count + 1 :]
-    loads = []
-    for n, block in enumerate(moved):
-        k = blocks.index(block)
-        load = pltpu.make_async_copy(sources[k], moved_buf.at[n], moved_sems.at[n])
-        load.start()
-        loads.append(load)
-        sources[k] = moved_buf.at[n]
+    sources, out_ref = refs[:count], refs[count]
+    total, out_buf, sems = refs[count + 1 :]
     halves, half = sources[0].shape[0], sources[0].shape[2] // 2
     hidden_units = weights_ref.shape[2]
     last = [blocks.index(block) for block in late]
     total[...] = partial_ref[...]
     add_forward(ring_size, index_ref, weights_ref, total, [sources[k] for k in last], late)
-    for load in loads:
-        load.wait()
     gate_part = total[:hidden_units]
     up_part = total[hidden_units : 2 * hidden_units]
     back_hidden = total[2 * hidden_units :]
@@ -210,7 +201,6 @@
         "early_4": [(far - 1, 1, 1), (far, 0, 0)],
     }
     late = [(far, 0, 1)]
-    from_hbm = [(1, 1, 0), (1, 0, 1), (2, 0, 0)]
     sums = jax.ShapeDtypeStruct((3 * hidden_units, slots), F32)
 
     partials = []
@@ -231,17 +221,14 @@
             )(index, expert_weights, *partials, *[raw.get(k, held[k]) for k in chosen])
         ]
     return pl.pallas_call(
-        functools.partial(grads_kernel, ring_size, blocks, late, from_hbm),
+        functools.partial(grads_kernel, ring_size, blocks, late),
         out_shape=jax.ShapeDtypeStruct(expert_weights.shape, BF16),
-        in_specs=[smem_spec, vmem_spec, vmem_spec]
-        + [pl.BlockSpec(memory_space=pl.ANY) if k in from_hbm else vmem_spec for k in blocks],
+        in_specs=[smem_spec, vmem_spec, vmem_spec] + [vmem_spec] * len(blocks),
         out_specs=pl.BlockSpec(memory_space=pl.ANY),
         scratch_shapes=[
             pltpu.VMEM(sums.shape, F32),
             pltpu.VMEM((len(blocks), 2, 3, hidden_units, width), BF16),
             pltpu.SemaphoreType.DMA((len(blocks), 2)),
-            pltpu.VMEM((len(from_hbm), 2, slots, 2 * width), BF16),
-            pltpu.SemaphoreType.DMA((len(from_hbm),)),
         ],
         cost_estimate=pl.CostEstimate(
             flops=len(blocks) * block_flops,

time: 118 us -> 117 us (level)
  no operation moved by 1% of the time
where the time goes in v7:
time: 117 us
  starting transfers between devices  55 us (47%)
  blocking collectives  30.5 us (26%)
  Pallas kernels  14.1 us (12%)
  local copies, waits for them, and re-layouts  10.3 us (9%)
  waiting for transfers between devices  6.32 us (5%)
    ppermute x7, starting transfers between devices, device_step(): piece = lax.ppermute(held[step - 1, chain, 0], ('ring', 'core'), around)  33.6 us
    all_to_all x1, blocking collectives, device_step(): lax.all_to_all(send.reshape(2 * groups, CAP, 2 * width), ('half', 'expert...  30.5 us
    ppermute x8, starting transfers between devices, swapped(): return lax.ppermute(x, 'core', [(0, 1), (1, 0)])  21.5 us
    unnamed x44, local copies, waits for them, and re-layouts  10.3 us
    pallas_call x5, Pallas kernels, device_step(): pl.pallas_call(functools.partial(forward_kernel, ring_size, chosen, chain...  7.08 us
    ppermute x7, waiting for transfers between devices, device_step(): piece = lax.ppermute(held[step - 1, chain, 0], ('ring', 'core'), around)  6.3 us
    pallas_call x1, Pallas kernels, device_step(): pl.pallas_call(functools.partial(grads_kernel, ring_size, blocks, late),...  4.77 us
  transfers between devices with their start and end apart: 15, of which 2 were waited for; matrix products, arithmetic and copies ran while one was open for 0% of the time, Pallas kernels for 6%

profile of v7, /device:TPU:1, one launch (start us, length us, event | category | flops | bytes accessed | tf_op | source)
XLA Modules:
  0.0 116.7 jit_solution(15828134918860154765)
XLA Ops:
  0.0 2.2 %shard_map.55 = bf16[2,640,256]{2,1,0:T(8,128)(2,1)} custom-call(s32[2,128]{1,0:T(2,128)} %bitcast.11, f32[2,128]{1,0:T(2,128)} %bitcast.12, bf16[128,128]{1,0:T(8,128)(2,1)} %tokens_ref.1, bf16[128,128]{1,0:T(8,128)(2,1)} %cotangent_ref.1), custom_call_target="tpu_custom_call" | custom-call | tf_op jit(solution)/shard_map/pallas_call | solution.py:152
  2.2 30.5 %all_to_all.5 = bf16[32,40,256]{2,1,0:T(8,128)(2,1)S(1)} all-to-all(bf16[32,40,256]{2,1,0:T(8,128)(2,1)} %bitcast.10), channel_id=1, replica_groups=mesh['half'=2,'ring'=8,'core'=2,'expert'=16] {'half','expert'}, dimensions={0} | all-to-all | bytes 1310720 | tf_op jit(solution)/shard_map/all_to_all | solution.py:165
  32.8 4.2 %collective-permute-start = (bf16[2,640,256]{2,1,0:T(8,128)(2,1)S(1)}, bf16[2,640,256]{2,1,0:T(8,128)(2,1)S(1)}, u32[]{:S(2)}, u32[]{:S(2)}) collective-permute-start(bf16[2,640,256]{2,1,0:T(8,128)(2,1)S(1)} %bitcast.6), channel_id=1, source_target_pairs={{0,16},{16,0},{1,17},{17,1},{2,18},{18,2},{3,19},{19,3},{4,20},{20... | collective-permute-start | bytes 1966088 | tf_op jit(solution)/shard_map/ppermute | solution.py:163
  36.9 10.7 %collective-permute-start.1 = (bf16[2,640,256]{2,1,0:T(8,128)(2,1)S(1)}, bf16[2,640,256]{2,1,0:T(8,128)(2,1)S(1)}, u32[]{:S(2)}, u32[]{:S(2)}) collective-permute-start(bf16[2,640,256]{2,1,0:T(8,128)(2,1)S(1)} %bitcast.7), channel_id=1, source_target_pairs={{0,32},{16,240},{32,64},{48,16},{64,96},{80,48},{96,128},{112,80},... | collective-permute-start | bytes 1966088 | tf_op jit(solution)/shard_map/ppermute | solution.py:177
  47.6 0.0 collective-permute-done.refs_1_
  47.6 2.2 %collective-permute-start.2 = (bf16[2,640,256]{2,1,0:T(8,128)(2,1)S(1)}, bf16[2,640,256]{2,1,0:T(8,128)(2,1)S(1)}, u32[]{:S(2)}, u32[]{:S(2)}) collective-permute-start(bf16[2,640,256]{2,1,0:T(8,128)(2,1)S(1)} %collective-permute-done.refs_1_), channel_id=1, source_target_pairs={{0,32},{16,240},{32,64},{48,16},{64,96},{80,48},{96,128},{112,80},... | collective-permute-start | bytes 1966088 | tf_op jit(solution)/shard_map/ppermute | solution.py:177
  49.8 0.0 copy-start.3
  49.8 0.8 copy-done.3
  50.6 4.5 %collective-permute-done.1.refs_1_.refs_2_ = bf16[2,640,256]{2,1,0:T(8,128)(2,1)S(1)} collective-permute-done((bf16[2,640,256]{2,1,0:T(8,128)(2,1)S(1)}, bf16[2,640,256]{2,1,0:T(8,128)(2,1)S(1)}, u32[]{:S(2)}, u32[]{:S(2)}) %collective-permute-start.1) | collective-permute-done | bytes 655392 | tf_op jit(solution)/shard_map/ppermute | solution.py:177
  55.1 5.0 %collective-permute-start.5 = (bf16[2,640,256]{2,1,0:T(8,128)(2,1)S(1)}, bf16[2,640,256]{2,1,0:T(8,128)(2,1)S(1)}, u32[]{:S(2)}, u32[]{:S(2)}) collective-permute-start(bf16[2,640,256]{2,1,0:T(8,128)(2,1)S(1)} %collective-permute-done.1.refs_1_.refs_2_), channel_id=1, source_target_pairs={{0,32},{16,240},{32,64},{48,16},{64,96},{80,48},{96,128},{112,80},... | collective-permute-start | bytes 1966088 | tf_op jit(solution)/shard_map/ppermute | solution.py:177
  60.1 1.9 %collective-permute-start.3 = (bf16[2,640,256]{2,1,0:T(8,128)(2,1)S(1)}, bf16[2,640,256]{2,1,0:T(8,128)(2,1)S(1)}, u32[]{:S(2)}, u32[]{:S(2)}) collective-permute-start(bf16[2,640,256]{2,1,0:T(8,128)(2,1)S(1)} %collective-permute-done.1.refs_1_.refs_2_), channel_id=1, source_target_pairs={{0,16},{16,0},{1,17},{17,1},{2,18},{18,2},{3,19},{19,3},{4,20},{20... | collective-permute-start | bytes 1966088 | tf_op jit(solution)/shard_map/ppermute | solution.py:163
  62.1 0.8 copy-done.6
  62.9 0.0 collective-permute-done.2.refs_2_.refs_3_
  62.9 4.2 %collective-permute-start.6 = (bf16[2,640,256]{2,1,0:T(8,128)(2,1)S(1)}, bf16[2,640,256]{2,1,0:T(8,128)(2,1)S(1)}, u32[]{:S(2)}, u32[]{:S(2)}) collective-permute-start(bf16[2,640,256]{2,1,0:T(8,128)(2,1)S(1)} %collective-permute-done.2.refs_2_.refs_3_), channel_id=1, source_target_pairs={{0,32},{16,240},{32,64},{48,16},{64,96},{80,48},{96,128},{112,80},... | collective-permute-start | bytes 1966088 | tf_op jit(solution)/shard_map/ppermute | solution.py:177
  67.1 1.9 %collective-permute-start.4 = (bf16[2,640,256]{2,1,0:T(8,128)(2,1)S(1)}, bf16[2,640,256]{2,1,0:T(8,128)(2,1)S(1)}, u32[]{:S(2)}, u32[]{:S(2)}) collective-permute-start(bf16[2,640,256]{2,1,0:T(8,128)(2,1)S(1)} %collective-permute-done.2.refs_2_.refs_3_), channel_id=1, source_target_pairs={{0,16},{16,0},{1,17},{17,1},{2,18},{18,2},{3,19},{19,3},{4,20},{20... | collective-permute-start | bytes 1966088 | tf_op jit(solution)/shard_map/ppermute | solution.py:163
  69.1 0.8 copy-done.8
  69.9 0.8 copy-done.12
  70.8 4.2 %collective-permute-start.9 = (bf16[2,640,256]{2,1,0:T(8,128)(2,1)S(1)}, bf16[2,640,256]{2,1,0:T(8,128)(2,1)S(1)}, u32[]{:S(2)}, u32[]{:S(2)}) collective-permute-start(bf16[2,640,256]{2,1,0:T(8,128)(2,1)S(1)} %collective-permute-done.5.refs_1_.refs_5_), channel_id=1, source_target_pairs={{0,32},{16,240},{32,64},{48,16},{64,96},{80,48},{96,128},{112,80},... | collective-permute-start | bytes 1966088 | tf_op jit(solution)/shard_map/ppermute | solution.py:177
  75.0 1.9 %collective-permute-start.7 = (bf16[2,640,256]{2,1,0:T(8,128)(2,1)S(1)}, bf16[2,640,256]{2,1,0:T(8,128)(2,1)S(1)}, u32[]{:S(2)}, u32[]{:S(2)}) collective-permute-start(bf16[2,640,256]{2,1,0:T(8,128)(2,1)S(1)} %collective-permute-done.5.refs_1_.refs_5_), channel_id=1, source_target_pairs={{0,16},{16,0},{1,17},{17,1},{2,18},{18,2},{3,19},{19,3},{4,20},{20... | collective-permute-start | bytes 1966088 | tf_op jit(solution)/shard_map/ppermute | solution.py:163
  76.9 0.9 copy-done.10
  77.8 0.0 collective-permute-done.6.refs_2_.refs_7_
  77.8 0.8 copy-done.16
  78.7 3.4 %collective-permute-start.11 = (bf16[2,640,256]{2,1,0:T(8,128)(2,1)S(1)}, bf16[2,640,256]{2,1,0:T(8,128)(2,1)S(1)}, u32[]{:S(2)}, u32[]{:S(2)}) collective-permute-start(bf16[2,640,256]{2,1,0:T(8,128)(2,1)S(1)} %collective-permute-done.6.refs_2_.refs_7_), channel_id=1, source_target_pairs={{0,32},{16,240},{32,64},{48,16},{64,96},{80,48},{96,128},{112,80},... | collective-permute-start | bytes 1966088 | tf_op jit(solution)/shard_map/ppermute | solution.py:177
  82.0 1.9 %collective-permute-start.8 = (bf16[2,640,256]{2,1,0:T(8,128)(2,1)S(1)}, bf16[2,640,256]{2,1,0:T(8,128)(2,1)S(1)}, u32[]{:S(2)}, u32[]{:S(2)}) collective-permute-start(bf16[2,640,256]{2,1,0:T(8,128)(2,1)S(1)} %collective-permute-done.6.refs_2_.refs_7_), channel_id=1, source_target_pairs={{0,16},{16,0},{1,17},{17,1},{2,18},{18,2},{3,19},{19,3},{4,20},{20... | collective-permute-start | bytes 1966088 | tf_op jit(solution)/shard_map/ppermute | solution.py:163
  84.0 0.8 copy-done.14
  84.8 0.8 copy-done.18
  85.7 3.9 %collective-permute-start.13 = (bf16[2,640,256]{2,1,0:T(8,128)(2,1)S(1)}, bf16[2,640,256]{2,1,0:T(8,128)(2,1)}, u32[]{:S(2)}, u32[]{:S(2)}) collective-permute-start(bf16[2,640,256]{2,1,0:T(8,128)(2,1)S(1)} %collective-permute-done.9.refs_1_.refs_9_), channel_id=1, source_target_pairs={{0,32},{16,240},{32,64},{48,16},{64,96},{80,48},{96,128},{112,80},... | collective-permute-start | bytes 1966088 | tf_op jit(solution)/shard_map/ppermute | solution.py:177
  89.5 1.9 %collective-permute-start.10 = (bf16[2,640,256]{2,1,0:T(8,128)(2,1)S(1)}, bf16[2,640,256]{2,1,0:T(8,128)(2,1)S(1)}, u32[]{:S(2)}, u32[]{:S(2)}) collective-permute-start(bf16[2,640,256]{2,1,0:T(8,128)(2,1)S(1)} %collective-permute-done.9.refs_1_.refs_9_), channel_id=1, source_target_pairs={{0,16},{16,0},{1,17},{17,1},{2,18},{18,2},{3,19},{19,3},{4,20},{20... | collective-permute-start | bytes 1966088 | tf_op jit(solution)/shard_map/ppermute | solution.py:163
  91.5 0.0 collective-permute-done.11.refs_3_.refs_11_
  91.5 0.8 copy-done.20
  92.3 3.2 %collective-permute-start.12 = (bf16[2,640,256]{2,1,0:T(8,128)(2,1)S(1)}, bf16[2,640,256]{2,1,0:T(8,128)(2,1)}, u32[]{:S(2)}, u32[]{:S(2)}) collective-permute-start(bf16[2,640,256]{2,1,0:T(8,128)(2,1)S(1)} %collective-permute-done.11.refs_3_.refs_11_), channel_id=1, source_target_pairs={{0,16},{16,0},{1,17},{17,1},{2,18},{18,2},{3,19},{19,3},{4,20},{20... | collective-permute-start | bytes 1966088 | tf_op jit(solution)/shard_map/ppermute | solution.py:163
  95.6 1.8 %collective-permute-done.13.refs_2_.refs_13_ = bf16[2,640,256]{2,1,0:T(8,128)(2,1)} collective-permute-done((bf16[2,640,256]{2,1,0:T(8,128)(2,1)S(1)}, bf16[2,640,256]{2,1,0:T(8,128)(2,1)}, u32[]{:S(2)}, u32[]{:S(2)}) %collective-permute-start.13) | collective-permute-done | bytes 655392 | tf_op jit(solution)/shard_map/ppermute | solution.py:177
  97.4 0.9 copy-done.1
  98.3 4.5 %collective-permute-start.14 = (bf16[2,640,256]{2,1,0:T(8,128)(2,1)}, bf16[2,640,256]{2,1,0:T(8,128)(2,1)}, u32[]{:S(2)}, u32[]{:S(2)}) collective-permute-start(bf16[2,640,256]{2,1,0:T(8,128)(2,1)} %collective-permute-done.13.refs_2_.refs_13_), channel_id=1, source_target_pairs={{0,16},{16,0},{1,17},{17,1},{2,18},{18,2},{3,19},{19,3},{4,20},{20... | collective-permute-start | bytes 1966088 | tf_op jit(solution)/shard_map/ppermute | solution.py:163
  102.8 0.1 pad_add_fusion.index_ref
  102.8 1.1 copy-done.4
  103.9 1.1 shard_map.56.refs_0_
  105.0 0.0 copy-done.7
  105.0 0.2 copy-done.9
  105.2 0.2 copy-done.13
  105.4 0.2 copy-done.17
  105.6 1.5 %shard_map.57.refs_0_ = f32[192,640]{1,0:T(8,128)S(1)} custom-call(s32[2]{0:T(128)S(1)} %pad_add_fusion.index_ref, bf16[1,3,64,4096]{3,2,1,0:T(8,128)(2,1)S(1)} %copy-done, f32[192,640]{1,0:T(8,128)S(1)} %shard_map.56.refs_0_, bf16[2,640,256]{2,1,0:T(8,128)(2,1)S(1)} %copy-done.7, bf16[2,640,256]{2,1,0:T(8,128)(2,1)S(1)} %copy-done.9, ...), custom_call_target="tpu_custom_call" | custom-call | flops 251658240 | bytes 2621440 | tf_op jit(solution)/shard_map/pallas_call | solution.py:210
  107.1 0.2 copy-done.21
  107.3 1.4 %shard_map.58.refs_0_ = f32[192,640]{1,0:T(8,128)S(1)} custom-call(s32[2]{0:T(128)S(1)} %pad_add_fusion.index_ref, bf16[1,3,64,4096]{3,2,1,0:T(8,128)(2,1)S(1)} %copy-done, f32[192,640]{1,0:T(8,128)S(1)} %shard_map.57.refs_0_, bf16[2,640,256]{2,1,0:T(8,128)(2,1)S(1)} %copy-done.11, bf16[2,640,256]{2,1,0:T(8,128)(2,1)S(1)} %copy-done.15, ...), custom_call_target="tpu_custom_call" | custom-call | flops 251658240 | bytes 2621440 | tf_op jit(solution)/shard_map/pallas_call | solution.py:210
  108.7 1.2 %shard_map.59.refs_0_ = f32[192,640]{1,0:T(8,128)S(1)} custom-call(s32[2]{0:T(128)S(1)} %pad_add_fusion.index_ref, bf16[1,3,64,4096]{3,2,1,0:T(8,128)(2,1)S(1)} %copy-done, f32[192,640]{1,0:T(8,128)S(1)} %shard_map.58.refs_0_, bf16[2,640,256]{2,1,0:T(8,128)(2,1)S(1)} %collective-permute-done.9.refs_1_.refs_9_, bf16[2,640,256]{2,1,0:T(8,128)(2,1)S(1)} %copy-done.2, ...), custom_call_target="tpu_custom_call" | custom-call | flops 188743680 | bytes 1966080 | tf_op jit(solution)/shard_map/pallas_call | solution.py:210
  110.0 0.0 copy-start.5
  110.0 1.9 %shard_map.60.partial_ref = f32[192,640]{1,0:T(8,128)S(1)} custom-call(s32[2]{0:T(128)S(1)} %pad_add_fusion.index_ref, bf16[1,3,64,4096]{3,2,1,0:T(8,128)(2,1)S(1)} %copy-done, f32[192,640]{1,0:T(8,128)S(1)} %shard_map.59.refs_0_, bf16[2,640,256]{2,1,0:T(8,128)(2,1)} %collective-permute-done.12.refs_1_.refs_14_, ...), custom_call_target="tpu_custom_call" | custom-call | flops 125829120 | bytes 1310720 | tf_op jit(solution)/shard_map/pallas_call | solution.py:210
  111.9 4.8 %shard_map.61 = bf16[1,3,64,4096]{3,2,1,0:T(8,128)(2,1)} custom-call(s32[2]{0:T(128)S(1)} %pad_add_fusion.index_ref, bf16[1,3,64,4096]{3,2,1,0:T(8,128)(2,1)S(1)} %copy-done, f32[192,640]{1,0:T(8,128)S(1)} %shard_map.60.partial_ref, bf16[2,640,256]{2,1,0:T(8,128)(2,1)S(1)} %bitcast.9, bf16[2,640,256]{2,1,0:T(8,128)(2,1)S(1)} %copy-done.5, ...), custom_call_target="tpu_custom_call" | custom-call | flops 1006632960 | bytes 12058624 | tf_op jit(solution)/shard_map/pallas_call | solution.py:223
  (35 shorter events, 0.1 us)
Async XLA Ops:
  0.0 102.8 %copy-start = (bf16[1,3,64,4096]{3,2,1,0:T(8,128)(2,1)S(1)}, bf16[1,3,64,4096]{3,2,1,0:T(8,128)(2,1)}, u32[]{:S(2)}) copy-start(bf16[1,3,64,4096]{3,2,1,0:T(8,128)(2,1)} %weights_ref.11) | copy-start | bytes 4718596
  32.8 14.8 %collective-permute-start = (bf16[2,640,256]{2,1,0:T(8,128)(2,1)S(1)}, bf16[2,640,256]{2,1,0:T(8,128)(2,1)S(1)}, u32[]{:S(2)}, u32[]{:S(2)}) collective-permute-start(bf16[2,640,256]{2,1,0:T(8,128)(2,1)S(1)} %bitcast.6), channel_id=1, source_target_pairs={{0,16},{16,0},{1,17},{17,1},{2,18},{18,2},{3,19},{19,3},{4,20},{20... | collective-permute-start | bytes 1966088 | tf_op jit(solution)/shard_map/ppermute | solution.py:163
  36.9 18.2 %collective-permute-start.1 = (bf16[2,640,256]{2,1,0:T(8,128)(2,1)S(1)}, bf16[2,640,256]{2,1,0:T(8,128)(2,1)S(1)}, u32[]{:S(2)}, u32[]{:S(2)}) collective-permute-start(bf16[2,640,256]{2,1,0:T(8,128)(2,1)S(1)} %bitcast.7), channel_id=1, source_target_pairs={{0,32},{16,240},{32,64},{48,16},{64,96},{80,48},{96,128},{112,80},... | collective-permute-start | bytes 1966088 | tf_op jit(solution)/shard_map/ppermute | solution.py:177
  47.6 15.3 %collective-permute-start.2 = (bf16[2,640,256]{2,1,0:T(8,128)(2,1)S(1)}, bf16[2,640,256]{2,1,0:T(8,128)(2,1)S(1)}, u32[]{:S(2)}, u32[]{:S(2)}) collective-permute-start(bf16[2,640,256]{2,1,0:T(8,128)(2,1)S(1)} %collective-permute-done.refs_1_), channel_id=1, source_target_pairs={{0,32},{16,240},{32,64},{48,16},{64,96},{80,48},{96,128},{112,80},... | collective-permute-start | bytes 1966088 | tf_op jit(solution)/shard_map/ppermute | solution.py:177
  49.8 0.8 copy-start.3
  55.1 14.8 %collective-permute-start.5 = (bf16[2,640,256]{2,1,0:T(8,128)(2,1)S(1)}, bf16[2,640,256]{2,1,0:T(8,128)(2,1)S(1)}, u32[]{:S(2)}, u32[]{:S(2)}) collective-permute-start(bf16[2,640,256]{2,1,0:T(8,128)(2,1)S(1)} %collective-permute-done.1.refs_1_.refs_2_), channel_id=1, source_target_pairs={{0,32},{16,240},{32,64},{48,16},{64,96},{80,48},{96,128},{112,80},... | collective-permute-start | bytes 1966088 | tf_op jit(solution)/shard_map/ppermute | solution.py:177
  60.1 9.8 %collective-permute-start.3 = (bf16[2,640,256]{2,1,0:T(8,128)(2,1)S(1)}, bf16[2,640,256]{2,1,0:T(8,128)(2,1)S(1)}, u32[]{:S(2)}, u32[]{:S(2)}) collective-permute-start(bf16[2,640,256]{2,1,0:T(8,128)(2,1)S(1)} %collective-permute-done.1.refs_1_.refs_2_), channel_id=1, source_target_pairs={{0,16},{16,0},{1,17},{17,1},{2,18},{18,2},{3,19},{19,3},{4,20},{20... | collective-permute-start | bytes 1966088 | tf_op jit(solution)/shard_map/ppermute | solution.py:163
  62.1 0.8 copy-start.6
  62.9 14.9 %collective-permute-start.6 = (bf16[2,640,256]{2,1,0:T(8,128)(2,1)S(1)}, bf16[2,640,256]{2,1,0:T(8,128)(2,1)S(1)}, u32[]{:S(2)}, u32[]{:S(2)}) collective-permute-start(bf16[2,640,256]{2,1,0:T(8,128)(2,1)S(1)} %collective-permute-done.2.refs_2_.refs_3_), channel_id=1, source_target_pairs={{0,32},{16,240},{32,64},{48,16},{64,96},{80,48},{96,128},{112,80},... | collective-permute-start | bytes 1966088 | tf_op jit(solution)/shard_map/ppermute | solution.py:177
  67.1 10.7 %collective-permute-start.4 = (bf16[2,640,256]{2,1,0:T(8,128)(2,1)S(1)}, bf16[2,640,256]{2,1,0:T(8,128)(2,1)S(1)}, u32[]{:S(2)}, u32[]{:S(2)}) collective-permute-start(bf16[2,640,256]{2,1,0:T(8,128)(2,1)S(1)} %collective-permute-done.2.refs_2_.refs_3_), channel_id=1, source_target_pairs={{0,16},{16,0},{1,17},{17,1},{2,18},{18,2},{3,19},{19,3},{4,20},{20... | collective-permute-start | bytes 1966088 | tf_op jit(solution)/shard_map/ppermute | solution.py:163
  69.1 0.9 copy-start.8
  69.9 0.8 copy-start.12
  70.8 14.0 %collective-permute-start.9 = (bf16[2,640,256]{2,1,0:T(8,128)(2,1)S(1)}, bf16[2,640,256]{2,1,0:T(8,128)(2,1)S(1)}, u32[]{:S(2)}, u32[]{:S(2)}) collective-permute-start(bf16[2,640,256]{2,1,0:T(8,128)(2,1)S(1)} %collective-permute-done.5.refs_1_.refs_5_), channel_id=1, source_target_pairs={{0,32},{16,240},{32,64},{48,16},{64,96},{80,48},{96,128},{112,80},... | collective-permute-start | bytes 1966088 | tf_op jit(solution)/shard_map/ppermute | solution.py:177
  75.0 9.8 %collective-permute-start.7 = (bf16[2,640,256]{2,1,0:T(8,128)(2,1)S(1)}, bf16[2,640,256]{2,1,0:T(8,128)(2,1)S(1)}, u32[]{:S(2)}, u32[]{:S(2)}) collective-permute-start(bf16[2,640,256]{2,1,0:T(8,128)(2,1)S(1)} %collective-permute-done.5.refs_1_.refs_5_), channel_id=1, source_target_pairs={{0,16},{16,0},{1,17},{17,1},{2,18},{18,2},{3,19},{19,3},{4,20},{20... | collective-permute-start | bytes 1966088 | tf_op jit(solution)/shard_map/ppermute | solution.py:163
  76.9 0.9 copy-start.10
  77.8 0.8 copy-start.16
  78.7 12.8 %collective-permute-start.11 = (bf16[2,640,256]{2,1,0:T(8,128)(2,1)S(1)}, bf16[2,640,256]{2,1,0:T(8,128)(2,1)S(1)}, u32[]{:S(2)}, u32[]{:S(2)}) collective-permute-start(bf16[2,640,256]{2,1,0:T(8,128)(2,1)S(1)} %collective-permute-done.6.refs_2_.refs_7_), channel_id=1, source_target_pairs={{0,32},{16,240},{32,64},{48,16},{64,96},{80,48},{96,128},{112,80},... | collective-permute-start | bytes 1966088 | tf_op jit(solution)/shard_map/ppermute | solution.py:177
  82.0 9.5 %collective-permute-start.8 = (bf16[2,640,256]{2,1,0:T(8,128)(2,1)S(1)}, bf16[2,640,256]{2,1,0:T(8,128)(2,1)S(1)}, u32[]{:S(2)}, u32[]{:S(2)}) collective-permute-start(bf16[2,640,256]{2,1,0:T(8,128)(2,1)S(1)} %collective-permute-done.6.refs_2_.refs_7_), channel_id=1, source_target_pairs={{0,16},{16,0},{1,17},{17,1},{2,18},{18,2},{3,19},{19,3},{4,20},{20... | collective-permute-start | bytes 1966088 | tf_op jit(solution)/shard_map/ppermute | solution.py:163
  84.0 0.9 copy-start.14
  84.8 0.9 copy-start.18
  85.7 11.7 %collective-permute-start.13 = (bf16[2,640,256]{2,1,0:T(8,128)(2,1)S(1)}, bf16[2,640,256]{2,1,0:T(8,128)(2,1)}, u32[]{:S(2)}, u32[]{:S(2)}) collective-permute-start(bf16[2,640,256]{2,1,0:T(8,128)(2,1)S(1)} %collective-permute-done.9.refs_1_.refs_9_), channel_id=1, source_target_pairs={{0,32},{16,240},{32,64},{48,16},{64,96},{80,48},{96,128},{112,80},... | collective-permute-start | bytes 1966088 | tf_op jit(solution)/shard_map/ppermute | solution.py:177
  89.5 7.9 %collective-permute-start.10 = (bf16[2,640,256]{2,1,0:T(8,128)(2,1)S(1)}, bf16[2,640,256]{2,1,0:T(8,128)(2,1)S(1)}, u32[]{:S(2)}, u32[]{:S(2)}) collective-permute-start(bf16[2,640,256]{2,1,0:T(8,128)(2,1)S(1)} %collective-permute-done.9.refs_1_.refs_9_), channel_id=1, source_target_pairs={{0,16},{16,0},{1,17},{17,1},{2,18},{18,2},{3,19},{19,3},{4,20},{20... | collective-permute-start | bytes 1966088 | tf_op jit(solution)/shard_map/ppermute | solution.py:163
  91.5 0.8 copy-start.20
  92.3 17.7 %collective-permute-start.12 = (bf16[2,640,256]{2,1,0:T(8,128)(2,1)S(1)}, bf16[2,640,256]{2,1,0:T(8,128)(2,1)}, u32[]{:S(2)}, u32[]{:S(2)}) collective-permute-start(bf16[2,640,256]{2,1,0:T(8,128)(2,1)S(1)} %collective-permute-done.11.refs_3_.refs_11_), channel_id=1, source_target_pairs={{0,16},{16,0},{1,17},{17,1},{2,18},{18,2},{3,19},{19,3},{4,20},{20... | collective-permute-start | bytes 1966088 | tf_op jit(solution)/shard_map/ppermute | solution.py:163
  97.4 0.9 copy-start.1
  98.3 13.6 %collective-permute-start.14 = (bf16[2,640,256]{2,1,0:T(8,128)(2,1)}, bf16[2,640,256]{2,1,0:T(8,128)(2,1)}, u32[]{:S(2)}, u32[]{:S(2)}) collective-permute-start(bf16[2,640,256]{2,1,0:T(8,128)(2,1)} %collective-permute-done.13.refs_2_.refs_13_), channel_id=1, source_target_pairs={{0,16},{16,0},{1,17},{17,1},{2,18},{18,2},{3,19},{19,3},{4,20},{20... | collective-permute-start | bytes 1966088 | tf_op jit(solution)/shard_map/ppermute | solution.py:163
  102.8 1.1 copy-start.4
  103.9 1.1 copy-start.7
  103.9 1.3 %copy-start.9 = (bf16[2,640,256]{2,1,0:T(8,128)(2,1)S(1)}, bf16[2,640,256]{2,1,0:T(8,128)(2,1)}, u32[]{:S(2)}) copy-start(bf16[2,640,256]{2,1,0:T(8,128)(2,1)} %copy-done.8) | copy-start | bytes 1966084
  103.9 1.5 %copy-start.13 = (bf16[2,640,256]{2,1,0:T(8,128)(2,1)S(1)}, bf16[2,640,256]{2,1,0:T(8,128)(2,1)}, u32[]{:S(2)}) copy-start(bf16[2,640,256]{2,1,0:T(8,128)(2,1)} %copy-done.12) | copy-start | bytes 1966084
  103.9 1.7 %copy-start.17 = (bf16[2,640,256]{2,1,0:T(8,128)(2,1)S(1)}, bf16[2,640,256]{2,1,0:T(8,128)(2,1)}, u32[]{:S(2)}) copy-start(bf16[2,640,256]{2,1,0:T(8,128)(2,1)} %copy-done.16) | copy-start | bytes 1966084
  105.6 1.5 %copy-start.11 = (bf16[2,640,256]{2,1,0:T(8,128)(2,1)S(1)}, bf16[2,640,256]{2,1,0:T(8,128)(2,1)}, u32[]{:S(2)}) copy-start(bf16[2,640,256]{2,1,0:T(8,128)(2,1)} %copy-done.10) | copy-start | bytes 1966084
  105.6 1.5 %copy-start.15 = (bf16[2,640,256]{2,1,0:T(8,128)(2,1)S(1)}, bf16[2,640,256]{2,1,0:T(8,128)(2,1)}, u32[]{:S(2)}) copy-start(bf16[2,640,256]{2,1,0:T(8,128)(2,1)} %copy-done.14) | copy-start | bytes 1966084
  105.6 1.5 %copy-start.19 = (bf16[2,640,256]{2,1,0:T(8,128)(2,1)S(1)}, bf16[2,640,256]{2,1,0:T(8,128)(2,1)}, u32[]{:S(2)}) copy-start(bf16[2,640,256]{2,1,0:T(8,128)(2,1)} %copy-done.18) | copy-start | bytes 1966084
  105.6 1.7 %copy-start.21 = (bf16[2,640,256]{2,1,0:T(8,128)(2,1)S(1)}, bf16[2,640,256]{2,1,0:T(8,128)(2,1)}, u32[]{:S(2)}) copy-start(bf16[2,640,256]{2,1,0:T(8,128)(2,1)} %copy-done.20) | copy-start | bytes 1966084
  107.3 1.5 %copy-start.2 = (bf16[2,640,256]{2,1,0:T(8,128)(2,1)S(1)}, bf16[2,640,256]{2,1,0:T(8,128)(2,1)}, u32[]{:S(2)}) copy-start(bf16[2,640,256]{2,1,0:T(8,128)(2,1)} %copy-done.1) | copy-start | bytes 1966084
  110.0 1.9 %copy-start.5 = (bf16[2,640,256]{2,1,0:T(8,128)(2,1)S(1)}, bf16[2,640,256]{2,1,0:T(8,128)(2,1)}, u32[]{:S(2)}) copy-start(bf16[2,640,256]{2,1,0:T(8,128)(2,1)} %copy-done.3) | copy-start | bytes 1966084
